TPU v7x, 32 devices: a whole 2x2x4 slice. The times are simulated.
32 devices in a mesh: cell: 16 (over z, y, core), dir: 2 (over x).
Axes of the slice: x: 2, y: 2, z: 4, core: 2. Of those that a mesh axis runs over, the one named last changes fastest.
Arguments:
- atom_features: bfloat16 [512, 128, 128], P('cell'), may hold values from -6 to 6
- positions: bfloat16 [512, 3, 128], P('cell'), may hold values from 0 to 12
- neighbours: int32 [512, 4], P('cell'), may hold values from 0 to 39, as said below
- counts: int32 [16], replicated, may hold values from 4 to 28, as said below
- filter_gains: float32 [8, 128], replicated, may hold values from -0.25 to 0.25
- w_update: bfloat16 [128, 128], replicated, may hold values from -0.5 to 0.5
- projections: bfloat16 [128, 384], replicated, may hold values from -0.5 to 0.5
- w_output: bfloat16 [128, 128], replicated, may hold values from -0.5 to 0.5
Outputs:
- attended: bfloat16 [256, 128, 128], P(('cell', 'dir'))
Inputs may be any that keep to these rules, and one draw needn't show every extreme that they name: counts[c] live slots (slots 0 to counts[c] - 1) in cell c; the counts sum to 256; some cell holds the least and some the most. `neighbours`: for a live slot of cell c every entry is below 4 (a face block of the cell before), or from 4 to 4 + counts[c] - 1 (a live block of c), or 36 or more (a face block of the cell after); entries of dead slots lie in the same range.
All inputs are finite; a program needn't handle non-finite values.
Results may differ from a plain program's by a relative error of at most 0.014.
Values may be sent and summed in bfloat16 or wider, within the bound.
A program may use at most 128 MiB of HBM per device.

v0:
```python
import math

import jax
import jax.numpy as jnp
from jax import lax
from jax.sharding import PartitionSpec as P

DIRS = 50
H = 4


slab_width = 12.0
radial_width = 0.6
golden_turn = math.pi * (3.0 - math.sqrt(5.0))


def extended(cells, sides, width):
    for axis, dim in sides:
        count = lax.axis_size(axis)
        head = lax.slice_in_dim(cells, 0, width, axis=dim)
        tail = lax.slice_in_dim(cells, cells.shape[dim] - width, cells.shape[dim], axis=dim)
        cells = jnp.concatenate(
            [
                lax.ppermute(tail, axis, [(i, (i + 1) % count) for i in range(count)]),
                cells,
                lax.ppermute(head, axis, [((i + 1) % count, i) for i in range(count)]),
            ],
            axis=dim,
        )
    return cells


def shift_component(positions_in, amount):
    marker = (jnp.arange(positions_in.shape[-2]) == 0).astype(jnp.float32)
    return positions_in + amount * marker[:, None]


def direction_table(total):
    dir_order = jnp.arange(total, dtype=jnp.float32)
    height = 1.0 - (2.0 * dir_order + 1.0) / total
    radius = jnp.sqrt(1.0 - height * height)
    turning = dir_order * golden_turn
    return jnp.stack([radius * jnp.cos(turning), radius * jnp.sin(turning), height], axis=1)


def half_frequencies(width):
    half_width = width // 2
    return 0.5 * (jnp.arange(half_width, dtype=jnp.float32) + 1.0) / half_width


def phases(coords, directions, frequencies):
    projected = (
        directions[:, 0:1] * coords[0][None]
        + directions[:, 1:2] * coords[1][None]
        + directions[:, 2:3] * coords[2][None]
    )
    return projected[:, :, None] * frequencies


def rotate_with(values, cosine, sine):
    half_width = values.shape[-1] // 2
    first_half = values[None, :, :half_width]
    second_half = values[None, :, half_width:]
    turned = jnp.concatenate(
        [first_half * cosine - second_half * sine, second_half * cosine + first_half * sine],
        axis=-1,
    )
    return turned.astype(jnp.bfloat16)


def group_size(count):
    for candidate in range(1, count + 1):
        if count % candidate == 0 and count // candidate <= 25:
            return candidate
    return count


def radial_terms(own_positions, near_positions, near_features, filter_gains):
    differ = own_positions[:, None, :, :, None] - near_positions[:, :, :, None, :]
    distance = jnp.sqrt(jnp.sum(differ * differ, axis=2))
    centers = 2.0 + 2.0 * jnp.arange(filter_gains.shape[0], dtype=jnp.float32)
    scaled = (distance[:, :, None] - centers[None, None, :, None, None]) / radial_width
    radial = jnp.exp(-scaled * scaled).astype(jnp.bfloat16)
    summed = jnp.einsum(
        "gnkab,gnbf->gkaf", radial, near_features, preferred_element_type=jnp.float32
    )
    return jnp.sum(summed * filter_gains[None, :, None, :], axis=1)


def block_messages(
    first_slot,
    live_count,
    slot_count,
    group_width,
    neighbours,
    extended_features,
    extended_positions,
    filter_gains,
    face_blocks,
):
    initial = jnp.zeros(
        (slot_count, extended_features.shape[1], extended_features.shape[2]), jnp.float32
    )

    def block_advance(turn_index, running):
        start_slot = first_slot + turn_index * group_width
        picked = lax.dynamic_slice_in_dim(neighbours, start_slot, group_width, 0)
        near_features = extended_features[picked]
        near_positions = extended_positions[picked]
        own_positions = lax.dynamic_slice_in_dim(
            extended_positions, start_slot + face_blocks, group_width, 0
        )
        result = radial_terms(own_positions, near_positions, near_features, filter_gains)
        return lax.dynamic_update_slice_in_dim(running, result, turn_index * group_width, 0)

    group_total = (live_count + group_width - 1) // group_width
    return lax.fori_loop(0, group_total, block_advance, initial)


def kv_states(keys_rows, values, coords, dir_groups, frequencies):

    def kv_advance(carried, group_dirs):
        angle = phases(coords, group_dirs, frequencies)
        cosine = jnp.cos(angle)
        sine = jnp.sin(angle)
        key_rot = rotate_with(keys_rows, cosine, sine)
        state = jnp.einsum("grf,rh->gfh", key_rot, values, preferred_element_type=jnp.float32)
        return (carried, (state, cosine, sine))

    carried, outputs = lax.scan(kv_advance, jnp.float32(0.0), dir_groups)
    states, cosines, sines = outputs
    return (states.reshape(-1, states.shape[-2], states.shape[-1]), cosines, sines)


def query_mix(queries, cosines, sines, state_groups):

    def query_advance(running, paired):
        cosine, sine, group_states = paired
        query_rot = rotate_with(queries, cosine, sine)
        return (
            running
            + jnp.einsum(
                "grf,gfh->rh", query_rot, group_states, preferred_element_type=jnp.float32
            ),
            None,
        )

    running, unused = lax.scan(
        query_advance, jnp.zeros(queries.shape, jnp.float32), (cosines, sines, state_groups)
    )
    return running


def per_device(
    atom_features, positions, neighbours, counts, filter_gains, w_update, projections, w_output
):
    cells = lax.axis_size("cell")
    cell_index = lax.axis_index("cell")
    dirs_count = lax.axis_size("dir")
    dir_index = lax.axis_index("dir")
    capacity, block_atoms, width = atom_features.shape
    balanced_blocks = capacity // 2
    face_blocks = H
    faces_features, faces_positions = (
        extended(atom_features[:face_blocks], (("cell", 0),), face_blocks),
        extended(positions[:face_blocks], (("cell", 0),), face_blocks),
    )
    float_positions = positions.astype(jnp.float32)
    faces_float = faces_positions.astype(jnp.float32)
    extended_features = jnp.concatenate(
        [faces_features[:face_blocks], atom_features, faces_features[2 * face_blocks :]], axis=0
    )
    extended_positions = jnp.concatenate(
        [
            shift_component(faces_float[:face_blocks], -slab_width),
            float_positions,
            shift_component(faces_float[2 * face_blocks :], slab_width),
        ],
        axis=0,
    )
    own_count = counts[cell_index]
    share_slots = capacity // dirs_count
    first_slot = dir_index * share_slots
    live_count = jnp.clip(own_count - first_slot, 0, share_slots)
    message = block_messages(
        first_slot,
        live_count,
        share_slots,
        2,
        neighbours,
        extended_features,
        extended_positions,
        filter_gains,
        face_blocks,
    )
    own_features = lax.dynamic_slice_in_dim(atom_features, first_slot, share_slots, 0)
    activated = jax.nn.silu(message).astype(jnp.bfloat16)
    updated_share = (
        own_features.astype(jnp.float32)
        + jnp.dot(activated, w_update, preferred_element_type=jnp.float32)
    ).astype(jnp.bfloat16)
    updated = lax.all_gather(updated_share, "dir", axis=0, tiled=True)
    count_ends = jnp.cumsum(counts)
    starts = count_ends - counts
    first_live = starts[cell_index]
    slot_cap = max(1, 2 * balanced_blocks // cells)
    period = cells * slot_cap
    slot_order = jnp.arange(period, dtype=jnp.int32)
    offset = (slot_order - first_live) % period
    is_live = offset < own_count
    rows_picked = jnp.where(is_live, offset, 0)
    send_features = jnp.where(
        is_live[:, None, None], updated[rows_picked], jnp.zeros((), jnp.bfloat16)
    )
    send_positions = jnp.where(
        is_live[:, None, None], positions[rows_picked], jnp.zeros((), jnp.bfloat16)
    )
    received_features, received_positions = (
        lax.all_to_all(send_features, "cell", split_axis=0, concat_axis=0, tiled=True),
        lax.all_to_all(send_positions, "cell", split_axis=0, concat_axis=0, tiled=True),
    )
    target = jnp.arange(balanced_blocks, dtype=jnp.int32)
    within = target % slot_cap
    global_index = (target // slot_cap * cells + cell_index) * slot_cap + within
    source = jnp.sum((count_ends[None, :] <= global_index[:, None]).astype(jnp.int32), axis=1)
    pick_rows = source * slot_cap + within
    balanced_features = received_features[pick_rows]
    balanced_positions = shift_component(
        received_positions[pick_rows].astype(jnp.float32),
        slab_width * source.astype(jnp.float32)[:, None, None],
    )
    dir_table = direction_table(DIRS)
    frequencies = half_frequencies(width)
    share_blocks = balanced_blocks // dirs_count
    rows_features = lax.dynamic_slice_in_dim(
        balanced_features, dir_index * share_blocks, share_blocks, 0
    )
    rows_positions = lax.dynamic_slice_in_dim(
        balanced_positions, dir_index * share_blocks, share_blocks, 0
    )
    flat = rows_features.reshape(-1, width)
    qkv = jnp.dot(flat, projections, preferred_element_type=jnp.float32)
    coords = jnp.transpose(rows_positions, (1, 0, 2)).reshape(3, -1)
    queries, keys_rows, values, coords = (
        qkv[:, :width],
        qkv[:, width : 2 * width],
        qkv[:, 2 * width :].astype(jnp.bfloat16),
        coords,
    )
    group_width = group_size(DIRS)
    dir_groups = dir_table.reshape(-1, group_width, 3)
    local_states, cosines, sines = kv_states(keys_rows, values, coords, dir_groups, frequencies)
    states = lax.psum(local_states, ("cell", "dir")).astype(jnp.bfloat16)
    mixed_rows = query_mix(
        queries, cosines, sines, states.reshape(dir_groups.shape[0], group_width, width, width)
    )
    mix_scale = 1.0 / math.sqrt(DIRS * cells * balanced_blocks * block_atoms * width)
    mixed = (mixed_rows * mix_scale).astype(jnp.bfloat16)
    attended = jnp.dot(mixed, w_output, preferred_element_type=jnp.float32).astype(jnp.bfloat16)
    return attended.reshape(-1, block_atoms, width)


def solution(mesh):
    placed = (
        P("cell", None, None),
        P("cell", None, None),
        P("cell", None),
        P(),
        P(),
        P(),
        P(),
        P(),
    )
    return jax.shard_map(
        per_device,
        mesh=mesh,
        in_specs=placed,
        out_specs=P(("cell", "dir"), None, None),
        check_vma=False,
    )
```

profile of v0, /device:TPU:0, one launch (start us, length us, event | category | flops | bytes accessed | tf_op | source)
XLA Modules:
  0.0 509.6 jit_solution(14115927774698587419)
XLA Ops:
  24.3 27.7 %while.39 = (s32[]{:T(128)}, f32[16,128,128]{2,1,0:T(8,128)}, s32[]{:T(128)}, s32[]{:T(128)}, f32[40,3,128]{2,1,0:T(4,128)S(1)}, /*index=5*/s32[32,4]{1,0:T(8,12...) while((s32[]{:T(128)}, f32[16,128,128]{2,1,0:T(8,128)}, ...), condition=%wide.region_5.6_spmd, body=%wide.region_2.0_spmd.sunk | while | flops 275219520 | bytes 3331651 | solution.py:117
  62.8 9.6 %all-gather.2.cloned.1.call-done = bf16[32,128,128]{2,1,0:T(8,128)(2,1)} async-done(((bf16[16,128,128]{2,1,0:T(8,128)(2,1)}), bf16[32,128,128]{2,1,0:T(8,128)(2,1)}) %all-gather.2.cloned.1.call-update) | async-done | bytes 1048592 | tf_op jit(solution)/shard_map/all_gather | solution.py:202
  75.4 5.6 %all-to-all-start = ((bf16[32,128,128]{2,1,0:T(8,128)(2,1)}), bf16[32,128,128]{2,1,0:T(8,128)(2,1)S(1)}, u32[]{:S(2)}, u32[]{:S(2)}) async-start(bf16[32,128,128]{2,1,0:T(8,128)(2,1)} %broadcast_select_fusion), calls=%async_computation | async-start | bytes 2097152 | tf_op jit(solution)/shard_map/all_to_all | solution.py:219
  82.2 21.7 %all-to-all-done = bf16[32,128,128]{2,1,0:T(8,128)(2,1)S(1)} async-done(((bf16[32,128,128]{2,1,0:T(8,128)(2,1)}), bf16[32,128,128]{2,1,0:T(8,128)(2,1)S(1)}, u32[]{:S(2)}, u32[]{:S(2)}) %all-to-all-start) | async-done | bytes 1048608 | tf_op jit(solution)/shard_map/all_to_all | solution.py:219
  105.3 229.3 %while.40 = (s32[]{:T(128)}, f32[25,2,128,128]{3,2,1,0:T(8,128)}, f32[25,2,1024,64]{3,2,1,0:T(8,128)}, f32[25,2,1024,64]{3,2,1,0:T(8,128)}, f32[1024,128]{0,1:T(...) while((s32[]{:T(128)}, f32[25,2,128,128]{3,2,1,0:T(8,128)}, ...), condition=%wide.region_7.8_spmd.clone.clone, body=%wide.region_6.7_spmd.clone.clone.sunk | while | flops 69478528 | bytes 5175257 | solution.py:130
  108.9 5.6 %fusion.100 = (f32[25,2,1024,64]{3,2,1,0:T(8,128)}, f32[25,2,1024,64]{3,2,1,0:T(8,128)}) fusion(f32[25,2,1024,64]{3,2,1,0:T(8,128)} %get-tuple-element.632, s32[]{:T(128)} %get-tuple-element.629, f32[64]{0:T(128)S(1)} %add_multiply_fusion.2, f32[2,1024]{1,0:T(2,128)S(1)} %multiply_add_fusion.6, f32[25,2,1024,64]{3,2,1,0:T(8,128)} %get-tuple-element.631), kind=kLoop, calls=%fused_computation.43.clone.1 | loop fusion | flops 131072 | bytes 2106112 | tf_op jit(solution)/shard_map/while/body/jit(dynamic_update_index_in_dim)/dynamic_update_slice | solution.py:130
  118.1 5.6 %fusion.100 = (f32[25,2,1024,64]{3,2,1,0:T(8,128)}, f32[25,2,1024,64]{3,2,1,0:T(8,128)}) fusion(f32[25,2,1024,64]{3,2,1,0:T(8,128)} %get-tuple-element.632, s32[]{:T(128)} %get-tuple-element.629, f32[64]{0:T(128)S(1)} %add_multiply_fusion.2, f32[2,1024]{1,0:T(2,128)S(1)} %multiply_add_fusion.6, f32[25,2,1024,64]{3,2,1,0:T(8,128)} %get-tuple-element.631), kind=kLoop, calls=%fused_computation.43.clone.1 | loop fusion | flops 131072 | bytes 2106112 | tf_op jit(solution)/shard_map/while/body/jit(dynamic_update_index_in_dim)/dynamic_update_slice | solution.py:130
  127.2 5.6 %fusion.100 = (f32[25,2,1024,64]{3,2,1,0:T(8,128)}, f32[25,2,1024,64]{3,2,1,0:T(8,128)}) fusion(f32[25,2,1024,64]{3,2,1,0:T(8,128)} %get-tuple-element.632, s32[]{:T(128)} %get-tuple-element.629, f32[64]{0:T(128)S(1)} %add_multiply_fusion.2, f32[2,1024]{1,0:T(2,128)S(1)} %multiply_add_fusion.6, f32[25,2,1024,64]{3,2,1,0:T(8,128)} %get-tuple-element.631), kind=kLoop, calls=%fused_computation.43.clone.1 | loop fusion | flops 131072 | bytes 2106112 | tf_op jit(solution)/shard_map/while/body/jit(dynamic_update_index_in_dim)/dynamic_update_slice | solution.py:130
  136.4 5.6 %fusion.100 = (f32[25,2,1024,64]{3,2,1,0:T(8,128)}, f32[25,2,1024,64]{3,2,1,0:T(8,128)}) fusion(f32[25,2,1024,64]{3,2,1,0:T(8,128)} %get-tuple-element.632, s32[]{:T(128)} %get-tuple-element.629, f32[64]{0:T(128)S(1)} %add_multiply_fusion.2, f32[2,1024]{1,0:T(2,128)S(1)} %multiply_add_fusion.6, f32[25,2,1024,64]{3,2,1,0:T(8,128)} %get-tuple-element.631), kind=kLoop, calls=%fused_computation.43.clone.1 | loop fusion | flops 131072 | bytes 2106112 | tf_op jit(solution)/shard_map/while/body/jit(dynamic_update_index_in_dim)/dynamic_update_slice | solution.py:130
  145.6 5.6 %fusion.100 = (f32[25,2,1024,64]{3,2,1,0:T(8,128)}, f32[25,2,1024,64]{3,2,1,0:T(8,128)}) fusion(f32[25,2,1024,64]{3,2,1,0:T(8,128)} %get-tuple-element.632, s32[]{:T(128)} %get-tuple-element.629, f32[64]{0:T(128)S(1)} %add_multiply_fusion.2, f32[2,1024]{1,0:T(2,128)S(1)} %multiply_add_fusion.6, f32[25,2,1024,64]{3,2,1,0:T(8,128)} %get-tuple-element.631), kind=kLoop, calls=%fused_computation.43.clone.1 | loop fusion | flops 131072 | bytes 2106112 | tf_op jit(solution)/shard_map/while/body/jit(dynamic_update_index_in_dim)/dynamic_update_slice | solution.py:130
  154.7 5.6 %fusion.100 = (f32[25,2,1024,64]{3,2,1,0:T(8,128)}, f32[25,2,1024,64]{3,2,1,0:T(8,128)}) fusion(f32[25,2,1024,64]{3,2,1,0:T(8,128)} %get-tuple-element.632, s32[]{:T(128)} %get-tuple-element.629, f32[64]{0:T(128)S(1)} %add_multiply_fusion.2, f32[2,1024]{1,0:T(2,128)S(1)} %multiply_add_fusion.6, f32[25,2,1024,64]{3,2,1,0:T(8,128)} %get-tuple-element.631), kind=kLoop, calls=%fused_computation.43.clone.1 | loop fusion | flops 131072 | bytes 2106112 | tf_op jit(solution)/shard_map/while/body/jit(dynamic_update_index_in_dim)/dynamic_update_slice | solution.py:130
  163.9 5.6 %fusion.100 = (f32[25,2,1024,64]{3,2,1,0:T(8,128)}, f32[25,2,1024,64]{3,2,1,0:T(8,128)}) fusion(f32[25,2,1024,64]{3,2,1,0:T(8,128)} %get-tuple-element.632, s32[]{:T(128)} %get-tuple-element.629, f32[64]{0:T(128)S(1)} %add_multiply_fusion.2, f32[2,1024]{1,0:T(2,128)S(1)} %multiply_add_fusion.6, f32[25,2,1024,64]{3,2,1,0:T(8,128)} %get-tuple-element.631), kind=kLoop, calls=%fused_computation.43.clone.1 | loop fusion | flops 131072 | bytes 2106112 | tf_op jit(solution)/shard_map/while/body/jit(dynamic_update_index_in_dim)/dynamic_update_slice | solution.py:130
  173.1 5.6 %fusion.100 = (f32[25,2,1024,64]{3,2,1,0:T(8,128)}, f32[25,2,1024,64]{3,2,1,0:T(8,128)}) fusion(f32[25,2,1024,64]{3,2,1,0:T(8,128)} %get-tuple-element.632, s32[]{:T(128)} %get-tuple-element.629, f32[64]{0:T(128)S(1)} %add_multiply_fusion.2, f32[2,1024]{1,0:T(2,128)S(1)} %multiply_add_fusion.6, f32[25,2,1024,64]{3,2,1,0:T(8,128)} %get-tuple-element.631), kind=kLoop, calls=%fused_computation.43.clone.1 | loop fusion | flops 131072 | bytes 2106112 | tf_op jit(solution)/shard_map/while/body/jit(dynamic_update_index_in_dim)/dynamic_update_slice | solution.py:130
  182.3 5.6 %fusion.100 = (f32[25,2,1024,64]{3,2,1,0:T(8,128)}, f32[25,2,1024,64]{3,2,1,0:T(8,128)}) fusion(f32[25,2,1024,64]{3,2,1,0:T(8,128)} %get-tuple-element.632, s32[]{:T(128)} %get-tuple-element.629, f32[64]{0:T(128)S(1)} %add_multiply_fusion.2, f32[2,1024]{1,0:T(2,128)S(1)} %multiply_add_fusion.6, f32[25,2,1024,64]{3,2,1,0:T(8,128)} %get-tuple-element.631), kind=kLoop, calls=%fused_computation.43.clone.1 | loop fusion | flops 131072 | bytes 2106112 | tf_op jit(solution)/shard_map/while/body/jit(dynamic_update_index_in_dim)/dynamic_update_slice | solution.py:130
  191.5 5.6 %fusion.100 = (f32[25,2,1024,64]{3,2,1,0:T(8,128)}, f32[25,2,1024,64]{3,2,1,0:T(8,128)}) fusion(f32[25,2,1024,64]{3,2,1,0:T(8,128)} %get-tuple-element.632, s32[]{:T(128)} %get-tuple-element.629, f32[64]{0:T(128)S(1)} %add_multiply_fusion.2, f32[2,1024]{1,0:T(2,128)S(1)} %multiply_add_fusion.6, f32[25,2,1024,64]{3,2,1,0:T(8,128)} %get-tuple-element.631), kind=kLoop, calls=%fused_computation.43.clone.1 | loop fusion | flops 131072 | bytes 2106112 | tf_op jit(solution)/shard_map/while/body/jit(dynamic_update_index_in_dim)/dynamic_update_slice | solution.py:130
  200.6 5.6 %fusion.100 = (f32[25,2,1024,64]{3,2,1,0:T(8,128)}, f32[25,2,1024,64]{3,2,1,0:T(8,128)}) fusion(f32[25,2,1024,64]{3,2,1,0:T(8,128)} %get-tuple-element.632, s32[]{:T(128)} %get-tuple-element.629, f32[64]{0:T(128)S(1)} %add_multiply_fusion.2, f32[2,1024]{1,0:T(2,128)S(1)} %multiply_add_fusion.6, f32[25,2,1024,64]{3,2,1,0:T(8,128)} %get-tuple-element.631), kind=kLoop, calls=%fused_computation.43.clone.1 | loop fusion | flops 131072 | bytes 2106112 | tf_op jit(solution)/shard_map/while/body/jit(dynamic_update_index_in_dim)/dynamic_update_slice | solution.py:130
  209.8 5.6 %fusion.100 = (f32[25,2,1024,64]{3,2,1,0:T(8,128)}, f32[25,2,1024,64]{3,2,1,0:T(8,128)}) fusion(f32[25,2,1024,64]{3,2,1,0:T(8,128)} %get-tuple-element.632, s32[]{:T(128)} %get-tuple-element.629, f32[64]{0:T(128)S(1)} %add_multiply_fusion.2, f32[2,1024]{1,0:T(2,128)S(1)} %multiply_add_fusion.6, f32[25,2,1024,64]{3,2,1,0:T(8,128)} %get-tuple-element.631), kind=kLoop, calls=%fused_computation.43.clone.1 | loop fusion | flops 131072 | bytes 2106112 | tf_op jit(solution)/shard_map/while/body/jit(dynamic_update_index_in_dim)/dynamic_update_slice | solution.py:130
  219.0 5.6 %fusion.100 = (f32[25,2,1024,64]{3,2,1,0:T(8,128)}, f32[25,2,1024,64]{3,2,1,0:T(8,128)}) fusion(f32[25,2,1024,64]{3,2,1,0:T(8,128)} %get-tuple-element.632, s32[]{:T(128)} %get-tuple-element.629, f32[64]{0:T(128)S(1)} %add_multiply_fusion.2, f32[2,1024]{1,0:T(2,128)S(1)} %multiply_add_fusion.6, f32[25,2,1024,64]{3,2,1,0:T(8,128)} %get-tuple-element.631), kind=kLoop, calls=%fused_computation.43.clone.1 | loop fusion | flops 131072 | bytes 2106112 | tf_op jit(solution)/shard_map/while/body/jit(dynamic_update_index_in_dim)/dynamic_update_slice | solution.py:130
  228.1 5.6 %fusion.100 = (f32[25,2,1024,64]{3,2,1,0:T(8,128)}, f32[25,2,1024,64]{3,2,1,0:T(8,128)}) fusion(f32[25,2,1024,64]{3,2,1,0:T(8,128)} %get-tuple-element.632, s32[]{:T(128)} %get-tuple-element.629, f32[64]{0:T(128)S(1)} %add_multiply_fusion.2, f32[2,1024]{1,0:T(2,128)S(1)} %multiply_add_fusion.6, f32[25,2,1024,64]{3,2,1,0:T(8,128)} %get-tuple-element.631), kind=kLoop, calls=%fused_computation.43.clone.1 | loop fusion | flops 131072 | bytes 2106112 | tf_op jit(solution)/shard_map/while/body/jit(dynamic_update_index_in_dim)/dynamic_update_slice | solution.py:130
  237.3 5.5 %fusion.100 = (f32[25,2,1024,64]{3,2,1,0:T(8,128)}, f32[25,2,1024,64]{3,2,1,0:T(8,128)}) fusion(f32[25,2,1024,64]{3,2,1,0:T(8,128)} %get-tuple-element.632, s32[]{:T(128)} %get-tuple-element.629, f32[64]{0:T(128)S(1)} %add_multiply_fusion.2, f32[2,1024]{1,0:T(2,128)S(1)} %multiply_add_fusion.6, f32[25,2,1024,64]{3,2,1,0:T(8,128)} %get-tuple-element.631), kind=kLoop, calls=%fused_computation.43.clone.1 | loop fusion | flops 131072 | bytes 2106112 | tf_op jit(solution)/shard_map/while/body/jit(dynamic_update_index_in_dim)/dynamic_update_slice | solution.py:130
  246.4 5.6 %fusion.100 = (f32[25,2,1024,64]{3,2,1,0:T(8,128)}, f32[25,2,1024,64]{3,2,1,0:T(8,128)}) fusion(f32[25,2,1024,64]{3,2,1,0:T(8,128)} %get-tuple-element.632, s32[]{:T(128)} %get-tuple-element.629, f32[64]{0:T(128)S(1)} %add_multiply_fusion.2, f32[2,1024]{1,0:T(2,128)S(1)} %multiply_add_fusion.6, f32[25,2,1024,64]{3,2,1,0:T(8,128)} %get-tuple-element.631), kind=kLoop, calls=%fused_computation.43.clone.1 | loop fusion | flops 131072 | bytes 2106112 | tf_op jit(solution)/shard_map/while/body/jit(dynamic_update_index_in_dim)/dynamic_update_slice | solution.py:130
  255.6 5.6 %fusion.100 = (f32[25,2,1024,64]{3,2,1,0:T(8,128)}, f32[25,2,1024,64]{3,2,1,0:T(8,128)}) fusion(f32[25,2,1024,64]{3,2,1,0:T(8,128)} %get-tuple-element.632, s32[]{:T(128)} %get-tuple-element.629, f32[64]{0:T(128)S(1)} %add_multiply_fusion.2, f32[2,1024]{1,0:T(2,128)S(1)} %multiply_add_fusion.6, f32[25,2,1024,64]{3,2,1,0:T(8,128)} %get-tuple-element.631), kind=kLoop, calls=%fused_computation.43.clone.1 | loop fusion | flops 131072 | bytes 2106112 | tf_op jit(solution)/shard_map/while/body/jit(dynamic_update_index_in_dim)/dynamic_update_slice | solution.py:130
  264.8 5.6 %fusion.100 = (f32[25,2,1024,64]{3,2,1,0:T(8,128)}, f32[25,2,1024,64]{3,2,1,0:T(8,128)}) fusion(f32[25,2,1024,64]{3,2,1,0:T(8,128)} %get-tuple-element.632, s32[]{:T(128)} %get-tuple-element.629, f32[64]{0:T(128)S(1)} %add_multiply_fusion.2, f32[2,1024]{1,0:T(2,128)S(1)} %multiply_add_fusion.6, f32[25,2,1024,64]{3,2,1,0:T(8,128)} %get-tuple-element.631), kind=kLoop, calls=%fused_computation.43.clone.1 | loop fusion | flops 131072 | bytes 2106112 | tf_op jit(solution)/shard_map/while/body/jit(dynamic_update_index_in_dim)/dynamic_update_slice | solution.py:130
  273.9 5.6 %fusion.100 = (f32[25,2,1024,64]{3,2,1,0:T(8,128)}, f32[25,2,1024,64]{3,2,1,0:T(8,128)}) fusion(f32[25,2,1024,64]{3,2,1,0:T(8,128)} %get-tuple-element.632, s32[]{:T(128)} %get-tuple-element.629, f32[64]{0:T(128)S(1)} %add_multiply_fusion.2, f32[2,1024]{1,0:T(2,128)S(1)} %multiply_add_fusion.6, f32[25,2,1024,64]{3,2,1,0:T(8,128)} %get-tuple-element.631), kind=kLoop, calls=%fused_computation.43.clone.1 | loop fusion | flops 131072 | bytes 2106112 | tf_op jit(solution)/shard_map/while/body/jit(dynamic_update_index_in_dim)/dynamic_update_slice | solution.py:130
  283.1 5.6 %fusion.100 = (f32[25,2,1024,64]{3,2,1,0:T(8,128)}, f32[25,2,1024,64]{3,2,1,0:T(8,128)}) fusion(f32[25,2,1024,64]{3,2,1,0:T(8,128)} %get-tuple-element.632, s32[]{:T(128)} %get-tuple-element.629, f32[64]{0:T(128)S(1)} %add_multiply_fusion.2, f32[2,1024]{1,0:T(2,128)S(1)} %multiply_add_fusion.6, f32[25,2,1024,64]{3,2,1,0:T(8,128)} %get-tuple-element.631), kind=kLoop, calls=%fused_computation.43.clone.1 | loop fusion | flops 131072 | bytes 2106112 | tf_op jit(solution)/shard_map/while/body/jit(dynamic_update_index_in_dim)/dynamic_update_slice | solution.py:130
  292.2 5.6 %fusion.100 = (f32[25,2,1024,64]{3,2,1,0:T(8,128)}, f32[25,2,1024,64]{3,2,1,0:T(8,128)}) fusion(f32[25,2,1024,64]{3,2,1,0:T(8,128)} %get-tuple-element.632, s32[]{:T(128)} %get-tuple-element.629, f32[64]{0:T(128)S(1)} %add_multiply_fusion.2, f32[2,1024]{1,0:T(2,128)S(1)} %multiply_add_fusion.6, f32[25,2,1024,64]{3,2,1,0:T(8,128)} %get-tuple-element.631), kind=kLoop, calls=%fused_computation.43.clone.1 | loop fusion | flops 131072 | bytes 2106112 | tf_op jit(solution)/shard_map/while/body/jit(dynamic_update_index_in_dim)/dynamic_update_slice | solution.py:130
  301.4 5.6 %fusion.100 = (f32[25,2,1024,64]{3,2,1,0:T(8,128)}, f32[25,2,1024,64]{3,2,1,0:T(8,128)}) fusion(f32[25,2,1024,64]{3,2,1,0:T(8,128)} %get-tuple-element.632, s32[]{:T(128)} %get-tuple-element.629, f32[64]{0:T(128)S(1)} %add_multiply_fusion.2, f32[2,1024]{1,0:T(2,128)S(1)} %multiply_add_fusion.6, f32[25,2,1024,64]{3,2,1,0:T(8,128)} %get-tuple-element.631), kind=kLoop, calls=%fused_computation.43.clone.1 | loop fusion | flops 131072 | bytes 2106112 | tf_op jit(solution)/shard_map/while/body/jit(dynamic_update_index_in_dim)/dynamic_update_slice | solution.py:130
  310.6 5.6 %fusion.100 = (f32[25,2,1024,64]{3,2,1,0:T(8,128)}, f32[25,2,1024,64]{3,2,1,0:T(8,128)}) fusion(f32[25,2,1024,64]{3,2,1,0:T(8,128)} %get-tuple-element.632, s32[]{:T(128)} %get-tuple-element.629, f32[64]{0:T(128)S(1)} %add_multiply_fusion.2, f32[2,1024]{1,0:T(2,128)S(1)} %multiply_add_fusion.6, f32[25,2,1024,64]{3,2,1,0:T(8,128)} %get-tuple-element.631), kind=kLoop, calls=%fused_computation.43.clone.1 | loop fusion | flops 131072 | bytes 2106112 | tf_op jit(solution)/shard_map/while/body/jit(dynamic_update_index_in_dim)/dynamic_update_slice | solution.py:130
  319.8 5.6 %fusion.100 = (f32[25,2,1024,64]{3,2,1,0:T(8,128)}, f32[25,2,1024,64]{3,2,1,0:T(8,128)}) fusion(f32[25,2,1024,64]{3,2,1,0:T(8,128)} %get-tuple-element.632, s32[]{:T(128)} %get-tuple-element.629, f32[64]{0:T(128)S(1)} %add_multiply_fusion.2, f32[2,1024]{1,0:T(2,128)S(1)} %multiply_add_fusion.6, f32[25,2,1024,64]{3,2,1,0:T(8,128)} %get-tuple-element.631), kind=kLoop, calls=%fused_computation.43.clone.1 | loop fusion | flops 131072 | bytes 2106112 | tf_op jit(solution)/shard_map/while/body/jit(dynamic_update_index_in_dim)/dynamic_update_slice | solution.py:130
  329.0 5.6 %fusion.100 = (f32[25,2,1024,64]{3,2,1,0:T(8,128)}, f32[25,2,1024,64]{3,2,1,0:T(8,128)}) fusion(f32[25,2,1024,64]{3,2,1,0:T(8,128)} %get-tuple-element.632, s32[]{:T(128)} %get-tuple-element.629, f32[64]{0:T(128)S(1)} %add_multiply_fusion.2, f32[2,1024]{1,0:T(2,128)S(1)} %multiply_add_fusion.6, f32[25,2,1024,64]{3,2,1,0:T(8,128)} %get-tuple-element.631), kind=kLoop, calls=%fused_computation.43.clone.1 | loop fusion | flops 131072 | bytes 2106112 | tf_op jit(solution)/shard_map/while/body/jit(dynamic_update_index_in_dim)/dynamic_update_slice | solution.py:130
  334.6 83.7 %all-reduce.1 = bf16[50,128,128]{2,1,0:T(8,128)(2,1)} all-reduce(f32[50,128,128]{2,1,0:T(8,128)} %bitcast.105), channel_id=1, replica_groups=mesh['cell'=16,'dir'=2] {'cell','dir'}, use_global_device_ids=true, to_apply=%region_8.9 | all-reduce | flops 819200 | bytes 4915200 | tf_op jit(solution)/shard_map/psum | solution.py:253
  418.3 83.5 %while.41 = (s32[]{:T(128)}, f32[1024,128]{1,0:T(8,128)S(1)}, f32[1024,128]{1,0:T(8,128)S(1)}, f32[25,2,1024,64]{3,2,1,0:T(8,128)}, f32[25,2,1024,64]{3,2,1,0:T(...) while((s32[]{:T(128)}, f32[1024,128]{1,0:T(8,128)S(1)}, ...), condition=%wide.region_10.11_spmd.clone, body=%wide.region_9.10_spmd.clone.sunk | while | flops 69468160 | bytes 4784739 | solution.py:148
  (441 shorter events, 233.2 us)
Async XLA Ops:
  6.5 98.1 %copy-start = (bf16[128,384]{1,0:T(8,128)(2,1)S(1)}, bf16[128,384]{1,0:T(8,128)(2,1)}, u32[]{:S(2)}) copy-start(bf16[128,384]{1,0:T(8,128)(2,1)} %param.20) | copy-start | bytes 294916
  6.5 17.7 %copy-start.7 = (f32[8,128]{1,0:T(8,128)S(1)}, f32[8,128]{1,0:T(8,128)}, u32[]{:S(2)}) copy-start(f32[8,128]{1,0:T(8,128)} %param.18) | copy-start | bytes 12292
  6.5 65.8 %all-gather.2.cloned.1.call-start = ((), (), s32[]{:S(2)}) async-start(), calls=%async_computation.2 | async-start | bytes 1572864 | tf_op jit(solution)/shard_map/all_gather | solution.py:202
  7.3 14.4 %collective-permute-start = (bf16[4,3,128]{2,0,1:T(4,128)(2,1)S(1)}, bf16[4,3,128]{2,0,1:T(4,128)(2,1)S(1)}, u32[]{:S(2)}, u32[]{:S(2)}) collective-permute-start(bf16[4,3,128]{2,0,1:T(4,128)(2,1)S(1)} %slice.58), channel_id=1, source_target_pairs={{0,2},{2,4},{4,6},{6,8},{8,10},{10,12},{12,14},{14,16},{16,18},{18... | collective-permute-start | bytes 9224 | tf_op jit(solution)/shard_map/ppermute | solution.py:24
  7.8 13.9 %collective-permute-start.1 = (bf16[4,3,128]{2,0,1:T(4,128)(2,1)S(1)}, bf16[4,3,128]{2,0,1:T(4,128)(2,1)S(1)}, u32[]{:S(2)}, u32[]{:S(2)}) collective-permute-start(bf16[4,3,128]{2,0,1:T(4,128)(2,1)S(1)} %slice.58), channel_id=1, source_target_pairs={{2,0},{4,2},{6,4},{8,6},{10,8},{12,10},{14,12},{16,14},{18,16},{20... | collective-permute-start | bytes 9224 | tf_op jit(solution)/shard_map/ppermute | solution.py:26
  13.7 8.1 %collective-permute-start.2 = (bf16[4,128,128]{2,1,0:T(8,128)(2,1)S(1)}, bf16[4,128,128]{2,1,0:T(8,128)(2,1)S(1)}, u32[]{:S(2)}, u32[]{:S(2)}) collective-permute-start(bf16[4,128,128]{2,1,0:T(8,128)(2,1)S(1)} %slice.61), channel_id=1, source_target_pairs={{0,2},{2,4},{4,6},{6,8},{8,10},{10,12},{12,14},{14,16},{16,18},{18... | collective-permute-start | bytes 393224 | tf_op jit(solution)/shard_map/ppermute | solution.py:24
  13.7 8.0 %collective-permute-start.3 = (bf16[4,128,128]{2,1,0:T(8,128)(2,1)S(1)}, bf16[4,128,128]{2,1,0:T(8,128)(2,1)S(1)}, u32[]{:S(2)}, u32[]{:S(2)}) collective-permute-start(bf16[4,128,128]{2,1,0:T(8,128)(2,1)S(1)} %slice.61), channel_id=1, source_target_pairs={{2,0},{4,2},{6,4},{8,6},{10,8},{12,10},{14,12},{16,14},{18,16},{20... | collective-permute-start | bytes 393224 | tf_op jit(solution)/shard_map/ppermute | solution.py:26
  24.3 27.7 %copy-start.3 = (bf16[32,128,128]{2,1,0:T(8,128)(2,1)S(1)}, bf16[32,128,128]{2,1,0:T(8,128)(2,1)}, u32[]{:S(2)}) copy-start(bf16[32,128,128]{2,1,0:T(8,128)(2,1)} %param.14) | copy-start | bytes 3145732
  24.3 27.7 %copy-start.6 = (bf16[128,128]{1,0:T(8,128)(2,1)S(1)}, bf16[128,128]{1,0:T(8,128)(2,1)}, u32[]{:S(2)}) copy-start(bf16[128,128]{1,0:T(8,128)(2,1)} %param.19) | copy-start | bytes 98308
  51.9 2.5 copy-start.5
  51.9 4.7 copy-start.2
  59.3 16.2 %all-to-all-start.1 = ((bf16[32,3,128]{2,1,0:T(4,128)(2,1)}), bf16[32,3,128]{2,1,0:T(4,128)(2,1)S(1)}, u32[]{:S(2)}, u32[]{:S(2)}) async-start(bf16[32,3,128]{2,1,0:T(4,128)(2,1)} %copy.37), calls=%async_computation.1 | async-start | bytes 65536 | tf_op jit(solution)/shard_map/all_to_all | solution.py:220
  75.4 28.5 %all-to-all-start = ((bf16[32,128,128]{2,1,0:T(8,128)(2,1)}), bf16[32,128,128]{2,1,0:T(8,128)(2,1)S(1)}, u32[]{:S(2)}, u32[]{:S(2)}) async-start(bf16[32,128,128]{2,1,0:T(8,128)(2,1)} %broadcast_select_fusion), calls=%async_computation | async-start | bytes 2097152 | tf_op jit(solution)/shard_map/all_to_all | solution.py:219
  418.3 83.5 %copy-start.4 = (bf16[128,128]{1,0:T(8,128)(2,1)S(1)}, bf16[128,128]{1,0:T(8,128)(2,1)}, u32[]{:S(2)}) copy-start(bf16[128,128]{1,0:T(8,128)(2,1)} %param.21) | copy-start | bytes 98308
  501.8 0.9 copy-start.1
Sparse Core Ops, SparseCore 0:
  54.5 17.7 all-gather.1
where the time goes:
time: 514 us; the launch traced here: 510 us
  other arithmetic  253 us (49%)
  blocking collectives  83.7 us (16%)
  matrix products  68.5 us (13%)
  local copies, waits for them, and re-layouts  37.8 us (7%)
  waiting for transfers between devices  31.3 us (6%)
  starting transfers between devices  19.1 us (4%)
  between operations  14.3 us (3%)
    dynamic_update_slice x25, other arithmetic, kv_states(): carried, outputs = lax.scan(kv_advance, jnp.float32(0.0), dir_groups)  140 us
    another operation x54, other arithmetic  103 us
    psum x1, blocking collectives, per_device(): states = lax.psum(local_states, ('cell', 'dir')).astype(jnp.bfloat16)  83.7 us
    dot_general x25, matrix products, query_advance(): jnp.einsum('grf,gfh->rh', query_rot, group_states, preferred_element_type...  32.1 us
    dot_general x25, matrix products, kv_advance(): jnp.einsum('grf,rh->gfh', key_rot, values, preferred_element_type=jnp.flo...  23.8 us
    all_to_all x1, waiting for transfers between devices, per_device(): lax.all_to_all(send_features, 'cell', split_axis=0, concat_axis=0, tiled=...  21.7 us
  transfers between devices with their start and end apart: 7, of which 2 were waited for; matrix products, arithmetic and copies ran while one was open for 3% of the time, Pallas kernels for 0%

commit v1 on v0

--- a/solution.py
+++ b/solution.py
@@ -1,8 +1,12 @@
+import functools
 import math
 
 import jax
 import jax.numpy as jnp
+import numpy as np
 from jax import lax
+from jax.experimental import pallas as pl
+from jax.experimental.pallas import tpu as pltpu
 from jax.sharding import PartitionSpec as P
 
 DIRS = 50
@@ -35,44 +39,179 @@
     return positions_in + amount * marker[:, None]
 
 
-def direction_table(total):
-    dir_order = jnp.arange(total, dtype=jnp.float32)
-    height = 1.0 - (2.0 * dir_order + 1.0) / total
-    radius = jnp.sqrt(1.0 - height * height)
-    turning = dir_order * golden_turn
-    return jnp.stack([radius * jnp.cos(turning), radius * jnp.sin(turning), height], axis=1)
-
-
-def half_frequencies(width):
-    half_width = width // 2
-    return 0.5 * (jnp.arange(half_width, dtype=jnp.float32) + 1.0) / half_width
-
-
-def phases(coords, directions, frequencies):
-    projected = (
-        directions[:, 0:1] * coords[0][None]
-        + directions[:, 1:2] * coords[1][None]
-        + directions[:, 2:3] * coords[2][None]
-    )
-    return projected[:, :, None] * frequencies
-
-
-def rotate_with(values, cosine, sine):
-    half_width = values.shape[-1] // 2
-    first_half = values[None, :, :half_width]
-    second_half = values[None, :, half_width:]
-    turned = jnp.concatenate(
-        [first_half * cosine - second_half * sine, second_half * cosine + first_half * sine],
-        axis=-1,
-    )
-    return turned.astype(jnp.bfloat16)
-
-
-def group_size(count):
-    for candidate in range(1, count + 1):
-        if count % candidate == 0 and count // candidate <= 25:
-            return candidate
-    return count
+def direction_rows(total):
+    order = np.arange(total, dtype=np.float64)
+    height = 1.0 - (2.0 * order + 1.0) / total
+    radius = np.sqrt(1.0 - height * height)
+    turning = order * golden_turn
+    padded = -(-total // 8) * 8
+    table = np.zeros((padded, 128), np.float32)
+    table[:total, 0] = radius * np.cos(turning)
+    table[:total, 1] = radius * np.sin(turning)
+    table[:total, 2] = height
+    table[:total, 3] = 1.0
+    return table
+
+
+def rotated_groups(table, coords, source, half, group, emit):
+    base = (
+        table[:, 0:1] * coords[0:1] + table[:, 1:2] * coords[1:2] + table[:, 2:3] * coords[2:3]
+    ) * (0.5 / half)
+    alive = jnp.broadcast_to(table[:, 3:4], base.shape)
+    c1, s1 = jnp.cos(base), jnp.sin(base)
+    c2, s2 = c1 * c1 - s1 * s1, 2.0 * (s1 * c1)
+    c3, s3 = c2 * c1 - s2 * s1, s2 * c1 + c2 * s1
+    c4, s4 = c2 * c2 - s2 * s2, 2.0 * (s2 * c2)
+    step = 2.0 * c4
+    c1, s1, c2, s2, c3, s3, c4, s4 = [v * alive for v in (c1, s1, c2, s2, c3, s3, c4, s4)]
+    zero = jnp.zeros_like(alive)
+    older = [(c3, -s3), (c2, -s2), (c1, -s1), (alive, zero)]
+    newer = [(c1, s1), (c2, s2), (c3, s3), (c4, s4)]
+    for first in range(0, half, group):
+        low, high = [], []
+        for p in range(first, first + group):
+            if p >= 4:
+                lane = p % 4
+                cosine = step * newer[lane][0] - older[lane][0]
+                sine = step * newer[lane][1] - older[lane][1]
+                older[lane] = newer[lane]
+                newer[lane] = (cosine, sine)
+            cosine, sine = newer[p % 4]
+            a = source(p)
+            b = source(p + half)
+            low.append(a * cosine - b * sine)
+            high.append(b * cosine + a * sine)
+        emit(first // group, jnp.concatenate(low + high, axis=0).astype(jnp.bfloat16))
+
+
+def kv_kernel(group, chunk, table_ref, coords_ref, rows_ref, weights_t_ref, weights_ref, states_ref, keys, values):
+    width = rows_ref.shape[1]
+    half = width // 2
+    atoms = rows_ref.shape[0]
+
+    @pl.when(pl.program_id(0) == 0)
+    def _():
+        keys[...] = lax.dot_general(
+            weights_t_ref[width : 2 * width, :], rows_ref[...], (((1,), (1,)), ((), ())),
+            preferred_element_type=jnp.float32,
+        )
+        values[...] = jnp.dot(
+            rows_ref[...], weights_ref[:, 2 * width :], preferred_element_type=jnp.float32
+        ).astype(jnp.bfloat16)
+
+    states_ref[...] = jnp.zeros_like(states_ref)
+    size = group * 16
+
+    def advance(turn, carried):
+        at = pl.ds(pl.multiple_of(turn * chunk, chunk), chunk)
+        value_rows = values[at, :]
+
+        def emit(index, turned):
+            states_ref[0, index * size : (index + 1) * size, :] += jnp.dot(
+                turned, value_rows, preferred_element_type=jnp.float32
+            )
+
+        rotated_groups(
+            table_ref[...], coords_ref[:, at],
+            lambda p: jnp.broadcast_to(keys[p : p + 1, at], (8, chunk)), half, group, emit,
+        )
+        return carried
+
+    lax.fori_loop(0, atoms // chunk, advance, 0)
+
+
+def query_kernel(group, chunk, scale, table_ref, coords_ref, rows_ref, weights_t_ref, output_ref, states_ref, out_ref, queries, total):
+    width = rows_ref.shape[1]
+    half = width // 2
+    atoms = rows_ref.shape[0]
+
+    @pl.when(pl.program_id(0) == 0)
+    def _():
+        queries[...] = lax.dot_general(
+            weights_t_ref[:width, :], rows_ref[...], (((1,), (1,)), ((), ())),
+            preferred_element_type=jnp.float32,
+        )
+        total[...] = jnp.zeros_like(total)
+
+    size = group * 16
+    flipped = states_ref[0].T
+
+    def advance(turn, carried):
+        at = pl.ds(pl.multiple_of(turn * chunk, chunk), chunk)
+        parts = []
+
+        def emit(index, turned):
+            parts.append(
+                jnp.dot(
+                    flipped[:, index * size : (index + 1) * size], turned,
+                    preferred_element_type=jnp.float32,
+                )
+            )
+
+        rotated_groups(
+            table_ref[...], coords_ref[:, at],
+            lambda p: jnp.broadcast_to(queries[p : p + 1, at], (8, chunk)), half, group, emit,
+        )
+        total[:, at] += sum(parts[1:], parts[0])
+        return carried
+
+    lax.fori_loop(0, atoms // chunk, advance, 0)
+
+    @pl.when(pl.program_id(0) == pl.num_programs(0) - 1)
+    def _():
+        mixed = (total[...] * scale).T.astype(jnp.bfloat16)
+        out_ref[...] = jnp.dot(
+            mixed, output_ref[...], preferred_element_type=jnp.float32
+        ).astype(jnp.bfloat16)
+
+
+def whole(shape):
+    return pl.BlockSpec(shape, lambda i: (0,) * len(shape))
+
+
+def kv_states(table, coords, flat, weights_t, weights):
+    atoms, width = flat.shape
+    groups = table.shape[0] // 8
+    chunk = min(256, atoms)
+    group = 16
+    return pl.pallas_call(
+        functools.partial(kv_kernel, group, chunk),
+        grid=(groups,),
+        out_shape=jax.ShapeDtypeStruct((groups, width * 8, width), jnp.float32),
+        in_specs=[
+            pl.BlockSpec((8, 128), lambda i: (i, 0)),
+            whole(coords.shape),
+            whole(flat.shape),
+            whole(weights_t.shape),
+            whole(weights.shape),
+        ],
+        out_specs=pl.BlockSpec((1, width * 8, width), lambda i: (i, 0, 0)),
+        scratch_shapes=[pltpu.VMEM((width, atoms), jnp.float32), pltpu.VMEM((atoms, width), jnp.bfloat16)],
+        name="kv_states",
+    )(table, coords, flat, weights_t, weights)
+
+
+def query_mix(table, coords, flat, weights_t, w_output, states, scale):
+    atoms, width = flat.shape
+    groups = table.shape[0] // 8
+    chunk = min(256, atoms)
+    group = 16
+    return pl.pallas_call(
+        functools.partial(query_kernel, group, chunk, scale),
+        grid=(groups,),
+        out_shape=jax.ShapeDtypeStruct((atoms, width), jnp.bfloat16),
+        in_specs=[
+            pl.BlockSpec((8, 128), lambda i: (i, 0)),
+            whole(coords.shape),
+            whole(flat.shape),
+            whole(weights_t.shape),
+            whole(w_output.shape),
+            pl.BlockSpec((1, width * 8, width), lambda i: (i, 0, 0)),
+        ],
+        out_specs=whole((atoms, width)),
+        scratch_shapes=[pltpu.VMEM((width, atoms), jnp.float32), pltpu.VMEM((width, atoms), jnp.float32)],
+        name="query_mix",
+    )(table, coords, flat, weights_t, w_output, states)
 
 
 def radial_terms(own_positions, near_positions, near_features, filter_gains):
@@ -115,40 +254,6 @@
 
     group_total = (live_count + group_width - 1) // group_width
     return lax.fori_loop(0, group_total, block_advance, initial)
-
-
-def kv_states(keys_rows, values, coords, dir_groups, frequencies):
-
-    def kv_advance(carried, group_dirs):
-        angle = phases(coords, group_dirs, frequencies)
-        cosine = jnp.cos(angle)
-        sine = jnp.sin(angle)
-        key_rot = rotate_with(keys_rows, cosine, sine)
-        state = jnp.einsum("grf,rh->gfh", key_rot, values, preferred_element_type=jnp.float32)
-        return (carried, (state, cosine, sine))
-
-    carried, outputs = lax.scan(kv_advance, jnp.float32(0.0), dir_groups)
-    states, cosines, sines = outputs
-    return (states.reshape(-1, states.shape[-2], states.shape[-1]), cosines, sines)
-
-
-def query_mix(queries, cosines, sines, state_groups):
-
-    def query_advance(running, paired):
-        cosine, sine, group_states = paired
-        query_rot = rotate_with(queries, cosine, sine)
-        return (
-            running
-            + jnp.einsum(
-                "grf,gfh->rh", query_rot, group_states, preferred_element_type=jnp.float32
-            ),
-            None,
-        )
-
-    running, unused = lax.scan(
-        query_advance, jnp.zeros(queries.shape, jnp.float32), (cosines, sines, state_groups)
-    )
-    return running
 
 
 def per_device(
@@ -229,8 +334,6 @@
         received_positions[pick_rows].astype(jnp.float32),
         slab_width * source.astype(jnp.float32)[:, None, None],
     )
-    dir_table = direction_table(DIRS)
-    frequencies = half_frequencies(width)
     share_blocks = balanced_blocks // dirs_count
     rows_features = lax.dynamic_slice_in_dim(
         balanced_features, dir_index * share_blocks, share_blocks, 0
@@ -239,24 +342,13 @@
         balanced_positions, dir_index * share_blocks, share_blocks, 0
     )
     flat = rows_features.reshape(-1, width)
-    qkv = jnp.dot(flat, projections, preferred_element_type=jnp.float32)
     coords = jnp.transpose(rows_positions, (1, 0, 2)).reshape(3, -1)
-    queries, keys_rows, values, coords = (
-        qkv[:, :width],
-        qkv[:, width : 2 * width],
-        qkv[:, 2 * width :].astype(jnp.bfloat16),
-        coords,
-    )
-    group_width = group_size(DIRS)
-    dir_groups = dir_table.reshape(-1, group_width, 3)
-    local_states, cosines, sines = kv_states(keys_rows, values, coords, dir_groups, frequencies)
+    table = jnp.asarray(direction_rows(DIRS))
+    weights_t = projections.T
+    local_states = kv_states(table, coords, flat, weights_t, projections)
     states = lax.psum(local_states, ("cell", "dir")).astype(jnp.bfloat16)
-    mixed_rows = query_mix(
-        queries, cosines, sines, states.reshape(dir_groups.shape[0], group_width, width, width)
-    )
     mix_scale = 1.0 / math.sqrt(DIRS * cells * balanced_blocks * block_atoms * width)
-    mixed = (mixed_rows * mix_scale).astype(jnp.bfloat16)
-    attended = jnp.dot(mixed, w_output, preferred_element_type=jnp.float32).astype(jnp.bfloat16)
+    attended = query_mix(table, coords, flat, weights_t, w_output, states, mix_scale)
     return attended.reshape(-1, block_atoms, width)
 
 

time: 514 us -> 238 us (0.46)
  other arithmetic: 253 us -> 9.01 us
  matrix products: 68.5 us -> 11.4 us
  Pallas kernels: 0 us -> 35.6 us
  local copies, waits for them, and re-layouts: 37.8 us -> 28 us
    dynamic_update_slice x25 -> x0, other arithmetic: 140 us -> none  [kv_states(): carried, outputs = lax.scan(kv_advance, jnp.float32(0.0), dir_groups)]
    another operation x55 -> x2, other arithmetic: 103 us -> 0.16 us
    dot_general x52 -> x0, matrix products: 57.1 us -> none  [the longest x25 32.1 us: query_advance(): jnp.einsum('grf,gfh->rh', query_rot, group_states, preferred_element_type...]
    pallas_call x0 -> x2, Pallas kernels: none -> 35.6 us  [the longest x1 18.7 us: query_mix(): pl.pallas_call(functools.partial(query_kernel, group, chunk, scale), grid...]
    slice x102 -> x0, local copies, waits for them, and re-layouts: 11 us -> none  [the longest x50 6.02 us: rotate_with(): first_half = values[None, :, :half_width]]
  transfers between devices with their start and end apart: 7 -> 7, of which waited for: 2 -> 3; matrix products, arithmetic and copies ran while one was open for 3% -> 6% of each run, Pallas kernels for 0% -> 0%
where the time goes in v1:
time: 238 us; the launch traced here: 237 us
  blocking collectives  86.4 us (36%)
  Pallas kernels  35.6 us (15%)
  waiting for transfers between devices  33 us (14%)
  local copies, waits for them, and re-layouts  28 us (12%)
  starting transfers between devices  19.1 us (8%)
  between operations  14.2 us (6%)
  matrix products  11.4 us (5%)
  other arithmetic  9.01 us (4%)
    psum x1, blocking collectives, per_device(): states = lax.psum(local_states, ('cell', 'dir')).astype(jnp.bfloat16)  86.4 us
    all_to_all x1, waiting for transfers between devices, per_device(): lax.all_to_all(send_features, 'cell', split_axis=0, concat_axis=0, tiled=...  20.5 us
    pallas_call x1, Pallas kernels, query_mix(): pl.pallas_call(functools.partial(query_kernel, group, chunk, scale), grid...  18.7 us
    pallas_call x1, Pallas kernels, kv_states(): pl.pallas_call(functools.partial(kv_kernel, group, chunk), grid=(groups,)...  16.9 us
    ppermute x2, starting transfers between devices, extended(): lax.ppermute(head, axis, [((i + 1) % count, i) for i in range(count)])  9.96 us
    dot_general x8, matrix products, radial_terms(): jnp.einsum('gnkab,gnbf->gkaf', radial, near_features, preferred_element_t...  8.9 us
    all_gather x1, waiting for transfers between devices, per_device(): updated = lax.all_gather(updated_share, 'dir', axis=0, tiled=True)  8.89 us
    all_to_all x1, starting transfers between devices, per_device(): lax.all_to_all(send_features, 'cell', split_axis=0, concat_axis=0, tiled=...  5.62 us
  transfers between devices with their start and end apart: 7, of which 3 were waited for; matrix products, arithmetic and copies ran while one was open for 6% of the time, Pallas kernels for 0%

profile of v1, /device:TPU:0, one launch (start us, length us, event | category | flops | bytes accessed | tf_op | source)
XLA Modules:
  0.0 236.9 jit_solution(8235678138684261276)
XLA Ops:
  7.2 5.5 %collective-permute-start.1 = (bf16[4,3,128]{2,0,1:T(4,128)(2,1)S(1)}, bf16[4,3,128]{2,0,1:T(4,128)(2,1)S(1)}, u32[]{:S(2)}, u32[]{:S(2)}) collective-permute-start(bf16[4,3,128]{2,0,1:T(4,128)(2,1)S(1)} %slice.12), channel_id=1, source_target_pairs={{2,0},{4,2},{6,4},{8,6},{10,8},{12,10},{14,12},{16,14},{18,16},{20... | collective-permute-start | bytes 9224 | tf_op jit(solution)/shard_map/ppermute | solution.py:30
  12.7 0.9 slice.15
  13.6 4.5 %collective-permute-start.3 = (bf16[4,128,128]{2,1,0:T(8,128)(2,1)S(1)}, bf16[4,128,128]{2,1,0:T(8,128)(2,1)S(1)}, u32[]{:S(2)}, u32[]{:S(2)}) collective-permute-start(bf16[4,128,128]{2,1,0:T(8,128)(2,1)S(1)} %slice.15), channel_id=1, source_target_pairs={{2,0},{4,2},{6,4},{8,6},{10,8},{12,10},{14,12},{16,14},{18,16},{20... | collective-permute-start | bytes 393224 | tf_op jit(solution)/shard_map/ppermute | solution.py:30
  18.1 1.2 dynamic_slice.28
  20.0 0.7 convert_element_type.56
  20.8 0.8 copy.36
  21.7 3.5 %collective-permute-done.2 = bf16[4,128,128]{2,1,0:T(8,128)(2,1)S(1)} collective-permute-done((bf16[4,128,128]{2,1,0:T(8,128)(2,1)S(1)}, bf16[4,128,128]{2,1,0:T(8,128)(2,1)S(1)}, u32[]{:S(2)}, u32[]{:S(2)}) %collective-permute-start.2) | collective-permute-done | bytes 131104 | tf_op jit(solution)/shard_map/ppermute | solution.py:28
  25.2 1.4 pad_maximum_fusion
  26.6 1.1 broadcast_in_dim.43
  27.7 27.5 %while.12 = (s32[]{:T(128)}, f32[16,128,128]{2,1,0:T(8,128)}, s32[]{:T(128)}, s32[]{:T(128)}, f32[40,3,128]{2,1,0:T(4,128)S(1)}, /*index=5*/s32[32,4]{1,0:T(8,12...) while((s32[]{:T(128)}, f32[16,128,128]{2,1,0:T(8,128)}, ...), condition=%wide.region_5.6_spmd, body=%wide.region_2.0_spmd.sunk | while | flops 275219520 | bytes 3331651 | solution.py:256
  29.4 1.1 fusion.37
  32.8 1.1 fusion.37
  36.2 1.1 fusion.37
  39.7 1.1 fusion.37
  43.1 1.1 fusion.37
  46.6 1.1 fusion.37
  50.0 1.1 fusion.37
  53.4 1.1 fusion.37
  55.2 2.5 %fusion.14 = bf16[16,128,128]{2,1,0:T(8,128)(2,1)} fusion(f32[16,128,128]{2,1,0:T(8,128)} %get-tuple-element.109, bf16[32,128,128]{2,1,0:T(8,128)(2,1)S(1)} %copy-done.2, s32[]{:T(128)S(6)} %select_n.139, bf16[128,128]{1,0:T(8,128)(2,1)S(1)} %copy-done), kind=kOutput, calls=%fused_computation.22 | convolution fusion | flops 69206016 | bytes 2129924 | tf_op jit(solution)/shard_map/dot_general | solution.py:305
  58.6 1.3 fusion.25
  60.6 1.3 fusion.22
  62.6 3.5 %all-to-all-start = ((bf16[32,3,128]{2,1,0:T(4,128)(2,1)}), bf16[32,3,128]{2,1,0:T(4,128)(2,1)S(1)}, u32[]{:S(2)}, u32[]{:S(2)}) async-start(bf16[32,3,128]{2,1,0:T(4,128)(2,1)} %copy.34), calls=%async_computation | async-start | bytes 65536 | tf_op jit(solution)/shard_map/all_to_all | solution.py:325
  66.1 8.9 %all-gather.2.cloned.1.call-done = bf16[32,128,128]{2,1,0:T(8,128)(2,1)} async-done(((bf16[16,128,128]{2,1,0:T(8,128)(2,1)}), bf16[32,128,128]{2,1,0:T(8,128)(2,1)}) %all-gather.2.cloned.1.call-update) | async-done | bytes 1048592 | tf_op jit(solution)/shard_map/all_gather | solution.py:307
  75.0 2.0 gather_fusion.4
  77.0 1.1 broadcast_select_fusion
  78.1 5.6 %all-to-all-start.1 = ((bf16[32,128,128]{2,1,0:T(8,128)(2,1)}), bf16[32,128,128]{2,1,0:T(8,128)(2,1)S(1)}, u32[]{:S(2)}, u32[]{:S(2)}) async-start(bf16[32,128,128]{2,1,0:T(8,128)(2,1)} %broadcast_select_fusion), calls=%async_computation.1 | async-start | bytes 2097152 | tf_op jit(solution)/shard_map/all_to_all | solution.py:324
  83.8 0.8 copy.37
  86.1 20.5 %all-to-all-done.1 = bf16[32,128,128]{2,1,0:T(8,128)(2,1)S(1)} async-done(((bf16[32,128,128]{2,1,0:T(8,128)(2,1)}), bf16[32,128,128]{2,1,0:T(8,128)(2,1)S(1)}, u32[]{:S(2)}, u32[]{:S(2)}) %all-to-all-start.1) | async-done | bytes 1048608 | tf_op jit(solution)/shard_map/all_to_all | solution.py:324
  107.3 0.8 constant_dynamic-slice_fusion.1
  108.1 16.9 %kv_states.1 = f32[7,1024,128]{2,1,0:T(8,128)} custom-call(f32[56,128]{1,0:T(8,128)} %constant.154.clone.table_ref, f32[3,1024]{1,0:T(4,128)} %add_bitcast_fusion.coords_ref, bf16[1024,128]{1,0:T(8,128)(2,1)} %bitcast.44, bf16[384,128]{1,0:T(8,128)(2,1)} %bitcast.47, bf16[128,384]{1,0:T(8,128)(2,1)} %weights_ref.1), custom_call_target="tpu_custom_call" | custom-call | tf_op jit(solution)/shard_map/kv_states/pallas_call | solution.py:177
  125.0 86.4 %all-reduce.1.states_ref = bf16[7,1024,128]{2,1,0:T(8,128)(2,1)} all-reduce(f32[7,1024,128]{2,1,0:T(8,128)} %kv_states.1), channel_id=1, replica_groups=mesh['cell'=16,'dir'=2] {'cell','dir'}, use_global_device_ids=true, to_apply=%region_6.7 | all-reduce | flops 917504 | bytes 5505024 | tf_op jit(solution)/shard_map/psum | solution.py:349
  211.3 18.7 %query_mix.1 = bf16[1024,128]{1,0:T(8,128)(2,1)} custom-call(f32[56,128]{1,0:T(8,128)} %constant.154.clone.table_ref, f32[3,1024]{1,0:T(4,128)} %add_bitcast_fusion.coords_ref, bf16[1024,128]{1,0:T(8,128)(2,1)} %bitcast.45, bf16[384,128]{1,0:T(8,128)(2,1)} %bitcast.48, bf16[128,128]{1,0:T(8,128)(2,1)} %output_ref.1, bf16[7,1024,128]{2,1,0:T(8,128)(2,1)} %all-reduce.1.states_ref), custom_call_target="tpu_custom_call" | custom-call | tf_op jit(solution)/shard_map/query_mix/pallas_call | solution.py:199
  (125 shorter events, 23.7 us)
Async XLA Ops:
  6.5 48.7 %copy-start = (bf16[128,128]{1,0:T(8,128)(2,1)S(1)}, bf16[128,128]{1,0:T(8,128)(2,1)}, u32[]{:S(2)}) copy-start(bf16[128,128]{1,0:T(8,128)(2,1)} %param.16) | copy-start | bytes 98308
  6.5 68.5 %all-gather.2.cloned.1.call-start = ((), (), s32[]{:S(2)}) async-start(), calls=%async_computation.2 | async-start | bytes 1572864 | tf_op jit(solution)/shard_map/all_gather | solution.py:307
  7.2 14.3 %collective-permute-start.1 = (bf16[4,3,128]{2,0,1:T(4,128)(2,1)S(1)}, bf16[4,3,128]{2,0,1:T(4,128)(2,1)S(1)}, u32[]{:S(2)}, u32[]{:S(2)}) collective-permute-start(bf16[4,3,128]{2,0,1:T(4,128)(2,1)S(1)} %slice.12), channel_id=1, source_target_pairs={{2,0},{4,2},{6,4},{8,6},{10,8},{12,10},{14,12},{16,14},{18,16},{20... | collective-permute-start | bytes 9224 | tf_op jit(solution)/shard_map/ppermute | solution.py:30
  12.7 8.8 %collective-permute-start = (bf16[4,3,128]{2,0,1:T(4,128)(2,1)S(1)}, bf16[4,3,128]{2,0,1:T(4,128)(2,1)S(1)}, u32[]{:S(2)}, u32[]{:S(2)}) collective-permute-start(bf16[4,3,128]{2,0,1:T(4,128)(2,1)S(1)} %slice.12), channel_id=1, source_target_pairs={{0,2},{2,4},{4,6},{6,8},{8,10},{10,12},{12,14},{14,16},{16,18},{18... | collective-permute-start | bytes 9224 | tf_op jit(solution)/shard_map/ppermute | solution.py:28
  13.6 8.1 %collective-permute-start.3 = (bf16[4,128,128]{2,1,0:T(8,128)(2,1)S(1)}, bf16[4,128,128]{2,1,0:T(8,128)(2,1)S(1)}, u32[]{:S(2)}, u32[]{:S(2)}) collective-permute-start(bf16[4,128,128]{2,1,0:T(8,128)(2,1)S(1)} %slice.15), channel_id=1, source_target_pairs={{2,0},{4,2},{6,4},{8,6},{10,8},{12,10},{14,12},{16,14},{18,16},{20... | collective-permute-start | bytes 393224 | tf_op jit(solution)/shard_map/ppermute | solution.py:30
  18.1 7.1 %collective-permute-start.2 = (bf16[4,128,128]{2,1,0:T(8,128)(2,1)S(1)}, bf16[4,128,128]{2,1,0:T(8,128)(2,1)S(1)}, u32[]{:S(2)}, u32[]{:S(2)}) collective-permute-start(bf16[4,128,128]{2,1,0:T(8,128)(2,1)S(1)} %slice.15), channel_id=1, source_target_pairs={{0,2},{2,4},{4,6},{6,8},{8,10},{10,12},{12,14},{14,16},{16,18},{18... | collective-permute-start | bytes 393224 | tf_op jit(solution)/shard_map/ppermute | solution.py:28
  21.7 6.0 %copy-start.5 = (f32[8,128]{1,0:T(8,128)S(1)}, f32[8,128]{1,0:T(8,128)}, u32[]{:S(2)}) copy-start(f32[8,128]{1,0:T(8,128)} %param.15) | copy-start | bytes 12292
  27.7 27.5 %copy-start.2 = (bf16[32,128,128]{2,1,0:T(8,128)(2,1)S(1)}, bf16[32,128,128]{2,1,0:T(8,128)(2,1)}, u32[]{:S(2)}) copy-start(bf16[32,128,128]{2,1,0:T(8,128)(2,1)} %param.11) | copy-start | bytes 3145732
  55.2 2.5 %copy-start.4 = (s32[16]{0:T(128)S(1)}, s32[16]{0:T(128)}, u32[]{:S(2)}) copy-start(s32[16]{0:T(128)} %param.14) | copy-start | bytes 196
  55.2 4.7 %copy-start.1 = (bf16[32,3,128]{2,0,1:T(8,128)(2,1)S(1)}, bf16[32,3,128]{2,0,1:T(8,128)(2,1)}, u32[]{:S(2)}) copy-start(bf16[32,3,128]{2,0,1:T(8,128)(2,1)} %param.12) | copy-start | bytes 73732
  62.6 15.5 %all-to-all-start = ((bf16[32,3,128]{2,1,0:T(4,128)(2,1)}), bf16[32,3,128]{2,1,0:T(4,128)(2,1)S(1)}, u32[]{:S(2)}, u32[]{:S(2)}) async-start(bf16[32,3,128]{2,1,0:T(4,128)(2,1)} %copy.34), calls=%async_computation | async-start | bytes 65536 | tf_op jit(solution)/shard_map/all_to_all | solution.py:325
  77.0 6.8 %copy-start.3 = (bf16[128,384]{1,0:T(8,128)(2,1)S(1)}, bf16[128,384]{1,0:T(8,128)(2,1)}, u32[]{:S(2)}) copy-start(bf16[128,384]{1,0:T(8,128)(2,1)} %weights_ref.1) | copy-start | bytes 294916
  78.1 28.5 %all-to-all-start.1 = ((bf16[32,128,128]{2,1,0:T(8,128)(2,1)}), bf16[32,128,128]{2,1,0:T(8,128)(2,1)S(1)}, u32[]{:S(2)}, u32[]{:S(2)}) async-start(bf16[32,128,128]{2,1,0:T(8,128)(2,1)} %broadcast_select_fusion), calls=%async_computation.1 | async-start | bytes 2097152 | tf_op jit(solution)/shard_map/all_to_all | solution.py:324
Sparse Core Ops, SparseCore 0:
  57.9 17.1 all-gather.1

commit v2 on v0

--- a/solution.py
+++ b/solution.py
@@ -1,8 +1,12 @@
+import functools
 import math
 
 import jax
 import jax.numpy as jnp
+import numpy as np
 from jax import lax
+from jax.experimental import pallas as pl
+from jax.experimental.pallas import tpu as pltpu
 from jax.sharding import PartitionSpec as P
 
 DIRS = 50
@@ -35,44 +39,291 @@
     return positions_in + amount * marker[:, None]
 
 
-def direction_table(total):
-    dir_order = jnp.arange(total, dtype=jnp.float32)
-    height = 1.0 - (2.0 * dir_order + 1.0) / total
-    radius = jnp.sqrt(1.0 - height * height)
-    turning = dir_order * golden_turn
-    return jnp.stack([radius * jnp.cos(turning), radius * jnp.sin(turning), height], axis=1)
-
-
-def half_frequencies(width):
-    half_width = width // 2
-    return 0.5 * (jnp.arange(half_width, dtype=jnp.float32) + 1.0) / half_width
-
-
-def phases(coords, directions, frequencies):
-    projected = (
-        directions[:, 0:1] * coords[0][None]
-        + directions[:, 1:2] * coords[1][None]
-        + directions[:, 2:3] * coords[2][None]
-    )
-    return projected[:, :, None] * frequencies
-
-
-def rotate_with(values, cosine, sine):
-    half_width = values.shape[-1] // 2
-    first_half = values[None, :, :half_width]
-    second_half = values[None, :, half_width:]
-    turned = jnp.concatenate(
-        [first_half * cosine - second_half * sine, second_half * cosine + first_half * sine],
-        axis=-1,
-    )
-    return turned.astype(jnp.bfloat16)
-
-
-def group_size(count):
-    for candidate in range(1, count + 1):
-        if count % candidate == 0 and count // candidate <= 25:
-            return candidate
-    return count
+def direction_rows(total, shares):
+    order = np.arange(total, dtype=np.float64)
+    height = 1.0 - (2.0 * order + 1.0) / total
+    radius = np.sqrt(1.0 - height * height)
+    turning = order * golden_turn
+    share = total // shares
+    table = np.zeros((shares, -(-share // 8) * 8, 128), np.float32)
+    unit = np.stack([radius * np.cos(turning), radius * np.sin(turning), height], axis=1)
+    table[:, :share, :3] = unit.reshape(shares, share, 3)
+    return table
+
+
+def directions_per_turn(share):
+    return max(g for g in range(1, 6) if share % g == 0)
+
+
+def store_powers(table, coords, half, cosines, sines):
+    base = (
+        table[:, 0:1] * coords[0:1] + table[:, 1:2] * coords[1:2] + table[:, 2:3] * coords[2:3]
+    ) * (0.5 / half)
+    count = table.shape[0]
+    c1, s1 = jnp.cos(base), jnp.sin(base)
+    powers = {1: (c1, s1)}
+    for n in range(2, 9):
+        (ca, sa), (cb, sb) = powers[n // 2], powers[n - n // 2]
+        powers[n] = (ca * cb - sa * sb, sa * cb + ca * sb)
+    for n in range(1, 9):
+        for tile in range(base.shape[1] // 128):
+            lanes = slice(tile * 128, (tile + 1) * 128)
+            cosines[tile, (n - 1) * count : n * count, :] = powers[n][0][:, lanes]
+            sines[tile, (n - 1) * count : n * count, :] = powers[n][1][:, lanes]
+
+
+def rotated(features, direction, count, half, cosines, sines):
+    rows = pl.ds(direction, 8, stride=count)
+    last = pl.ds(7 * count + direction, 1)
+
+    def across(held, at):
+        return jnp.concatenate([held[tile, at, :] for tile in range(held.shape[0])], axis=1)
+
+    cosine, sine = across(cosines, rows), across(sines, rows)
+    step_c = jnp.broadcast_to(across(cosines, last), cosine.shape)
+    step_s = jnp.broadcast_to(across(sines, last), sine.shape)
+    double = 2.0 * step_c
+    older = None
+    low, high = [], []
+    for first in range(0, half, 8):
+        if first == 8:
+            older = (cosine, sine)
+            cosine, sine = cosine * step_c - sine * step_s, sine * step_c + cosine * step_s
+        elif first > 8:
+            held = (cosine, sine)
+            cosine, sine = double * cosine - older[0], double * sine - older[1]
+            older = held
+        a = features[first : first + 8, :]
+        b = features[half + first : half + first + 8, :]
+        low.append(a * cosine - b * sine)
+        high.append(b * cosine + a * sine)
+    return [jnp.concatenate(low + high, axis=0).astype(jnp.bfloat16)]
+
+
+def kv_kernel(chunk, share, live_ref, table_ref, coords_ref, rows_ref, weights_t_ref, weights_ref, states_ref, keys, cosines, sines):
+    width = rows_ref.shape[1]
+    half = width // 2
+    count = table_ref.shape[0]
+    per_turn = directions_per_turn(share)
+    states_ref[...] = jnp.zeros_like(states_ref)
+    live = live_ref[0]
+
+    def advance(turn, carried):
+        at = pl.ds(pl.multiple_of(turn * chunk, chunk), chunk)
+        rows = rows_ref[at, :]
+        keys[...] = lax.dot_general(
+            weights_t_ref[width : 2 * width, :], rows, (((1,), (1,)), ((), ())),
+            preferred_element_type=jnp.float32,
+        )
+        values = jnp.dot(rows, weights_ref[:, 2 * width :], preferred_element_type=jnp.float32)
+        index = turn * chunk + lax.broadcasted_iota(jnp.int32, values.shape, 0)
+        values = jnp.where(index < live, values, 0.0).astype(jnp.bfloat16)
+        store_powers(table_ref[...], coords_ref[:, at], half, cosines, sines)
+
+        def inner(group, held):
+            parts = []
+            for j in range(per_turn):
+                parts += rotated(keys, group * per_turn + j, count, half, cosines, sines)
+            size = per_turn * width
+            out = pl.ds(pl.multiple_of(group * size, size), size)
+            states_ref[out, :] += jnp.dot(
+                jnp.concatenate(parts, axis=0), values, preferred_element_type=jnp.float32
+            )
+            return held
+
+        return lax.fori_loop(0, share // per_turn, inner, carried)
+
+    lax.fori_loop(0, (live + chunk - 1) // chunk, advance, 0)
+
+
+def query_kernel(chunk, share, table_ref, coords_ref, rows_ref, weights_t_ref, states_ref, out_ref, queries, flipped, cosines, sines, total):
+    atoms, width = rows_ref.shape
+    half = width // 2
+    count = table_ref.shape[0]
+    per_turn = directions_per_turn(share)
+    for d in range(share):
+        flipped[:, d * width : (d + 1) * width] = states_ref[d * width : (d + 1) * width, :].T
+
+    def advance(turn, carried):
+        at = pl.ds(pl.multiple_of(turn * chunk, chunk), chunk)
+        queries[...] = lax.dot_general(
+            weights_t_ref[:width, :], rows_ref[at, :], (((1,), (1,)), ((), ())),
+            preferred_element_type=jnp.float32,
+        )
+        store_powers(table_ref[...], coords_ref[:, at], half, cosines, sines)
+        total[...] = jnp.zeros_like(total)
+
+        def inner(group, held):
+            parts = []
+            for j in range(per_turn):
+                parts += rotated(queries, group * per_turn + j, count, half, cosines, sines)
+            size = per_turn * width
+            columns = pl.ds(pl.multiple_of(group * size, size), size)
+            total[...] += jnp.dot(
+                flipped[:, columns], jnp.concatenate(parts, axis=0),
+                preferred_element_type=jnp.float32,
+            )
+            return held
+
+        lax.fori_loop(0, share // per_turn, inner, 0)
+        out_ref[at, :] = total[...].T
+        return carried
+
+    lax.fori_loop(0, atoms // chunk, advance, 0)
+
+
+def vmem(count):
+    return [pl.BlockSpec(memory_space=pltpu.VMEM)] * count
+
+
+def kv_states(live, table, coords, flat, weights_t, weights, share, padded_rows):
+    width = flat.shape[1]
+    chunk = 256
+    count = table.shape[0]
+    atoms = flat.shape[0] // 2
+    return pl.pallas_call(
+        functools.partial(kv_kernel, chunk, share),
+        out_shape=jax.ShapeDtypeStruct((padded_rows, width), jnp.float32),
+        in_specs=[pl.BlockSpec(memory_space=pltpu.SMEM)] + vmem(5),
+        out_specs=pl.BlockSpec(memory_space=pltpu.VMEM),
+        scratch_shapes=[
+            pltpu.VMEM((width, chunk), jnp.float32),
+            pltpu.VMEM((chunk // 128, 8 * count, 128), jnp.float32),
+            pltpu.VMEM((chunk // 128, 8 * count, 128), jnp.float32),
+        ],
+        cost_estimate=pl.CostEstimate(
+            flops=2 * share * atoms * width * width * 8, bytes_accessed=20_000_000, transcendentals=0
+        ),
+        name="kv_states",
+    )(live, table, coords, flat, weights_t, weights)
+
+
+def query_mix(table, coords, flat, weights_t, states, share):
+    atoms, width = flat.shape
+    chunk = 256
+    count = table.shape[0]
+    return pl.pallas_call(
+        functools.partial(query_kernel, chunk, share),
+        out_shape=jax.ShapeDtypeStruct((atoms, width), jnp.float32),
+        in_specs=vmem(5),
+        out_specs=pl.BlockSpec(memory_space=pltpu.VMEM),
+        scratch_shapes=[
+            pltpu.VMEM((width, chunk), jnp.float32),
+            pltpu.VMEM((width, share * width), jnp.bfloat16),
+            pltpu.VMEM((chunk // 128, 8 * count, 128), jnp.float32),
+            pltpu.VMEM((chunk // 128, 8 * count, 128), jnp.float32),
+            pltpu.VMEM((width, chunk), jnp.float32),
+        ],
+        cost_estimate=pl.CostEstimate(
+            flops=2 * share * atoms * width * width * 8, bytes_accessed=20_000_000, transcendentals=0
+        ),
+        name="query_mix",
+    )(table, coords, flat, weights_t, states)
+
+
+def reduce_orders(bits):
+    first = list(range(bits))
+    second = list(first)
+    if bits > 2:
+        second[1], second[2] = second[2], second[1]
+    return [first, second]
+
+
+def reduce_kernel(bits, local_ref, out_ref, total, sent, landed, send_sems, recv_sems, gather_send, gather_recv):
+    me = lax.axis_index("cell")
+
+    def bit_of(b):
+        return lax.rem(me // (1 << b), 2)
+
+    def partner(b):
+        return {"cell": me + (1 - 2 * bit_of(b)) * (1 << b)}
+
+    barrier = pltpu.get_barrier_semaphore()
+    for b in range(bits):
+        pl.semaphore_signal(
+            barrier, inc=1, device_id=partner(b), device_id_type=pl.DeviceIdType.MESH
+        )
+    orders = reduce_orders(bits)
+    piece = local_ref.shape[0] // len(orders)
+    starts = [k * piece for k in range(len(orders))]
+    length = piece
+    offset = 0
+    for step in range(bits):
+        half = length // 2
+        copies = []
+        for k, order in enumerate(orders):
+            b = order[step]
+            away = pl.multiple_of(starts[k] + (1 - bit_of(b)) * half, 16)
+            at = pl.ds(k * piece + offset, half)
+            source = local_ref if step == 0 else total
+            sent[at, :] = source[pl.ds(away, half), :].astype(jnp.bfloat16)
+            if step == 0 and k == 0:
+                pl.semaphore_wait(barrier, bits)
+            copy = pltpu.make_async_remote_copy(
+                src_ref=sent.at[at, :],
+                dst_ref=landed.at[at, :],
+                send_sem=send_sems.at[k, step],
+                recv_sem=recv_sems.at[k, step],
+                device_id=partner(b),
+                device_id_type=pl.DeviceIdType.MESH,
+            )
+            copy.start()
+            copies.append(copy)
+        for k, order in enumerate(orders):
+            b = order[step]
+            keep = pl.multiple_of(starts[k] + bit_of(b) * half, 16)
+            at = pl.ds(k * piece + offset, half)
+            source = local_ref if step == 0 else total
+            copies[k].wait_recv()
+            summed = source[pl.ds(keep, half), :] + landed[at, :].astype(jnp.float32)
+            if step == bits - 1:
+                out_ref[pl.ds(keep, half), :] = summed.astype(jnp.bfloat16)
+            else:
+                total[pl.ds(keep, half), :] = summed
+            starts[k] = keep
+        for copy in copies:
+            copy.wait_send()
+        length = half
+        offset += half
+    for step in reversed(range(bits)):
+        copies = []
+        for k, order in enumerate(orders):
+            b = order[step]
+            at = pl.ds(pl.multiple_of(starts[k], 16), length)
+            copy = pltpu.make_async_remote_copy(
+                src_ref=out_ref.at[at, :],
+                dst_ref=out_ref.at[at, :],
+                send_sem=gather_send.at[k, step],
+                recv_sem=gather_recv.at[k, step],
+                device_id=partner(b),
+                device_id_type=pl.DeviceIdType.MESH,
+            )
+            copy.start()
+            copies.append(copy)
+        for k, order in enumerate(orders):
+            copies[k].wait()
+            starts[k] = starts[k] - bit_of(order[step]) * length
+        length = 2 * length
+
+
+def reduce_states(local, cells):
+    bits = cells.bit_length() - 1
+    rows, width = local.shape
+    pieces = len(reduce_orders(bits))
+    return pl.pallas_call(
+        functools.partial(reduce_kernel, bits),
+        out_shape=jax.ShapeDtypeStruct((rows, width), jnp.bfloat16),
+        in_specs=vmem(1),
+        out_specs=pl.BlockSpec(memory_space=pltpu.VMEM),
+        scratch_shapes=[
+            pltpu.VMEM((rows, width), jnp.float32),
+            pltpu.VMEM((rows, width), jnp.bfloat16),
+            pltpu.VMEM((rows, width), jnp.bfloat16),
+        ]
+        + [pltpu.SemaphoreType.DMA((pieces, bits))] * 4,
+        compiler_params=pltpu.CompilerParams(collective_id=0, has_side_effects=True),
+        name="reduce_states",
+    )(local)
 
 
 def radial_terms(own_positions, near_positions, near_features, filter_gains):
@@ -115,40 +366,6 @@
 
     group_total = (live_count + group_width - 1) // group_width
     return lax.fori_loop(0, group_total, block_advance, initial)
-
-
-def kv_states(keys_rows, values, coords, dir_groups, frequencies):
-
-    def kv_advance(carried, group_dirs):
-        angle = phases(coords, group_dirs, frequencies)
-        cosine = jnp.cos(angle)
-        sine = jnp.sin(angle)
-        key_rot = rotate_with(keys_rows, cosine, sine)
-        state = jnp.einsum("grf,rh->gfh", key_rot, values, preferred_element_type=jnp.float32)
-        return (carried, (state, cosine, sine))
-
-    carried, outputs = lax.scan(kv_advance, jnp.float32(0.0), dir_groups)
-    states, cosines, sines = outputs
-    return (states.reshape(-1, states.shape[-2], states.shape[-1]), cosines, sines)
-
-
-def query_mix(queries, cosines, sines, state_groups):
-
-    def query_advance(running, paired):
-        cosine, sine, group_states = paired
-        query_rot = rotate_with(queries, cosine, sine)
-        return (
-            running
-            + jnp.einsum(
-                "grf,gfh->rh", query_rot, group_states, preferred_element_type=jnp.float32
-            ),
-            None,
-        )
-
-    running, unused = lax.scan(
-        query_advance, jnp.zeros(queries.shape, jnp.float32), (cosines, sines, state_groups)
-    )
-    return running
 
 
 def per_device(
@@ -229,31 +446,36 @@
         received_positions[pick_rows].astype(jnp.float32),
         slab_width * source.astype(jnp.float32)[:, None, None],
     )
-    dir_table = direction_table(DIRS)
-    frequencies = half_frequencies(width)
+    share = DIRS // dirs_count
+    unit_rows = 32 * cells
+    padded_rows = -(-share * width // unit_rows) * unit_rows
+    table = lax.dynamic_index_in_dim(
+        jnp.asarray(direction_rows(DIRS, dirs_count)), dir_index, 0, keepdims=False
+    )
+    weights_t = projections.T
+    own_global = shift_component(float_positions, slab_width * cell_index.astype(jnp.float32))
+    own_coords = jnp.transpose(own_global, (1, 0, 2)).reshape(3, -1)
+    live_atoms = (own_count * block_atoms).astype(jnp.int32).reshape(1)
+    local_states = kv_states(
+        live_atoms, table, own_coords, updated.reshape(-1, width), weights_t, projections, share, padded_rows
+    )
+    states = reduce_states(local_states, cells)
     share_blocks = balanced_blocks // dirs_count
-    rows_features = lax.dynamic_slice_in_dim(
-        balanced_features, dir_index * share_blocks, share_blocks, 0
-    )
-    rows_positions = lax.dynamic_slice_in_dim(
-        balanced_positions, dir_index * share_blocks, share_blocks, 0
-    )
-    flat = rows_features.reshape(-1, width)
-    qkv = jnp.dot(flat, projections, preferred_element_type=jnp.float32)
-    coords = jnp.transpose(rows_positions, (1, 0, 2)).reshape(3, -1)
-    queries, keys_rows, values, coords = (
-        qkv[:, :width],
-        qkv[:, width : 2 * width],
-        qkv[:, 2 * width :].astype(jnp.bfloat16),
-        coords,
-    )
-    group_width = group_size(DIRS)
-    dir_groups = dir_table.reshape(-1, group_width, 3)
-    local_states, cosines, sines = kv_states(keys_rows, values, coords, dir_groups, frequencies)
-    states = lax.psum(local_states, ("cell", "dir")).astype(jnp.bfloat16)
-    mixed_rows = query_mix(
-        queries, cosines, sines, states.reshape(dir_groups.shape[0], group_width, width, width)
-    )
+
+    def partial_mix(owner):
+        features = lax.dynamic_slice_in_dim(balanced_features, owner * share_blocks, share_blocks, 0)
+        places = lax.dynamic_slice_in_dim(balanced_positions, owner * share_blocks, share_blocks, 0)
+        coords = jnp.transpose(places, (1, 0, 2)).reshape(3, -1)
+        return query_mix(table, coords, features.reshape(-1, width), weights_t, states, share)
+
+    mixed_rows = None
+    for hop in range(1, dirs_count):
+        away = partial_mix((dir_index + hop) % dirs_count).astype(jnp.bfloat16)
+        came = lax.ppermute(away, "dir", [(i, (i + hop) % dirs_count) for i in range(dirs_count)])
+        came = came.astype(jnp.float32)
+        mixed_rows = came if mixed_rows is None else mixed_rows + came
+    kept = partial_mix(dir_index)
+    mixed_rows = kept if mixed_rows is None else kept + mixed_rows
     mix_scale = 1.0 / math.sqrt(DIRS * cells * balanced_blocks * block_atoms * width)
     mixed = (mixed_rows * mix_scale).astype(jnp.bfloat16)
     attended = jnp.dot(mixed, w_output, preferred_element_type=jnp.float32).astype(jnp.bfloat16)

time: 514 us -> 192 us (0.37)
  other arithmetic: 253 us -> 9.43 us
  blocking collectives: 83.7 us -> 0 us
  Pallas kernels: 0 us -> 81.7 us
  matrix products: 68.5 us -> 12.2 us
  local copies, waits for them, and re-layouts: 37.8 us -> 28.5 us
  waiting for transfers between devices: 31.3 us -> 24.3 us
    dynamic_update_slice x25 -> x0, other arithmetic: 140 us -> none  [kv_states(): carried, outputs = lax.scan(kv_advance, jnp.float32(0.0), dir_groups)]
    another operation x55 -> x2, other arithmetic: 103 us -> 0.15 us
    psum x1 -> x0, blocking collectives: 83.7 us -> none  [per_device(): states = lax.psum(local_states, ('cell', 'dir')).astype(jnp.bfloat16)]
    pallas_call x0 -> x4, Pallas kernels: none -> 81.7 us  [the longest x1 43.7 us: reduce_states(): pl.pallas_call(functools.partial(reduce_kernel, bits), out_shape=jax.Shap...]
    dot_general x51 -> x0, matrix products: 56.2 us -> none  [the longest x25 32.1 us: query_advance(): jnp.einsum('grf,gfh->rh', query_rot, group_states, preferred_element_type...]
    all_to_all x1, waiting for transfers between devices: 21.7 us -> 0.01 us  [per_device(): lax.all_to_all(send_features, 'cell', split_axis=0, concat_axis=0, tiled=...]
    all_gather x1, waiting for transfers between devices: 9.58 us -> 24.3 us  [per_device(): updated = lax.all_gather(updated_share, 'dir', axis=0, tiled=True)]
    slice x102 -> x0, local copies, waits for them, and re-layouts: 11 us -> none  [the longest x50 6.02 us: rotate_with(): first_half = values[None, :, :half_width]]
  transfers between devices with their start and end apart: 7 -> 8, of which waited for: 2 -> 1; matrix products, arithmetic and copies ran while one was open for 3% -> 23% of each run, Pallas kernels for 0% -> 37%
where the time goes in v2:
time: 192 us; the launch traced here: 191 us
  Pallas kernels  81.7 us (43%)
  local copies, waits for them, and re-layouts  28.5 us (15%)
  waiting for transfers between devices  24.3 us (13%)
  starting transfers between devices  19.8 us (10%)
  between operations  14.9 us (8%)
  matrix products  12.2 us (6%)
  other arithmetic  9.43 us (5%)
    pallas_call x1, Pallas kernels, reduce_states(): pl.pallas_call(functools.partial(reduce_kernel, bits), out_shape=jax.Shap...  43.7 us
    all_gather x1, waiting for transfers between devices, per_device(): updated = lax.all_gather(updated_share, 'dir', axis=0, tiled=True)  24.3 us
    pallas_call x2, Pallas kernels, query_mix(): pl.pallas_call(functools.partial(query_kernel, chunk, share), out_shape=j...  21.8 us
    pallas_call x1, Pallas kernels, kv_states(): pl.pallas_call(functools.partial(kv_kernel, chunk, share), out_shape=jax....  16.2 us
    ppermute x2, starting transfers between devices, extended(): lax.ppermute(head, axis, [((i + 1) % count, i) for i in range(count)])  9.46 us
    dot_general x7, matrix products, radial_terms(): jnp.einsum('gnkab,gnbf->gkaf', radial, near_features, preferred_element_t...  7.79 us
    all_to_all x1, starting transfers between devices, per_device(): lax.all_to_all(send_features, 'cell', split_axis=0, concat_axis=0, tiled=...  5.62 us
    dynamic_update_slice x7, local copies, waits for them, and re-layouts, block_advance(): lax.dynamic_update_slice_in_dim(running, result, turn_index * group_width...  4.62 us
  transfers between devices with their start and end apart: 8, of which 1 were waited for; matrix products, arithmetic and copies ran while one was open for 23% of the time, Pallas kernels for 37%

profile of v2, /device:TPU:0, one launch (start us, length us, event | category | flops | bytes accessed | tf_op | source)
XLA Modules:
  0.0 191.3 jit_solution(15989106317801929290)
XLA Ops:
  6.5 0.8 slice.28
  7.8 5.0 %collective-permute-start.1 = (bf16[4,3,128]{2,1,0:T(4,128)(2,1)S(1)}, bf16[4,3,128]{2,1,0:T(4,128)(2,1)S(1)}, u32[]{:S(2)}, u32[]{:S(2)}) collective-permute-start(bf16[4,3,128]{2,1,0:T(4,128)(2,1)S(1)} %copy.37), channel_id=1, source_target_pairs={{2,0},{4,2},{6,4},{8,6},{10,8},{12,10},{14,12},{16,14},{18,16},{20... | collective-permute-start | bytes 9224 | tf_op jit(solution)/shard_map/ppermute | solution.py:30
  12.9 0.9 slice.15
  13.8 4.4 %collective-permute-start.3 = (bf16[4,128,128]{2,1,0:T(8,128)(2,1)S(1)}, bf16[4,128,128]{2,1,0:T(8,128)(2,1)S(1)}, u32[]{:S(2)}, u32[]{:S(2)}) collective-permute-start(bf16[4,128,128]{2,1,0:T(8,128)(2,1)S(1)} %slice.15), channel_id=1, source_target_pairs={{2,0},{4,2},{6,4},{8,6},{10,8},{12,10},{14,12},{16,14},{18,16},{20... | collective-permute-start | bytes 393224 | tf_op jit(solution)/shard_map/ppermute | solution.py:30
  18.3 1.3 dynamic_slice.39
  21.7 1.3 fusion.26
  23.0 1.3 fusion.23
  24.3 1.4 gather_fusion.2
  26.4 3.5 %all-to-all-start = ((bf16[32,3,128]{2,1,0:T(4,128)(2,1)}), bf16[32,3,128]{2,1,0:T(4,128)(2,1)S(1)}, u32[]{:S(2)}, u32[]{:S(2)}) async-start(bf16[32,3,128]{2,1,0:T(4,128)(2,1)} %copy.28), calls=%async_computation | async-start | bytes 65536 | tf_op jit(solution)/shard_map/all_to_all | solution.py:437
  29.9 0.8 copy_convert_fusion
  31.6 0.8 copy.31
  32.7 1.1 broadcast_in_dim.43
  33.7 24.2 %while.12 = (s32[]{:T(128)}, f32[16,128,128]{2,1,0:T(8,128)}, s32[]{:T(128)}, s32[]{:T(128)}, f32[40,3,128]{2,1,0:T(4,128)S(1)}, /*index=5*/s32[32,4]{1,0:T(8,12...) while((s32[]{:T(128)}, f32[16,128,128]{2,1,0:T(8,128)}, ...), condition=%wide.region_5.6_spmd, body=%wide.region_2.0_spmd.sunk | while | flops 275219520 | bytes 3331651 | solution.py:368
  35.4 1.1 fusion.41
  38.9 1.1 fusion.41
  42.3 1.1 fusion.41
  45.8 1.1 fusion.41
  49.2 1.1 fusion.41
  52.7 1.1 fusion.41
  56.1 1.1 fusion.41
  57.9 2.5 %fusion.14 = bf16[16,128,128]{2,1,0:T(8,128)(2,1)} fusion(f32[16,128,128]{2,1,0:T(8,128)} %get-tuple-element.109, bf16[32,128,128]{2,1,0:T(8,128)(2,1)S(1)} %copy-done.2, s32[]{:T(128)S(6)} %select_n.154, bf16[128,128]{1,0:T(8,128)(2,1)S(1)} %copy-done), kind=kOutput, calls=%fused_computation.22 | convolution fusion | flops 69206016 | bytes 2129924 | tf_op jit(solution)/shard_map/dot_general | solution.py:417
  61.2 24.3 %all-gather.2.cloned.1.call-done = bf16[32,128,128]{2,1,0:T(8,128)(2,1)} async-done(((bf16[16,128,128]{2,1,0:T(8,128)(2,1)}), bf16[32,128,128]{2,1,0:T(8,128)(2,1)}) %all-gather.2.cloned.1.call-update) | async-done | bytes 1048592 | tf_op jit(solution)/shard_map/all_gather | solution.py:419
  85.4 2.0 %gather_fusion.4 = bf16[32,128,128]{2,1,0:T(8,128)(2,1)S(1)} fusion(bf16[32,128,128]{2,1,0:T(8,128)(2,1)} %all-gather.2.cloned.1.call-done, s32[1024]{0:T(1024)S(1)} %pad_clamp_fusion.2), kind=kCustom, calls=%fused_computation.4 | custom fusion | bytes 2097280 | tf_op jit(solution)/shard_map/gather | solution.py:430
  87.4 1.1 broadcast_select_fusion
  88.6 5.6 %all-to-all-start.1 = ((bf16[32,128,128]{2,1,0:T(8,128)(2,1)}), bf16[32,128,128]{2,1,0:T(8,128)(2,1)S(1)}, u32[]{:S(2)}, u32[]{:S(2)}) async-start(bf16[32,128,128]{2,1,0:T(8,128)(2,1)} %broadcast_select_fusion), calls=%async_computation.1 | async-start | bytes 2097152 | tf_op jit(solution)/shard_map/all_to_all | solution.py:436
  97.6 16.2 %kv_states.1.local_ref = f32[3584,128]{1,0:T(8,128)} custom-call(s32[1]{0:T(128)} %bitcast.18.live_ref, f32[32,128]{1,0:T(8,128)} %dynamic-slice_bitcast_fusion.2.table_ref, f32[3,4096]{1,0:T(4,128)} %add_bitcast_fusion.coords_ref, bf16[4096,128]{1,0:T(8,128)(2,1)} %bitcast.59, bf16[384,128]{1,0:T(8,128)(2,1)} %bitcast.62, bf16[128,384]{1,0:T(8,128)(2,1)} %weights_ref.1), custom_call_target="tpu_custom_call" | custom-call | flops 13421772800 | bytes 20000000 | tf_op jit(solution)/shard_map/kv_states/pallas_call | solution.py:184
  113.8 43.7 %reduce_states.1.states_ref = bf16[3584,128]{1,0:T(8,128)(2,1)} custom-call(f32[3584,128]{1,0:T(8,128)} %kv_states.1.local_ref), custom_call_target="tpu_custom_call" | custom-call | tf_op jit(solution)/shard_map/reduce_states/pallas_call | solution.py:313
  158.1 0.8 constant_dynamic-slice_fusion.1
  159.0 10.9 %query_mix.3 = f32[1024,128]{1,0:T(8,128)} custom-call(f32[32,128]{1,0:T(8,128)} %dynamic-slice_bitcast_fusion.2.table_ref, f32[3,1024]{1,0:T(4,128)} %get-tuple-element.160.coords_ref, bf16[1024,128]{1,0:T(8,128)(2,1)} %bitcast.61, bf16[384,128]{1,0:T(8,128)(2,1)} %bitcast.63, bf16[3584,128]{1,0:T(8,128)(2,1)} %reduce_states.1.states_ref), custom_call_target="tpu_custom_call" | custom-call | flops 6710886400 | bytes 20000000 | tf_op jit(solution)/shard_map/query_mix/pallas_call | solution.py:205
  169.9 1.1 convert_element_type.75
  171.6 10.9 %query_mix.2 = f32[1024,128]{1,0:T(8,128)} custom-call(f32[32,128]{1,0:T(8,128)} %dynamic-slice_bitcast_fusion.2.table_ref, f32[3,1024]{1,0:T(4,128)} %get-tuple-element.161.coords_ref, bf16[1024,128]{1,0:T(8,128)(2,1)} %bitcast.60, bf16[384,128]{1,0:T(8,128)(2,1)} %bitcast.64, bf16[3584,128]{1,0:T(8,128)(2,1)} %reduce_states.1.states_ref), custom_call_target="tpu_custom_call" | custom-call | flops 6710886400 | bytes 20000000 | tf_op jit(solution)/shard_map/query_mix/pallas_call | solution.py:205
  182.5 2.0 %convolution_convert_fusion = bf16[1024,128]{1,0:T(8,128)(2,1)} fusion(bf16[128,128]{1,0:T(8,128)(2,1)S(1)} %copy-done.4, f32[1024,128]{1,0:T(8,128)} %query_mix.2, bf16[1024,128]{1,0:T(8,128)(2,1)S(1)} %collective-permute-done.4), kind=kOutput, calls=%fused_computation.23 | convolution fusion | flops 34209792 | bytes 1081344 | tf_op jit(solution)/shard_map/dot_general | solution.py:481
  (124 shorter events, 24.7 us)
Async XLA Ops:
  6.5 51.4 %copy-start = (bf16[128,128]{1,0:T(8,128)(2,1)S(1)}, bf16[128,128]{1,0:T(8,128)(2,1)}, u32[]{:S(2)}) copy-start(bf16[128,128]{1,0:T(8,128)(2,1)} %param.16) | copy-start | bytes 98308
  6.5 25.9 %copy-start.2 = (bf16[32,128,128]{2,1,0:T(8,128)(2,1)S(1)}, bf16[32,128,128]{2,1,0:T(8,128)(2,1)}, u32[]{:S(2)}) copy-start(bf16[32,128,128]{2,1,0:T(8,128)(2,1)} %param.11) | copy-start | bytes 3145732
  7.3 25.0 %collective-permute-start = (bf16[4,3,128]{2,1,0:T(4,128)(2,1)S(1)}, bf16[4,3,128]{2,1,0:T(4,128)(2,1)S(1)}, u32[]{:S(2)}, u32[]{:S(2)}) collective-permute-start(bf16[4,3,128]{2,1,0:T(4,128)(2,1)S(1)} %copy.37), channel_id=1, source_target_pairs={{0,2},{2,4},{4,6},{6,8},{8,10},{10,12},{12,14},{14,16},{16,18},{18... | collective-permute-start | bytes 9224 | tf_op jit(solution)/shard_map/ppermute | solution.py:28
  7.8 24.5 %collective-permute-start.1 = (bf16[4,3,128]{2,1,0:T(4,128)(2,1)S(1)}, bf16[4,3,128]{2,1,0:T(4,128)(2,1)S(1)}, u32[]{:S(2)}, u32[]{:S(2)}) collective-permute-start(bf16[4,3,128]{2,1,0:T(4,128)(2,1)S(1)} %copy.37), channel_id=1, source_target_pairs={{2,0},{4,2},{6,4},{8,6},{10,8},{12,10},{14,12},{16,14},{18,16},{20... | collective-permute-start | bytes 9224 | tf_op jit(solution)/shard_map/ppermute | solution.py:30
  13.8 18.7 %collective-permute-start.2 = (bf16[4,128,128]{2,1,0:T(8,128)(2,1)S(1)}, bf16[4,128,128]{2,1,0:T(8,128)(2,1)S(1)}, u32[]{:S(2)}, u32[]{:S(2)}) collective-permute-start(bf16[4,128,128]{2,1,0:T(8,128)(2,1)S(1)} %slice.15), channel_id=1, source_target_pairs={{0,2},{2,4},{4,6},{6,8},{8,10},{10,12},{12,14},{14,16},{16,18},{18... | collective-permute-start | bytes 393224 | tf_op jit(solution)/shard_map/ppermute | solution.py:28
  13.8 18.6 %collective-permute-start.3 = (bf16[4,128,128]{2,1,0:T(8,128)(2,1)S(1)}, bf16[4,128,128]{2,1,0:T(8,128)(2,1)S(1)}, u32[]{:S(2)}, u32[]{:S(2)}) collective-permute-start(bf16[4,128,128]{2,1,0:T(8,128)(2,1)S(1)} %slice.15), channel_id=1, source_target_pairs={{2,0},{4,2},{6,4},{8,6},{10,8},{12,10},{14,12},{16,14},{18,16},{20... | collective-permute-start | bytes 393224 | tf_op jit(solution)/shard_map/ppermute | solution.py:30
  26.4 62.2 %all-to-all-start = ((bf16[32,3,128]{2,1,0:T(4,128)(2,1)}), bf16[32,3,128]{2,1,0:T(4,128)(2,1)S(1)}, u32[]{:S(2)}, u32[]{:S(2)}) async-start(bf16[32,3,128]{2,1,0:T(4,128)(2,1)} %copy.28), calls=%async_computation | async-start | bytes 65536 | tf_op jit(solution)/shard_map/all_to_all | solution.py:437
  29.9 55.6 %all-gather.2.cloned.1.call-start = ((), (), s32[]{:S(2)}) async-start(), calls=%async_computation.2 | async-start | bytes 1572864 | tf_op jit(solution)/shard_map/all_gather | solution.py:419
  32.4 1.3 copy-start.6
  57.9 2.5 %copy-start.1 = (bf16[32,3,128]{2,0,1:T(8,128)(2,1)S(1)}, bf16[32,3,128]{2,0,1:T(8,128)(2,1)}, u32[]{:S(2)}) copy-start(bf16[32,3,128]{2,0,1:T(8,128)(2,1)} %param.12) | copy-start | bytes 73732
  87.4 7.4 %copy-start.3 = (bf16[128,384]{1,0:T(8,128)(2,1)S(1)}, bf16[128,384]{1,0:T(8,128)(2,1)}, u32[]{:S(2)}) copy-start(bf16[128,384]{1,0:T(8,128)(2,1)} %weights_ref.1) | copy-start | bytes 294916
  87.4 8.2 %copy-start.5 = (f32[2,32,128]{2,1,0:T(8,128)S(1)}, f32[2,32,128]{2,1,0:T(8,128)}, u32[]{:S(2)}) copy-start(f32[2,32,128]{2,1,0:T(8,128)} %constant.170.clone) | copy-start | bytes 98308
  88.6 68.9 %all-to-all-start.1 = ((bf16[32,128,128]{2,1,0:T(8,128)(2,1)}), bf16[32,128,128]{2,1,0:T(8,128)(2,1)S(1)}, u32[]{:S(2)}, u32[]{:S(2)}) async-start(bf16[32,128,128]{2,1,0:T(8,128)(2,1)} %broadcast_select_fusion), calls=%async_computation.1 | async-start | bytes 2097152 | tf_op jit(solution)/shard_map/all_to_all | solution.py:436
  171.0 11.5 %collective-permute-start.4 = (bf16[1024,128]{1,0:T(8,128)(2,1)S(1)}, bf16[1024,128]{1,0:T(8,128)(2,1)S(1)}, u32[]{:S(2)}, u32[]{:S(2)}) collective-permute-start(bf16[1024,128]{1,0:T(8,128)(2,1)S(1)} %convert_element_type.75), channel_id=1, source_target_pairs={{0,1},{1,0},{2,3},{3,2},{4,5},{5,4},{6,7},{7,6},{8,9},{9,8},{10,11... | collective-permute-start | bytes 786440 | tf_op jit(solution)/shard_map/ppermute | solution.py:474
  171.6 10.9 %copy-start.4 = (bf16[128,128]{1,0:T(8,128)(2,1)S(1)}, bf16[128,128]{1,0:T(8,128)(2,1)}, u32[]{:S(2)}) copy-start(bf16[128,128]{1,0:T(8,128)(2,1)} %param.18) | copy-start | bytes 98308
Sparse Core Ops, SparseCore 0:
  60.5 24.8 all-gather.1

commit v3 on v2

--- a/solution.py
+++ b/solution.py
@@ -16,22 +16,6 @@
 slab_width = 12.0
 radial_width = 0.6
 golden_turn = math.pi * (3.0 - math.sqrt(5.0))
-
-
-def extended(cells, sides, width):
-    for axis, dim in sides:
-        count = lax.axis_size(axis)
-        head = lax.slice_in_dim(cells, 0, width, axis=dim)
-        tail = lax.slice_in_dim(cells, cells.shape[dim] - width, cells.shape[dim], axis=dim)
-        cells = jnp.concatenate(
-            [
-                lax.ppermute(tail, axis, [(i, (i + 1) % count) for i in range(count)]),
-                cells,
-                lax.ppermute(head, axis, [((i + 1) % count, i) for i in range(count)]),
-            ],
-            axis=dim,
-        )
-    return cells
 
 
 def shift_component(positions_in, amount):
@@ -100,7 +84,7 @@
     return [jnp.concatenate(low + high, axis=0).astype(jnp.bfloat16)]
 
 
-def kv_kernel(chunk, share, live_ref, table_ref, coords_ref, rows_ref, weights_t_ref, weights_ref, states_ref, keys, cosines, sines):
+def kv_kernel(chunk, share, live_ref, table_ref, coords_ref, rows_ref, weights_t_ref, weights_ref, out_ref, states_ref, keys, cosines, sines):
     width = rows_ref.shape[1]
     half = width // 2
     count = table_ref.shape[0]
@@ -134,6 +118,7 @@
         return lax.fori_loop(0, share // per_turn, inner, carried)
 
     lax.fori_loop(0, (live + chunk - 1) // chunk, advance, 0)
+    out_ref[...] = states_ref[...].astype(out_ref.dtype)
 
 
 def query_kernel(chunk, share, table_ref, coords_ref, rows_ref, weights_t_ref, states_ref, out_ref, queries, flipped, cosines, sines, total):
@@ -176,17 +161,18 @@
     return [pl.BlockSpec(memory_space=pltpu.VMEM)] * count
 
 
-def kv_states(live, table, coords, flat, weights_t, weights, share, padded_rows):
+def kv_states(live, table, coords, flat, weights_t, weights, share, padded_rows, dtype):
     width = flat.shape[1]
     chunk = 256
     count = table.shape[0]
     atoms = flat.shape[0] // 2
     return pl.pallas_call(
         functools.partial(kv_kernel, chunk, share),
-        out_shape=jax.ShapeDtypeStruct((padded_rows, width), jnp.float32),
+        out_shape=jax.ShapeDtypeStruct((padded_rows, width), dtype),
         in_specs=[pl.BlockSpec(memory_space=pltpu.SMEM)] + vmem(5),
         out_specs=pl.BlockSpec(memory_space=pltpu.VMEM),
         scratch_shapes=[
+            pltpu.VMEM((padded_rows, width), jnp.float32),
             pltpu.VMEM((width, chunk), jnp.float32),
             pltpu.VMEM((chunk // 128, 8 * count, 128), jnp.float32),
             pltpu.VMEM((chunk // 128, 8 * count, 128), jnp.float32),
@@ -229,7 +215,12 @@
     return [first, second]
 
 
-def reduce_kernel(bits, local_ref, out_ref, total, sent, landed, send_sems, recv_sems, gather_send, gather_recv):
+def piece_rows(rows, unit, pieces):
+    units = rows // unit
+    return [(units // pieces + (k < units % pieces)) * unit for k in range(pieces)]
+
+
+def reduce_kernel(bits, local_ref, came_ref, out_ref, total, sent, landed, send_sems, recv_sems, gather_send, gather_recv):
     me = lax.axis_index("cell")
 
     def bit_of(b):
@@ -244,19 +235,22 @@
             barrier, inc=1, device_id=partner(b), device_id_type=pl.DeviceIdType.MESH
         )
     orders = reduce_orders(bits)
-    piece = local_ref.shape[0] // len(orders)
-    starts = [k * piece for k in range(len(orders))]
-    length = piece
-    offset = 0
+    lengths = piece_rows(local_ref.shape[0], 16 * (1 << bits), len(orders))
+    starts = [sum(lengths[:k]) for k in range(len(orders))]
+    offsets = list(starts)
+
+    def own(step, at):
+        if step == 0:
+            return local_ref[at, :] + came_ref[at, :].astype(jnp.float32)
+        return total[at, :]
+
     for step in range(bits):
-        half = length // 2
         copies = []
         for k, order in enumerate(orders):
-            b = order[step]
+            b, half = order[step], lengths[k] // 2
             away = pl.multiple_of(starts[k] + (1 - bit_of(b)) * half, 16)
-            at = pl.ds(k * piece + offset, half)
-            source = local_ref if step == 0 else total
-            sent[at, :] = source[pl.ds(away, half), :].astype(jnp.bfloat16)
+            at = pl.ds(offsets[k], half)
+            sent[at, :] = own(step, pl.ds(away, half)).astype(jnp.bfloat16)
             if step == 0 and k == 0:
                 pl.semaphore_wait(barrier, bits)
             copy = pltpu.make_async_remote_copy(
@@ -270,50 +264,48 @@
             copy.start()
             copies.append(copy)
         for k, order in enumerate(orders):
-            b = order[step]
+            b, half = order[step], lengths[k] // 2
             keep = pl.multiple_of(starts[k] + bit_of(b) * half, 16)
-            at = pl.ds(k * piece + offset, half)
-            source = local_ref if step == 0 else total
+            at = pl.ds(offsets[k], half)
             copies[k].wait_recv()
-            summed = source[pl.ds(keep, half), :] + landed[at, :].astype(jnp.float32)
+            summed = own(step, pl.ds(keep, half)) + landed[at, :].astype(jnp.float32)
             if step == bits - 1:
                 out_ref[pl.ds(keep, half), :] = summed.astype(jnp.bfloat16)
             else:
                 total[pl.ds(keep, half), :] = summed
             starts[k] = keep
+            lengths[k] = half
+            offsets[k] += half
         for copy in copies:
             copy.wait_send()
-        length = half
-        offset += half
     for step in reversed(range(bits)):
         copies = []
         for k, order in enumerate(orders):
-            b = order[step]
-            at = pl.ds(pl.multiple_of(starts[k], 16), length)
+            at = pl.ds(pl.multiple_of(starts[k], 16), lengths[k])
             copy = pltpu.make_async_remote_copy(
                 src_ref=out_ref.at[at, :],
                 dst_ref=out_ref.at[at, :],
                 send_sem=gather_send.at[k, step],
                 recv_sem=gather_recv.at[k, step],
-                device_id=partner(b),
+                device_id=partner(order[step]),
                 device_id_type=pl.DeviceIdType.MESH,
             )
             copy.start()
             copies.append(copy)
         for k, order in enumerate(orders):
             copies[k].wait()
-            starts[k] = starts[k] - bit_of(order[step]) * length
-        length = 2 * length
-
-
-def reduce_states(local, cells):
+            starts[k] = starts[k] - bit_of(order[step]) * lengths[k]
+            lengths[k] = 2 * lengths[k]
+
+
+def reduce_states(local, came, cells):
     bits = cells.bit_length() - 1
     rows, width = local.shape
     pieces = len(reduce_orders(bits))
     return pl.pallas_call(
         functools.partial(reduce_kernel, bits),
         out_shape=jax.ShapeDtypeStruct((rows, width), jnp.bfloat16),
-        in_specs=vmem(1),
+        in_specs=vmem(2),
         out_specs=pl.BlockSpec(memory_space=pltpu.VMEM),
         scratch_shapes=[
             pltpu.VMEM((rows, width), jnp.float32),
@@ -322,8 +314,9 @@
         ]
         + [pltpu.SemaphoreType.DMA((pieces, bits))] * 4,
         compiler_params=pltpu.CompilerParams(collective_id=0, has_side_effects=True),
+        cost_estimate=pl.CostEstimate(flops=20_000_000_000, bytes_accessed=60_000_000, transcendentals=0),
         name="reduce_states",
-    )(local)
+    )(local, came)
 
 
 def radial_terms(own_positions, near_positions, near_features, filter_gains):
@@ -338,34 +331,28 @@
     return jnp.sum(summed * filter_gains[None, :, None, :], axis=1)
 
 
-def block_messages(
-    first_slot,
-    live_count,
-    slot_count,
-    group_width,
-    neighbours,
-    extended_features,
-    extended_positions,
-    filter_gains,
-    face_blocks,
-):
+def block_messages(live_count, group_width, picks, own_positions, extended_features, extended_positions, filter_gains):
+    slot_count = picks.shape[0]
     initial = jnp.zeros(
         (slot_count, extended_features.shape[1], extended_features.shape[2]), jnp.float32
     )
 
     def block_advance(turn_index, running):
-        start_slot = first_slot + turn_index * group_width
-        picked = lax.dynamic_slice_in_dim(neighbours, start_slot, group_width, 0)
+        at = turn_index * group_width
+        picked = lax.dynamic_slice_in_dim(picks, at, group_width, 0)
         near_features = extended_features[picked]
         near_positions = extended_positions[picked]
-        own_positions = lax.dynamic_slice_in_dim(
-            extended_positions, start_slot + face_blocks, group_width, 0
-        )
-        result = radial_terms(own_positions, near_positions, near_features, filter_gains)
-        return lax.dynamic_update_slice_in_dim(running, result, turn_index * group_width, 0)
+        own = lax.dynamic_slice_in_dim(own_positions, at, group_width, 0)
+        result = radial_terms(own, near_positions, near_features, filter_gains)
+        return lax.dynamic_update_slice_in_dim(running, result, at, 0)
 
     group_total = (live_count + group_width - 1) // group_width
     return lax.fori_loop(0, group_total, block_advance, initial)
+
+
+def join(features, places):
+    padded = jnp.pad(places, ((0, 0), (0, 16 - places.shape[1]), (0, 0)))
+    return jnp.concatenate([features, padded], axis=1)
 
 
 def per_device(
@@ -378,102 +365,133 @@
     capacity, block_atoms, width = atom_features.shape
     balanced_blocks = capacity // 2
     face_blocks = H
-    faces_features, faces_positions = (
-        extended(atom_features[:face_blocks], (("cell", 0),), face_blocks),
-        extended(positions[:face_blocks], (("cell", 0),), face_blocks),
-    )
+    faces = join(atom_features[:face_blocks], positions[:face_blocks])
+    before = lax.ppermute(faces, "cell", [(i, (i + 1) % cells) for i in range(cells)])
+    after = lax.ppermute(faces, "cell", [((i + 1) % cells, i) for i in range(cells)])
     float_positions = positions.astype(jnp.float32)
-    faces_float = faces_positions.astype(jnp.float32)
     extended_features = jnp.concatenate(
-        [faces_features[:face_blocks], atom_features, faces_features[2 * face_blocks :]], axis=0
-    )
+        [before[:, :block_atoms], atom_features, after[:, :block_atoms]], axis=0
+    )
+    axes = positions.shape[1]
+    places_of = slice(block_atoms, block_atoms + axes)
     extended_positions = jnp.concatenate(
         [
-            shift_component(faces_float[:face_blocks], -slab_width),
+            shift_component(before[:, places_of].astype(jnp.float32), -slab_width),
             float_positions,
-            shift_component(faces_float[2 * face_blocks :], slab_width),
+            shift_component(after[:, places_of].astype(jnp.float32), slab_width),
         ],
         axis=0,
     )
     own_count = counts[cell_index]
+    count_ends = jnp.cumsum(counts)
+    first_live = (count_ends - counts)[cell_index]
     share_slots = capacity // dirs_count
-    first_slot = dir_index * share_slots
-    live_count = jnp.clip(own_count - first_slot, 0, share_slots)
+    first_slot = (dir_index - first_live) % dirs_count
+
+    def mine(array):
+        dealt = array.reshape((share_slots, dirs_count) + array.shape[1:])
+        return lax.dynamic_index_in_dim(dealt, first_slot, 1, keepdims=False)
+
+    live_count = (own_count - first_slot + dirs_count - 1) // dirs_count
+    own_features = mine(atom_features)
+    own_places = mine(positions)
+    own_float = own_places.astype(jnp.float32)
     message = block_messages(
-        first_slot,
-        live_count,
-        share_slots,
-        2,
-        neighbours,
-        extended_features,
-        extended_positions,
-        filter_gains,
-        face_blocks,
-    )
-    own_features = lax.dynamic_slice_in_dim(atom_features, first_slot, share_slots, 0)
+        live_count, 2, mine(neighbours), own_float, extended_features, extended_positions, filter_gains
+    )
     activated = jax.nn.silu(message).astype(jnp.bfloat16)
-    updated_share = (
+    updated = (
         own_features.astype(jnp.float32)
         + jnp.dot(activated, w_update, preferred_element_type=jnp.float32)
     ).astype(jnp.bfloat16)
-    updated = lax.all_gather(updated_share, "dir", axis=0, tiled=True)
-    count_ends = jnp.cumsum(counts)
-    starts = count_ends - counts
-    first_live = starts[cell_index]
+
+    share = DIRS // dirs_count
+    unit_rows = 16 * cells
+    padded_rows = -(-share * width // unit_rows) * unit_rows
+    tables = jnp.asarray(direction_rows(DIRS, dirs_count))
+    weights_t = projections.T
+    own_global = shift_component(own_float, slab_width * cell_index.astype(jnp.float32))
+    own_coords = jnp.transpose(own_global, (1, 0, 2)).reshape(axes, -1)
+    live_atoms = (live_count * block_atoms).astype(jnp.int32).reshape(1)
+
+    def states_of(owner, dtype):
+        part = lax.dynamic_index_in_dim(tables, owner, 0, keepdims=False)
+        return kv_states(
+            live_atoms, part, own_coords, updated.reshape(-1, width), weights_t, projections, share,
+            padded_rows, dtype,
+        )
+
+    came = jnp.zeros((padded_rows, width), jnp.bfloat16)
+    for hop in range(1, dirs_count):
+        away = states_of((dir_index + hop) % dirs_count, jnp.bfloat16)
+        arrived = lax.ppermute(away, "dir", [(i, (i + hop) % dirs_count) for i in range(dirs_count)])
+        came = arrived if hop == 1 else came + arrived
+    local_states = states_of(dir_index, jnp.float32)
+    states = reduce_states(local_states, came, cells)
+
     slot_cap = max(1, 2 * balanced_blocks // cells)
     period = cells * slot_cap
-    slot_order = jnp.arange(period, dtype=jnp.int32)
-    offset = (slot_order - first_live) % period
-    is_live = offset < own_count
-    rows_picked = jnp.where(is_live, offset, 0)
-    send_features = jnp.where(
-        is_live[:, None, None], updated[rows_picked], jnp.zeros((), jnp.bfloat16)
-    )
-    send_positions = jnp.where(
-        is_live[:, None, None], positions[rows_picked], jnp.zeros((), jnp.bfloat16)
-    )
-    received_features, received_positions = (
-        lax.all_to_all(send_features, "cell", split_axis=0, concat_axis=0, tiled=True),
-        lax.all_to_all(send_positions, "cell", split_axis=0, concat_axis=0, tiled=True),
-    )
+    owner = jnp.arange(cells, dtype=jnp.int32)
+    whole_rounds = slot_cap % dirs_count == 0
+    per_owner = slot_cap // dirs_count if whole_rounds else slot_cap
+    lane = jnp.arange(per_owner, dtype=jnp.int32)
+    if whole_rounds:
+        wanted = owner[:, None] * slot_cap + lane[None, :] * dirs_count + dir_index
+    else:
+        wanted = owner[:, None] * slot_cap + lane[None, :]
+    offset = ((wanted - first_live) % period).reshape(-1)
+    index = (offset - first_slot) // dirs_count
+    is_mine = (offset < own_count) & ((offset - first_slot) % dirs_count == 0)
+    picked = jnp.where(is_mine, index, 0)
+    parcels = jnp.where(
+        is_mine[:, None, None], join(updated, own_places)[picked], jnp.zeros((), jnp.bfloat16)
+    )
+    received = lax.all_to_all(parcels, "cell", split_axis=0, concat_axis=0, tiled=True)
     target = jnp.arange(balanced_blocks, dtype=jnp.int32)
-    within = target % slot_cap
-    global_index = (target // slot_cap * cells + cell_index) * slot_cap + within
+    global_index = (target // slot_cap * cells + cell_index) * slot_cap + target % slot_cap
     source = jnp.sum((count_ends[None, :] <= global_index[:, None]).astype(jnp.int32), axis=1)
-    pick_rows = source * slot_cap + within
-    balanced_features = received_features[pick_rows]
+    if whole_rounds:
+        def dealt_to(array, part):
+            split = array.reshape((-1, dirs_count) + array.shape[1:])
+            return lax.dynamic_index_in_dim(split, part, 1, keepdims=False)
+
+        within = dealt_to(target % slot_cap, dir_index) // dirs_count
+        rows = received[dealt_to(source, dir_index) * per_owner + within]
+        gathered = [rows]
+        for hop in range(1, dirs_count):
+            gathered.append(
+                lax.ppermute(rows, "dir", [(i, (i + hop) % dirs_count) for i in range(dirs_count)])
+            )
+        parts = jnp.stack(gathered, axis=1)
+        order = (dir_index - jnp.arange(dirs_count, dtype=jnp.int32)) % dirs_count
+        balanced = parts[:, order].reshape((balanced_blocks,) + parts.shape[2:])
+    else:
+        rows = received[source * per_owner + target % slot_cap]
+        balanced = rows
+        for hop in range(1, dirs_count):
+            other = lax.ppermute(rows, "dir", [(i, (i + hop) % dirs_count) for i in range(dirs_count)])
+            held = global_index % dirs_count == (dir_index - hop) % dirs_count
+            balanced = jnp.where(held[:, None, None], other, balanced)
+    balanced_features = balanced[:, :block_atoms]
     balanced_positions = shift_component(
-        received_positions[pick_rows].astype(jnp.float32),
+        balanced[:, places_of].astype(jnp.float32),
         slab_width * source.astype(jnp.float32)[:, None, None],
     )
-    share = DIRS // dirs_count
-    unit_rows = 32 * cells
-    padded_rows = -(-share * width // unit_rows) * unit_rows
-    table = lax.dynamic_index_in_dim(
-        jnp.asarray(direction_rows(DIRS, dirs_count)), dir_index, 0, keepdims=False
-    )
-    weights_t = projections.T
-    own_global = shift_component(float_positions, slab_width * cell_index.astype(jnp.float32))
-    own_coords = jnp.transpose(own_global, (1, 0, 2)).reshape(3, -1)
-    live_atoms = (own_count * block_atoms).astype(jnp.int32).reshape(1)
-    local_states = kv_states(
-        live_atoms, table, own_coords, updated.reshape(-1, width), weights_t, projections, share, padded_rows
-    )
-    states = reduce_states(local_states, cells)
     share_blocks = balanced_blocks // dirs_count
+    table = lax.dynamic_index_in_dim(tables, dir_index, 0, keepdims=False)
 
     def partial_mix(owner):
         features = lax.dynamic_slice_in_dim(balanced_features, owner * share_blocks, share_blocks, 0)
         places = lax.dynamic_slice_in_dim(balanced_positions, owner * share_blocks, share_blocks, 0)
-        coords = jnp.transpose(places, (1, 0, 2)).reshape(3, -1)
+        coords = jnp.transpose(places, (1, 0, 2)).reshape(axes, -1)
         return query_mix(table, coords, features.reshape(-1, width), weights_t, states, share)
 
     mixed_rows = None
     for hop in range(1, dirs_count):
         away = partial_mix((dir_index + hop) % dirs_count).astype(jnp.bfloat16)
-        came = lax.ppermute(away, "dir", [(i, (i + hop) % dirs_count) for i in range(dirs_count)])
-        came = came.astype(jnp.float32)
-        mixed_rows = came if mixed_rows is None else mixed_rows + came
+        arrived = lax.ppermute(away, "dir", [(i, (i + hop) % dirs_count) for i in range(dirs_count)])
+        arrived = arrived.astype(jnp.float32)
+        mixed_rows = arrived if mixed_rows is None else mixed_rows + arrived
     kept = partial_mix(dir_index)
     mixed_rows = kept if mixed_rows is None else kept + mixed_rows
     mix_scale = 1.0 / math.sqrt(DIRS * cells * balanced_blocks * block_atoms * width)

time: 192 us -> 147 us (0.77)
  waiting for transfers between devices: 24.3 us -> 3.83 us
  between operations: 14.9 us -> 1.61 us
  local copies, waits for them, and re-layouts: 28.5 us -> 20.1 us
  matrix products: 12.2 us -> 6.98 us
  starting transfers between devices: 19.8 us -> 22.8 us
  Pallas kernels: 81.7 us -> 83.7 us
    all_gather x1 -> x0, waiting for transfers between devices: 24.3 us -> none  [per_device(): updated = lax.all_gather(updated_share, 'dir', axis=0, tiled=True)]
    all_to_all x2 -> x1, starting transfers between devices: 9.12 us -> 15.1 us  [per_device(): lax.all_to_all(parcels, 'cell', split_axis=0, concat_axis=0, tiled=True)]
    dot_general x7 -> x3, matrix products: 7.79 us -> 3.38 us  [radial_terms(): jnp.einsum('gnkab,gnbf->gkaf', radial, near_features, preferred_element_t...]
    ppermute x4 -> x3, starting transfers between devices: 10 us -> 6.13 us  [the longest x1 5.53 us: per_device(): lax.ppermute(faces, 'cell', [((i + 1) % cells, i) for i in range(cells)])]
    ppermute x1 -> x2, waiting for transfers between devices: 0.01 us -> 3.81 us  [per_device(): lax.ppermute(away, 'dir', [(i, (i + hop) % dirs_count) for i in range(dir...]
    unnamed x16 -> x17, local copies, waits for them, and re-layouts: 0.79 us -> 3.44 us
    gather x4, local copies, waits for them, and re-layouts: 4.61 us -> 1.97 us  [the longest x2 0.7 us: per_device(): balanced = parts[:, order].reshape((balanced_blocks,) + parts.shape[2:])]
    dynamic_update_slice x7 -> x3, local copies, waits for them, and re-layouts: 4.62 us -> 2.01 us  [block_advance(): return lax.dynamic_update_slice_in_dim(running, result, at, 0)]
  transfers between devices with their start and end apart: 8 -> 6, of which waited for: 1 -> 1; matrix products, arithmetic and copies ran while one was open for 23% -> 8% of each run, Pallas kernels for 37% -> 49%
where the time goes in v3:
time: 147 us; the launch traced here: 148 us
  Pallas kernels  83.7 us (57%)
  starting transfers between devices  22.8 us (16%)
  local copies, waits for them, and re-layouts  20.1 us (14%)
  other arithmetic  8.65 us (6%)
  matrix products  6.98 us (5%)
  waiting for transfers between devices  3.83 us (3%)
  between operations  1.61 us (1%)
    pallas_call x1, Pallas kernels, reduce_states(): pl.pallas_call(functools.partial(reduce_kernel, bits), out_shape=jax.Shap...  45.6 us
    pallas_call x2, Pallas kernels, query_mix(): pl.pallas_call(functools.partial(query_kernel, chunk, share), out_shape=j...  21.8 us
    pallas_call x2, Pallas kernels, kv_states(): pl.pallas_call(functools.partial(kv_kernel, chunk, share), out_shape=jax....  16.3 us
    all_to_all x1, starting transfers between devices, per_device(): lax.all_to_all(parcels, 'cell', split_axis=0, concat_axis=0, tiled=True)  15.1 us
    ppermute x1, starting transfers between devices, per_device(): lax.ppermute(faces, 'cell', [((i + 1) % cells, i) for i in range(cells)])  5.53 us
    ppermute x2, waiting for transfers between devices, per_device(): lax.ppermute(away, 'dir', [(i, (i + hop) % dirs_count) for i in range(dir...  3.81 us
    unnamed x17, local copies, waits for them, and re-layouts  3.44 us
    dot_general x3, matrix products, radial_terms(): jnp.einsum('gnkab,gnbf->gkaf', radial, near_features, preferred_element_t...  3.38 us
  transfers between devices with their start and end apart: 6, of which 1 were waited for; matrix products, arithmetic and copies ran while one was open for 8% of the time, Pallas kernels for 49%

profile of v3, /device:TPU:0, one launch (start us, length us, event | category | flops | bytes accessed | tf_op | source)
XLA Modules:
  0.0 147.8 jit_solution(13668967313026674314)
XLA Ops:
  0.0 1.0 slice.24
  1.1 0.7 slice.25
  1.9 5.5 %collective-permute-start.1 = (bf16[4,144,128]{2,0,1:T(4,128)(2,1)S(1)}, bf16[4,144,128]{2,0,1:T(4,128)(2,1)S(1)}, u32[]{:S(2)}, u32[]{:S(2)}) collective-permute-start(bf16[4,144,128]{2,0,1:T(4,128)(2,1)S(1)} %fusion.20), channel_id=1, source_target_pairs={{2,0},{4,2},{6,4},{8,6},{10,8},{12,10},{14,12},{16,14},{18,16},{20... | collective-permute-start | bytes 442376 | tf_op jit(solution)/shard_map/ppermute | solution.py:370
  7.4 0.7 copy.38
  10.2 1.3 dynamic_slice.53
  11.5 1.3 fusion.35
  12.8 1.3 compare_and_fusion
  14.5 0.8 copy.41
  15.2 0.8 constant_dynamic-slice_fusion.4
  16.2 0.7 add_bitcast_fusion
  17.6 0.7 convert_element_type.79
  18.4 1.6 %copy.49 = bf16[128,384]{0,1:T(8,128)(2,1)} copy(bf16[128,384]{1,0:T(8,128)(2,1)} %weights_ref.3) | data formatting | bytes 196608 | tf_op args[6]
  21.2 1.1 broadcast_in_dim.21
  22.3 10.4 %while.10 = (s32[]{:T(128)}, f32[16,128,128]{2,1,0:T(8,128)}, s32[]{:T(128)}, f32[16,3,128]{2,1,0:T(4,128)S(1)}, s32[16,4]{1,0:T(8,128)S(1)}, /*index=5*/f32[40,...) while((s32[]{:T(128)}, f32[16,128,128]{2,1,0:T(8,128)}, ...), condition=%wide.region_4.5_spmd, body=%wide.region_1.4_spmd.sunk | while | flops 275219488 | bytes 3331535 | solution.py:350
  23.9 1.1 fusion.50
  27.4 1.1 fusion.50
  30.8 1.1 fusion.50
  32.0 0.7 constant_dynamic-update-slice_fusion.2
  32.7 1.6 %fusion.14 = bf16[16,128,128]{2,1,0:T(8,128)(2,1)S(1)} fusion(f32[16,128,128]{2,1,0:T(8,128)} %get-tuple-element.48, bf16[16,2,128,128]{3,2,1,0:T(8,128)(2,1)S(1)} %bitcast.76, s32[]{:T(128)S(6)} %select_n.196, bf16[128,128]{1,0:T(8,128)(2,1)S(1)} %copy-done), kind=kOutput, calls=%fused_computation.21 | convolution fusion | flops 69206016 | bytes 2129924 | tf_op jit(solution)/shard_map/dot_general | solution.py:405
  35.0 0.9 broadcast_select_fusion
  36.0 15.1 %all-to-all-start = ((bf16[16,144,128]{2,1,0:T(8,128)(2,1)}), bf16[16,144,128]{2,1,0:T(8,128)(2,1)S(1)}, u32[]{:S(2)}, u32[]{:S(2)}) async-start(bf16[16,144,128]{2,1,0:T(8,128)(2,1)} %broadcast_select_fusion), calls=%async_computation | async-start | bytes 1179648 | tf_op jit(solution)/shard_map/all_to_all | solution.py:449
  51.1 8.0 %kv_states.3 = bf16[3328,128]{1,0:T(8,128)(2,1)} custom-call(s32[1]{0:T(128)} %bitcast.27.live_ref, f32[32,128]{1,0:T(8,128)} %get-tuple-element.103.table_ref, f32[3,2048]{1,0:T(4,128)} %get-tuple-element.97.coords_ref, bf16[2048,128]{1,0:T(8,128)(2,1)} %bitcast.78, bf16[384,128]{1,0:T(8,128)(2,1)} %bitcast.84, bf16[128,384]{1,0:T(8,128)(2,1)} %weights_ref.3), custom_call_target="tpu_custom_call" | custom-call | flops 6710886400 | bytes 20000000 | tf_op jit(solution)/shard_map/kv_states/pallas_call | solution.py:169
  59.1 1.5 %collective-permute-start.3 = (bf16[3328,128]{1,0:T(8,128)(2,1)}, bf16[3328,128]{1,0:T(8,128)(2,1)S(1)}, u32[]{:S(2)}, u32[]{:S(2)}) collective-permute-start(bf16[3328,128]{1,0:T(8,128)(2,1)} %kv_states.3), channel_id=1, source_target_pairs={{0,1},{1,0},{2,3},{3,2},{4,5},{5,4},{6,7},{7,6},{8,9},{9,8},{10,11... | collective-permute-start | bytes 2555912 | tf_op jit(solution)/shard_map/ppermute | solution.py:427
  60.6 8.3 %kv_states.2.local_ref = f32[3328,128]{1,0:T(8,128)} custom-call(s32[1]{0:T(128)} %bitcast.27.live_ref, f32[32,128]{1,0:T(8,128)} %get-tuple-element.104.table_ref, f32[3,2048]{1,0:T(4,128)} %get-tuple-element.97.coords_ref, bf16[2048,128]{1,0:T(8,128)(2,1)} %bitcast.79, bf16[384,128]{1,0:T(8,128)(2,1)} %bitcast.85, bf16[128,384]{1,0:T(8,128)(2,1)} %weights_ref.3), custom_call_target="tpu_custom_call" | custom-call | flops 6710886400 | bytes 20000000 | tf_op jit(solution)/shard_map/kv_states/pallas_call | solution.py:169
  70.2 3.8 %collective-permute-done.3.came_ref = bf16[3328,128]{1,0:T(8,128)(2,1)S(1)} collective-permute-done((bf16[3328,128]{1,0:T(8,128)(2,1)}, bf16[3328,128]{1,0:T(8,128)(2,1)S(1)}, u32[]{:S(2)}, u32[]{:S(2)}) %collective-permute-start.3) | collective-permute-done | bytes 852000 | tf_op jit(solution)/shard_map/ppermute | solution.py:427
  74.0 0.9 copy-done.5
  74.9 45.6 %reduce_states.1.states_ref = bf16[3328,128]{1,0:T(8,128)(2,1)} custom-call(f32[3328,128]{1,0:T(8,128)} %kv_states.2.local_ref, bf16[3328,128]{1,0:T(8,128)(2,1)} %copy-done.5), custom_call_target="tpu_custom_call" | custom-call | flops 20000000000 | bytes 60000000 | tf_op jit(solution)/shard_map/reduce_states/pallas_call | solution.py:305
  121.5 0.8 constant_dynamic-slice_fusion.1
  122.9 10.9 %query_mix.3 = f32[1024,128]{1,0:T(8,128)} custom-call(f32[32,128]{1,0:T(8,128)} %get-tuple-element.104.table_ref, f32[3,1024]{1,0:T(4,128)} %get-tuple-element.101.coords_ref, bf16[1024,128]{1,0:T(8,128)(2,1)} %bitcast.82, bf16[384,128]{1,0:T(8,128)(2,1)} %bitcast.86, bf16[3328,128]{1,0:T(8,128)(2,1)} %reduce_states.1.states_ref), custom_call_target="tpu_custom_call" | custom-call | flops 6710886400 | bytes 20000000 | tf_op jit(solution)/shard_map/query_mix/pallas_call | solution.py:191
  133.8 1.1 convert_element_type.88
  134.9 10.9 %query_mix.2 = f32[1024,128]{1,0:T(8,128)} custom-call(f32[32,128]{1,0:T(8,128)} %get-tuple-element.104.table_ref, f32[3,1024]{1,0:T(4,128)} %get-tuple-element.102.coords_ref, bf16[1024,128]{1,0:T(8,128)(2,1)} %bitcast.81, bf16[384,128]{1,0:T(8,128)(2,1)} %bitcast.87, bf16[3328,128]{1,0:T(8,128)(2,1)} %reduce_states.1.states_ref), custom_call_target="tpu_custom_call" | custom-call | flops 6710886400 | bytes 20000000 | tf_op jit(solution)/shard_map/query_mix/pallas_call | solution.py:191
  145.8 2.0 %convolution_convert_fusion = bf16[1024,128]{1,0:T(8,128)(2,1)} fusion(bf16[128,128]{1,0:T(8,128)(2,1)S(1)} %copy-done.3, f32[1024,128]{1,0:T(8,128)} %query_mix.2, bf16[1024,128]{1,0:T(8,128)(2,1)S(1)} %collective-permute-done.4), kind=kOutput, calls=%fused_computation.22 | convolution fusion | flops 34209792 | bytes 1081344 | tf_op jit(solution)/shard_map/dot_general | solution.py:499
  (91 shorter events, 13.0 us)
Async XLA Ops:
  0.0 32.7 %copy-start = (bf16[128,128]{1,0:T(8,128)(2,1)S(1)}, bf16[128,128]{1,0:T(8,128)(2,1)}, u32[]{:S(2)}) copy-start(bf16[128,128]{1,0:T(8,128)(2,1)} %param.16) | copy-start | bytes 98308
  0.0 20.0 %copy-start.4 = (f32[2,32,128]{2,1,0:T(8,128)S(1)}, f32[2,32,128]{2,1,0:T(8,128)}, u32[]{:S(2)}) copy-start(f32[2,32,128]{2,1,0:T(8,128)} %constant.207.clone) | copy-start | bytes 98308
  0.0 21.0 %copy-start.1 = (bf16[32,128,128]{2,1,0:T(8,128)(2,1)S(1)}, bf16[32,128,128]{2,1,0:T(8,128)(2,1)}, u32[]{:S(2)}) copy-start(bf16[32,128,128]{2,1,0:T(8,128)(2,1)} %param.11) | copy-start | bytes 3145732
  1.9 18.7 %collective-permute-start.1 = (bf16[4,144,128]{2,0,1:T(4,128)(2,1)S(1)}, bf16[4,144,128]{2,0,1:T(4,128)(2,1)S(1)}, u32[]{:S(2)}, u32[]{:S(2)}) collective-permute-start(bf16[4,144,128]{2,0,1:T(4,128)(2,1)S(1)} %fusion.20), channel_id=1, source_target_pairs={{2,0},{4,2},{6,4},{8,6},{10,8},{12,10},{14,12},{16,14},{18,16},{20... | collective-permute-start | bytes 442376 | tf_op jit(solution)/shard_map/ppermute | solution.py:370
  7.4 13.3 %collective-permute-start = (bf16[4,144,128]{2,0,1:T(4,128)(2,1)S(1)}, bf16[4,144,128]{2,0,1:T(4,128)(2,1)S(1)}, u32[]{:S(2)}, u32[]{:S(2)}) collective-permute-start(bf16[4,144,128]{2,0,1:T(4,128)(2,1)S(1)} %fusion.20), channel_id=1, source_target_pairs={{0,2},{2,4},{4,6},{6,8},{8,10},{10,12},{12,14},{14,16},{16,18},{18... | collective-permute-start | bytes 442376 | tf_op jit(solution)/shard_map/ppermute | solution.py:369
  21.0 1.3 copy-start.6
  34.3 1.7 %copy-start.2 = (bf16[16,128,128]{2,1,0:T(8,128)(2,1)}, bf16[16,128,128]{2,1,0:T(8,128)(2,1)S(1)}, u32[]{:S(2)}) copy-start(bf16[16,128,128]{2,1,0:T(8,128)(2,1)S(1)} %fusion.14) | copy-start | bytes 1572868
  36.0 33.0 %all-to-all-start = ((bf16[16,144,128]{2,1,0:T(8,128)(2,1)}), bf16[16,144,128]{2,1,0:T(8,128)(2,1)S(1)}, u32[]{:S(2)}, u32[]{:S(2)}) async-start(bf16[16,144,128]{2,1,0:T(8,128)(2,1)} %broadcast_select_fusion), calls=%async_computation | async-start | bytes 1179648 | tf_op jit(solution)/shard_map/all_to_all | solution.py:449
  59.1 14.9 %collective-permute-start.3 = (bf16[3328,128]{1,0:T(8,128)(2,1)}, bf16[3328,128]{1,0:T(8,128)(2,1)S(1)}, u32[]{:S(2)}, u32[]{:S(2)}) collective-permute-start(bf16[3328,128]{1,0:T(8,128)(2,1)} %kv_states.3), channel_id=1, source_target_pairs={{0,1},{1,0},{2,3},{3,2},{4,5},{5,4},{6,7},{7,6},{8,9},{9,8},{10,11... | collective-permute-start | bytes 2555912 | tf_op jit(solution)/shard_map/ppermute | solution.py:427
  69.6 51.0 %collective-permute-start.2 = (bf16[8,144,128]{2,1,0:T(8,128)(2,1)S(1)}, bf16[8,144,128]{2,1,0:T(8,128)(2,1)S(1)}, u32[]{:S(2)}, u32[]{:S(2)}) collective-permute-start(bf16[8,144,128]{2,1,0:T(8,128)(2,1)S(1)} %gather_fusion.3), channel_id=1, source_target_pairs={{0,1},{1,0},{2,3},{3,2},{4,5},{5,4},{6,7},{7,6},{8,9},{9,8},{10,11... | collective-permute-start | bytes 884744 | tf_op jit(solution)/shard_map/ppermute | solution.py:463
  74.0 0.9 copy-start.5
  134.9 11.0 %collective-permute-start.4 = (bf16[1024,128]{1,0:T(8,128)(2,1)S(1)}, bf16[1024,128]{1,0:T(8,128)(2,1)S(1)}, u32[]{:S(2)}, u32[]{:S(2)}) collective-permute-start(bf16[1024,128]{1,0:T(8,128)(2,1)S(1)} %convert_element_type.88), channel_id=1, source_target_pairs={{0,1},{1,0},{2,3},{3,2},{4,5},{5,4},{6,7},{7,6},{8,9},{9,8},{10,11... | collective-permute-start | bytes 786440 | tf_op jit(solution)/shard_map/ppermute | solution.py:492
  134.9 10.9 %copy-start.3 = (bf16[128,128]{1,0:T(8,128)(2,1)S(1)}, bf16[128,128]{1,0:T(8,128)(2,1)}, u32[]{:S(2)}) copy-start(bf16[128,128]{1,0:T(8,128)(2,1)} %param.18) | copy-start | bytes 98308

commit v4 on v3

--- a/solution.py
+++ b/solution.py
@@ -68,7 +68,7 @@
     step_s = jnp.broadcast_to(across(sines, last), sine.shape)
     double = 2.0 * step_c
     older = None
-    low, high = [], []
+    turned = []
     for first in range(0, half, 8):
         if first == 8:
             older = (cosine, sine)
@@ -77,11 +77,19 @@
             held = (cosine, sine)
             cosine, sine = double * cosine - older[0], double * sine - older[1]
             older = held
-        a = features[first : first + 8, :]
-        b = features[half + first : half + first + 8, :]
+        turned.append((cosine, sine))
+    low, high = [], []
+    for first in range(0, half, 16):
+        pair = turned[first // 8 : first // 8 + 2]
+        cosine, sine = [
+            jnp.concatenate([both[which] for both in pair], axis=0).astype(jnp.bfloat16)
+            for which in range(2)
+        ]
+        a = features[first : first + 16, :]
+        b = features[half + first : half + first + 16, :]
         low.append(a * cosine - b * sine)
         high.append(b * cosine + a * sine)
-    return [jnp.concatenate(low + high, axis=0).astype(jnp.bfloat16)]
+    return [jnp.concatenate(low + high, axis=0)]
 
 
 def kv_kernel(chunk, share, live_ref, table_ref, coords_ref, rows_ref, weights_t_ref, weights_ref, out_ref, states_ref, keys, cosines, sines):
@@ -98,30 +106,27 @@
         keys[...] = lax.dot_general(
             weights_t_ref[width : 2 * width, :], rows, (((1,), (1,)), ((), ())),
             preferred_element_type=jnp.float32,
-        )
+        ).astype(jnp.bfloat16)
         values = jnp.dot(rows, weights_ref[:, 2 * width :], preferred_element_type=jnp.float32)
         index = turn * chunk + lax.broadcasted_iota(jnp.int32, values.shape, 0)
         values = jnp.where(index < live, values, 0.0).astype(jnp.bfloat16)
         store_powers(table_ref[...], coords_ref[:, at], half, cosines, sines)
 
-        def inner(group, held):
+        for group in range(share // per_turn):
             parts = []
             for j in range(per_turn):
                 parts += rotated(keys, group * per_turn + j, count, half, cosines, sines)
             size = per_turn * width
-            out = pl.ds(pl.multiple_of(group * size, size), size)
-            states_ref[out, :] += jnp.dot(
+            states_ref[group * size : (group + 1) * size, :] += jnp.dot(
                 jnp.concatenate(parts, axis=0), values, preferred_element_type=jnp.float32
             )
-            return held
-
-        return lax.fori_loop(0, share // per_turn, inner, carried)
+        return carried
 
     lax.fori_loop(0, (live + chunk - 1) // chunk, advance, 0)
     out_ref[...] = states_ref[...].astype(out_ref.dtype)
 
 
-def query_kernel(chunk, share, table_ref, coords_ref, rows_ref, weights_t_ref, states_ref, out_ref, queries, flipped, cosines, sines, total):
+def query_kernel(chunk, share, table_ref, coords_ref, rows_ref, weights_t_ref, states_ref, out_ref, queries, flipped, cosines, sines):
     atoms, width = rows_ref.shape
     half = width // 2
     count = table_ref.shape[0]
@@ -134,24 +139,20 @@
         queries[...] = lax.dot_general(
             weights_t_ref[:width, :], rows_ref[at, :], (((1,), (1,)), ((), ())),
             preferred_element_type=jnp.float32,
-        )
+        ).astype(jnp.bfloat16)
         store_powers(table_ref[...], coords_ref[:, at], half, cosines, sines)
-        total[...] = jnp.zeros_like(total)
-
-        def inner(group, held):
+        summed = None
+        for group in range(share // per_turn):
             parts = []
             for j in range(per_turn):
                 parts += rotated(queries, group * per_turn + j, count, half, cosines, sines)
             size = per_turn * width
-            columns = pl.ds(pl.multiple_of(group * size, size), size)
-            total[...] += jnp.dot(
-                flipped[:, columns], jnp.concatenate(parts, axis=0),
+            term = jnp.dot(
+                flipped[:, group * size : (group + 1) * size], jnp.concatenate(parts, axis=0),
                 preferred_element_type=jnp.float32,
             )
-            return held
-
-        lax.fori_loop(0, share // per_turn, inner, 0)
-        out_ref[at, :] = total[...].T
+            summed = term if summed is None else summed + term
+        out_ref[at, :] = summed.T
         return carried
 
     lax.fori_loop(0, atoms // chunk, advance, 0)
@@ -173,7 +174,7 @@
         out_specs=pl.BlockSpec(memory_space=pltpu.VMEM),
         scratch_shapes=[
             pltpu.VMEM((padded_rows, width), jnp.float32),
-            pltpu.VMEM((width, chunk), jnp.float32),
+            pltpu.VMEM((width, chunk), jnp.bfloat16),
             pltpu.VMEM((chunk // 128, 8 * count, 128), jnp.float32),
             pltpu.VMEM((chunk // 128, 8 * count, 128), jnp.float32),
         ],
@@ -194,11 +195,10 @@
         in_specs=vmem(5),
         out_specs=pl.BlockSpec(memory_space=pltpu.VMEM),
         scratch_shapes=[
-            pltpu.VMEM((width, chunk), jnp.float32),
+            pltpu.VMEM((width, chunk), jnp.bfloat16),
             pltpu.VMEM((width, share * width), jnp.bfloat16),
             pltpu.VMEM((chunk // 128, 8 * count, 128), jnp.float32),
             pltpu.VMEM((chunk // 128, 8 * count, 128), jnp.float32),
-            pltpu.VMEM((width, chunk), jnp.float32),
         ],
         cost_estimate=pl.CostEstimate(
             flops=2 * share * atoms * width * width * 8, bytes_accessed=20_000_000, transcendentals=0
@@ -212,7 +212,7 @@
     second = list(first)
     if bits > 2:
         second[1], second[2] = second[2], second[1]
-    return [first, second]
+    return [first, second, first, second]
 
 
 def piece_rows(rows, unit, pieces):
@@ -244,58 +244,66 @@
             return local_ref[at, :] + came_ref[at, :].astype(jnp.float32)
         return total[at, :]
 
-    for step in range(bits):
-        copies = []
-        for k, order in enumerate(orders):
-            b, half = order[step], lengths[k] // 2
+    pieces = range(len(orders))
+    running = {}
+
+    def copy_to(b, source, target, send_sem, recv_sem):
+        copy = pltpu.make_async_remote_copy(
+            src_ref=source,
+            dst_ref=target,
+            send_sem=send_sem,
+            recv_sem=recv_sem,
+            device_id=partner(b),
+            device_id_type=pl.DeviceIdType.MESH,
+        )
+        copy.start()
+        return copy
+
+    def issue(k, stage):
+        if stage < bits:
+            b, half = orders[k][stage], lengths[k] // 2
             away = pl.multiple_of(starts[k] + (1 - bit_of(b)) * half, 16)
             at = pl.ds(offsets[k], half)
-            sent[at, :] = own(step, pl.ds(away, half)).astype(jnp.bfloat16)
-            if step == 0 and k == 0:
+            sent[at, :] = own(stage, pl.ds(away, half)).astype(jnp.bfloat16)
+            if stage == 0 and k == 0:
                 pl.semaphore_wait(barrier, bits)
-            copy = pltpu.make_async_remote_copy(
-                src_ref=sent.at[at, :],
-                dst_ref=landed.at[at, :],
-                send_sem=send_sems.at[k, step],
-                recv_sem=recv_sems.at[k, step],
-                device_id=partner(b),
-                device_id_type=pl.DeviceIdType.MESH,
+            running[k, stage] = copy_to(
+                b, sent.at[at, :], landed.at[at, :], send_sems.at[k, stage], recv_sems.at[k, stage]
             )
-            copy.start()
-            copies.append(copy)
-        for k, order in enumerate(orders):
-            b, half = order[step], lengths[k] // 2
-            keep = pl.multiple_of(starts[k] + bit_of(b) * half, 16)
+        else:
+            step = 2 * bits - 1 - stage
+            at = pl.ds(pl.multiple_of(starts[k], 16), lengths[k])
+            running[k, stage] = copy_to(
+                orders[k][step], out_ref.at[at, :], out_ref.at[at, :],
+                gather_send.at[k, step], gather_recv.at[k, step],
+            )
+
+    def finish(k, stage):
+        running[k, stage].wait_recv()
+        if stage < bits:
+            half = lengths[k] // 2
+            keep = pl.multiple_of(starts[k] + bit_of(orders[k][stage]) * half, 16)
             at = pl.ds(offsets[k], half)
-            copies[k].wait_recv()
-            summed = own(step, pl.ds(keep, half)) + landed[at, :].astype(jnp.float32)
-            if step == bits - 1:
+            summed = own(stage, pl.ds(keep, half)) + landed[at, :].astype(jnp.float32)
+            if stage == bits - 1:
                 out_ref[pl.ds(keep, half), :] = summed.astype(jnp.bfloat16)
             else:
                 total[pl.ds(keep, half), :] = summed
-            starts[k] = keep
-            lengths[k] = half
+            starts[k], lengths[k] = keep, half
             offsets[k] += half
-        for copy in copies:
-            copy.wait_send()
-    for step in reversed(range(bits)):
-        copies = []
-        for k, order in enumerate(orders):
-            at = pl.ds(pl.multiple_of(starts[k], 16), lengths[k])
-            copy = pltpu.make_async_remote_copy(
-                src_ref=out_ref.at[at, :],
-                dst_ref=out_ref.at[at, :],
-                send_sem=gather_send.at[k, step],
-                recv_sem=gather_recv.at[k, step],
-                device_id=partner(order[step]),
-                device_id_type=pl.DeviceIdType.MESH,
-            )
-            copy.start()
-            copies.append(copy)
-        for k, order in enumerate(orders):
-            copies[k].wait()
-            starts[k] = starts[k] - bit_of(order[step]) * lengths[k]
+        else:
+            step = 2 * bits - 1 - stage
+            starts[k] = starts[k] - bit_of(orders[k][step]) * lengths[k]
             lengths[k] = 2 * lengths[k]
+
+    for stage in range(2 * bits + 1):
+        for k in pieces:
+            if stage > 0:
+                finish(k, stage - 1)
+            if stage < 2 * bits:
+                issue(k, stage)
+    for copy in running.values():
+        copy.wait_send()
 
 
 def reduce_states(local, came, cells):

time: 147 us -> 135 us (0.918); the launches traced: 148 us -> 134 us
  Pallas kernels: 83.7 us -> 65.6 us
  starting transfers between devices: 22.8 us -> 10.1 us
  local copies, waits for them, and re-layouts: 20.1 us -> 28.3 us
  matrix products: 6.98 us -> 11.5 us
  waiting for transfers between devices: 3.83 us -> 6.67 us
    pallas_call x1, Pallas kernels: 45.6 us -> 30.2 us  [reduce_states(): pl.pallas_call(functools.partial(reduce_kernel, bits), out_shape=jax.Shap...]
    all_to_all x1, starting transfers between devices: 15.1 us -> 3.58 us  [per_device(): lax.all_to_all(parcels, 'cell', split_axis=0, concat_axis=0, tiled=True)]
    pallas_call x2, Pallas kernels: 21.8 us -> 14.3 us  [query_mix(): pl.pallas_call(functools.partial(query_kernel, chunk, share), out_shape=j...]
    pallas_call x2, Pallas kernels: 16.3 us -> 21.1 us  [kv_states(): pl.pallas_call(functools.partial(kv_kernel, chunk, share), out_shape=jax....]
    dot_general x3 -> x7, matrix products: 3.38 us -> 7.88 us  [radial_terms(): jnp.einsum('gnkab,gnbf->gkaf', radial, near_features, preferred_element_t...]
    ppermute x2, waiting for transfers between devices: 3.81 us -> 6.66 us  [per_device(): lax.ppermute(away, 'dir', [(i, (i + hop) % dirs_count) for i in range(dir...]
    dynamic_update_slice x3 -> x7, local copies, waits for them, and re-layouts: 2.01 us -> 4.66 us  [block_advance(): return lax.dynamic_update_slice_in_dim(running, result, at, 0)]
    gather x3 -> x7, local copies, waits for them, and re-layouts: 1.79 us -> 4.18 us  [block_advance(): near_features = extended_features[picked]]
  transfers between devices with their start and end apart: 6 -> 6, of which waited for: 1 -> 2; matrix products, arithmetic and copies ran while one was open for 8% -> 9% of each run, Pallas kernels for 49% -> 44%
where the time goes in v4:
time: 135 us; the launch traced here: 134 us
  Pallas kernels  65.6 us (49%)
  local copies, waits for them, and re-layouts  28.3 us (21%)
  matrix products  11.5 us (9%)
  starting transfers between devices  10.1 us (7%)
  other arithmetic  9.6 us (7%)
  waiting for transfers between devices  6.67 us (5%)
  between operations  1.6 us (1%)
    pallas_call x1, Pallas kernels, reduce_states(): pl.pallas_call(functools.partial(reduce_kernel, bits), out_shape=jax.Shap...  30.2 us
    pallas_call x2, Pallas kernels, kv_states(): pl.pallas_call(functools.partial(kv_kernel, chunk, share), out_shape=jax....  21.1 us
    pallas_call x2, Pallas kernels, query_mix(): pl.pallas_call(functools.partial(query_kernel, chunk, share), out_shape=j...  14.3 us
    dot_general x7, matrix products, radial_terms(): jnp.einsum('gnkab,gnbf->gkaf', radial, near_features, preferred_element_t...  7.88 us
    ppermute x2, waiting for transfers between devices, per_device(): lax.ppermute(away, 'dir', [(i, (i + hop) % dirs_count) for i in range(dir...  6.66 us
    ppermute x1, starting transfers between devices, per_device(): lax.ppermute(faces, 'cell', [((i + 1) % cells, i) for i in range(cells)])  5.53 us
    dynamic_update_slice x7, local copies, waits for them, and re-layouts, block_advance(): return lax.dynamic_update_slice_in_dim(running, result, at, 0)  4.66 us
    gather x7, local copies, waits for them, and re-layouts, block_advance(): near_features = extended_features[picked]  4.18 us
  transfers between devices with their start and end apart: 6, of which 2 were waited for; matrix products, arithmetic and copies ran while one was open for 9% of the time, Pallas kernels for 44%

profile of v4, /device:TPU:0, one launch (start us, length us, event | category | flops | bytes accessed | tf_op | source)
XLA Modules:
  0.0 133.7 jit_solution(12640539766895321837)
XLA Ops:
  0.0 1.0 slice.24
  1.9 5.5 %collective-permute-start.1 = (bf16[4,144,128]{2,0,1:T(4,128)(2,1)S(1)}, bf16[4,144,128]{2,0,1:T(4,128)(2,1)S(1)}, u32[]{:S(2)}, u32[]{:S(2)}) collective-permute-start(bf16[4,144,128]{2,0,1:T(4,128)(2,1)S(1)} %fusion.20), channel_id=1, source_target_pairs={{2,0},{4,2},{6,4},{8,6},{10,8},{12,10},{14,12},{16,14},{18,16},{20... | collective-permute-start | bytes 442376 | tf_op jit(solution)/shard_map/ppermute | solution.py:378
  10.2 1.3 dynamic_slice.53
  11.5 1.3 fusion.35
  12.8 1.3 compare_and_fusion
  14.5 0.8 copy.41
  15.2 0.8 constant_dynamic-slice_fusion.4
  18.4 1.6 %copy.49 = bf16[128,384]{0,1:T(8,128)(2,1)} copy(bf16[128,384]{1,0:T(8,128)(2,1)} %weights_ref.3) | data formatting | bytes 196608 | tf_op args[6]
  21.2 1.1 broadcast_in_dim.21
  22.3 24.2 %while.10 = (s32[]{:T(128)}, f32[16,128,128]{2,1,0:T(8,128)}, s32[]{:T(128)}, f32[16,3,128]{2,1,0:T(4,128)S(1)}, s32[16,4]{1,0:T(8,128)S(1)}, /*index=5*/f32[40,...) while((s32[]{:T(128)}, f32[16,128,128]{2,1,0:T(8,128)}, ...), condition=%wide.region_4.5_spmd, body=%wide.region_1.4_spmd.sunk | while | flops 275219488 | bytes 3331535 | solution.py:358
  23.9 1.1 fusion.50
  27.4 1.1 fusion.50
  30.8 1.1 fusion.50
  34.3 1.1 fusion.50
  37.8 1.1 fusion.50
  41.2 1.1 fusion.50
  44.7 1.1 fusion.50
  46.5 1.6 %fusion.14 = bf16[16,128,128]{2,1,0:T(8,128)(2,1)S(1)} fusion(f32[16,128,128]{2,1,0:T(8,128)} %get-tuple-element.48, bf16[16,2,128,128]{3,2,1,0:T(8,128)(2,1)S(1)} %bitcast.76, s32[]{:T(128)S(6)} %select_n.196, bf16[128,128]{1,0:T(8,128)(2,1)S(1)} %copy-done), kind=kOutput, calls=%fused_computation.21 | convolution fusion | flops 69206016 | bytes 2129924 | tf_op jit(solution)/shard_map/dot_general | solution.py:413
  48.9 0.9 broadcast_select_fusion
  49.8 3.6 %all-to-all-start = ((bf16[16,144,128]{2,1,0:T(8,128)(2,1)}), bf16[16,144,128]{2,1,0:T(8,128)(2,1)S(1)}, u32[]{:S(2)}, u32[]{:S(2)}) async-start(bf16[16,144,128]{2,1,0:T(8,128)(2,1)} %broadcast_select_fusion), calls=%async_computation | async-start | bytes 1179648 | tf_op jit(solution)/shard_map/all_to_all | solution.py:457
  53.4 10.4 %kv_states.3 = bf16[3328,128]{1,0:T(8,128)(2,1)} custom-call(s32[1]{0:T(128)} %bitcast.27.live_ref, f32[32,128]{1,0:T(8,128)} %get-tuple-element.103.table_ref, f32[3,2048]{1,0:T(4,128)} %get-tuple-element.97.coords_ref, bf16[2048,128]{1,0:T(8,128)(2,1)} %bitcast.78, bf16[384,128]{1,0:T(8,128)(2,1)} %bitcast.84, bf16[128,384]{1,0:T(8,128)(2,1)} %weights_ref.3), custom_call_target="tpu_custom_call" | custom-call | flops 6710886400 | bytes 20000000 | tf_op jit(solution)/shard_map/kv_states/pallas_call | solution.py:170
  63.8 10.7 %kv_states.2.local_ref = f32[3328,128]{1,0:T(8,128)} custom-call(s32[1]{0:T(128)} %bitcast.27.live_ref, f32[32,128]{1,0:T(8,128)} %get-tuple-element.104.table_ref, f32[3,2048]{1,0:T(4,128)} %get-tuple-element.97.coords_ref, bf16[2048,128]{1,0:T(8,128)(2,1)} %bitcast.79, bf16[384,128]{1,0:T(8,128)(2,1)} %bitcast.85, bf16[128,384]{1,0:T(8,128)(2,1)} %weights_ref.3), custom_call_target="tpu_custom_call" | custom-call | flops 6710886400 | bytes 20000000 | tf_op jit(solution)/shard_map/kv_states/pallas_call | solution.py:170
  75.1 0.9 collective-permute-start.2
  76.1 5.2 %collective-permute-done.3.came_ref = bf16[3328,128]{1,0:T(8,128)(2,1)S(1)} collective-permute-done((bf16[3328,128]{1,0:T(8,128)(2,1)}, bf16[3328,128]{1,0:T(8,128)(2,1)S(1)}, u32[]{:S(2)}, u32[]{:S(2)}) %collective-permute-start.3) | collective-permute-done | bytes 852000 | tf_op jit(solution)/shard_map/ppermute | solution.py:435
  81.3 0.9 copy-done.5
  82.2 30.2 %reduce_states.1.states_ref = bf16[3328,128]{1,0:T(8,128)(2,1)} custom-call(f32[3328,128]{1,0:T(8,128)} %kv_states.2.local_ref, bf16[3328,128]{1,0:T(8,128)(2,1)} %copy-done.5), custom_call_target="tpu_custom_call" | custom-call | flops 20000000000 | bytes 60000000 | tf_op jit(solution)/shard_map/reduce_states/pallas_call | solution.py:313
  113.4 0.8 constant_dynamic-slice_fusion.1
  114.8 7.2 %query_mix.3 = f32[1024,128]{1,0:T(8,128)} custom-call(f32[32,128]{1,0:T(8,128)} %get-tuple-element.104.table_ref, f32[3,1024]{1,0:T(4,128)} %get-tuple-element.101.coords_ref, bf16[1024,128]{1,0:T(8,128)(2,1)} %bitcast.82, bf16[384,128]{1,0:T(8,128)(2,1)} %bitcast.86, bf16[3328,128]{1,0:T(8,128)(2,1)} %reduce_states.1.states_ref), custom_call_target="tpu_custom_call" | custom-call | flops 6710886400 | bytes 20000000 | tf_op jit(solution)/shard_map/query_mix/pallas_call | solution.py:192
  121.9 1.1 convert_element_type.88
  123.1 7.2 %query_mix.2 = f32[1024,128]{1,0:T(8,128)} custom-call(f32[32,128]{1,0:T(8,128)} %get-tuple-element.104.table_ref, f32[3,1024]{1,0:T(4,128)} %get-tuple-element.102.coords_ref, bf16[1024,128]{1,0:T(8,128)(2,1)} %bitcast.81, bf16[384,128]{1,0:T(8,128)(2,1)} %bitcast.87, bf16[3328,128]{1,0:T(8,128)(2,1)} %reduce_states.1.states_ref), custom_call_target="tpu_custom_call" | custom-call | flops 6710886400 | bytes 20000000 | tf_op jit(solution)/shard_map/query_mix/pallas_call | solution.py:192
  130.3 1.4 %collective-permute-done.4 = bf16[1024,128]{1,0:T(8,128)(2,1)S(1)} collective-permute-done((bf16[1024,128]{1,0:T(8,128)(2,1)S(1)}, bf16[1024,128]{1,0:T(8,128)(2,1)S(1)}, u32[]{:S(2)}, u32[]{:S(2)}) %collective-permute-start.4) | collective-permute-done | bytes 262176 | tf_op jit(solution)/shard_map/ppermute | solution.py:500
  131.7 2.0 %convolution_convert_fusion = bf16[1024,128]{1,0:T(8,128)(2,1)} fusion(bf16[128,128]{1,0:T(8,128)(2,1)S(1)} %copy-done.3, f32[1024,128]{1,0:T(8,128)} %query_mix.2, bf16[1024,128]{1,0:T(8,128)(2,1)S(1)} %collective-permute-done.4), kind=kOutput, calls=%fused_computation.22 | convolution fusion | flops 34209792 | bytes 1081344 | tf_op jit(solution)/shard_map/dot_general | solution.py:507
  (135 shorter events, 25.1 us)
Async XLA Ops:
  0.0 46.5 %copy-start = (bf16[128,128]{1,0:T(8,128)(2,1)S(1)}, bf16[128,128]{1,0:T(8,128)(2,1)}, u32[]{:S(2)}) copy-start(bf16[128,128]{1,0:T(8,128)(2,1)} %param.16) | copy-start | bytes 98308
  0.0 20.0 %copy-start.4 = (f32[2,32,128]{2,1,0:T(8,128)S(1)}, f32[2,32,128]{2,1,0:T(8,128)}, u32[]{:S(2)}) copy-start(f32[2,32,128]{2,1,0:T(8,128)} %constant.207.clone) | copy-start | bytes 98308
  0.0 21.0 %copy-start.1 = (bf16[32,128,128]{2,1,0:T(8,128)(2,1)S(1)}, bf16[32,128,128]{2,1,0:T(8,128)(2,1)}, u32[]{:S(2)}) copy-start(bf16[32,128,128]{2,1,0:T(8,128)(2,1)} %param.11) | copy-start | bytes 3145732
  1.9 18.7 %collective-permute-start.1 = (bf16[4,144,128]{2,0,1:T(4,128)(2,1)S(1)}, bf16[4,144,128]{2,0,1:T(4,128)(2,1)S(1)}, u32[]{:S(2)}, u32[]{:S(2)}) collective-permute-start(bf16[4,144,128]{2,0,1:T(4,128)(2,1)S(1)} %fusion.20), channel_id=1, source_target_pairs={{2,0},{4,2},{6,4},{8,6},{10,8},{12,10},{14,12},{16,14},{18,16},{20... | collective-permute-start | bytes 442376 | tf_op jit(solution)/shard_map/ppermute | solution.py:378
  7.4 13.3 %collective-permute-start = (bf16[4,144,128]{2,0,1:T(4,128)(2,1)S(1)}, bf16[4,144,128]{2,0,1:T(4,128)(2,1)S(1)}, u32[]{:S(2)}, u32[]{:S(2)}) collective-permute-start(bf16[4,144,128]{2,0,1:T(4,128)(2,1)S(1)} %fusion.20), channel_id=1, source_target_pairs={{0,2},{2,4},{4,6},{6,8},{8,10},{10,12},{12,14},{14,16},{16,18},{18... | collective-permute-start | bytes 442376 | tf_op jit(solution)/shard_map/ppermute | solution.py:377
  21.0 1.3 copy-start.6
  48.1 1.7 %copy-start.2 = (bf16[16,128,128]{2,1,0:T(8,128)(2,1)}, bf16[16,128,128]{2,1,0:T(8,128)(2,1)S(1)}, u32[]{:S(2)}) copy-start(bf16[16,128,128]{2,1,0:T(8,128)(2,1)S(1)} %fusion.14) | copy-start | bytes 1572868
  49.8 24.7 %all-to-all-start = ((bf16[16,144,128]{2,1,0:T(8,128)(2,1)}), bf16[16,144,128]{2,1,0:T(8,128)(2,1)S(1)}, u32[]{:S(2)}, u32[]{:S(2)}) async-start(bf16[16,144,128]{2,1,0:T(8,128)(2,1)} %broadcast_select_fusion), calls=%async_computation | async-start | bytes 1179648 | tf_op jit(solution)/shard_map/all_to_all | solution.py:457
  63.8 17.5 %collective-permute-start.3 = (bf16[3328,128]{1,0:T(8,128)(2,1)}, bf16[3328,128]{1,0:T(8,128)(2,1)S(1)}, u32[]{:S(2)}, u32[]{:S(2)}) collective-permute-start(bf16[3328,128]{1,0:T(8,128)(2,1)} %kv_states.3), channel_id=1, source_target_pairs={{0,1},{1,0},{2,3},{3,2},{4,5},{5,4},{6,7},{7,6},{8,9},{9,8},{10,11... | collective-permute-start | bytes 2555912 | tf_op jit(solution)/shard_map/ppermute | solution.py:435
  75.1 37.3 %collective-permute-start.2 = (bf16[8,144,128]{2,1,0:T(8,128)(2,1)S(1)}, bf16[8,144,128]{2,1,0:T(8,128)(2,1)S(1)}, u32[]{:S(2)}, u32[]{:S(2)}) collective-permute-start(bf16[8,144,128]{2,1,0:T(8,128)(2,1)S(1)} %gather_fusion.3), channel_id=1, source_target_pairs={{0,1},{1,0},{2,3},{3,2},{4,5},{5,4},{6,7},{7,6},{8,9},{9,8},{10,11... | collective-permute-start | bytes 884744 | tf_op jit(solution)/shard_map/ppermute | solution.py:471
  81.3 0.9 copy-start.5
  123.0 8.7 %collective-permute-start.4 = (bf16[1024,128]{1,0:T(8,128)(2,1)S(1)}, bf16[1024,128]{1,0:T(8,128)(2,1)S(1)}, u32[]{:S(2)}, u32[]{:S(2)}) collective-permute-start(bf16[1024,128]{1,0:T(8,128)(2,1)S(1)} %convert_element_type.88), channel_id=1, source_target_pairs={{0,1},{1,0},{2,3},{3,2},{4,5},{5,4},{6,7},{7,6},{8,9},{9,8},{10,11... | collective-permute-start | bytes 786440 | tf_op jit(solution)/shard_map/ppermute | solution.py:500
  123.1 8.6 %copy-start.3 = (bf16[128,128]{1,0:T(8,128)(2,1)S(1)}, bf16[128,128]{1,0:T(8,128)(2,1)}, u32[]{:S(2)}) copy-start(bf16[128,128]{1,0:T(8,128)(2,1)} %param.18) | copy-start | bytes 98308

commit v5 on v4

--- a/solution.py
+++ b/solution.py
@@ -220,7 +220,7 @@
     return [(units // pieces + (k < units % pieces)) * unit for k in range(pieces)]
 
 
-def reduce_kernel(bits, local_ref, came_ref, out_ref, total, sent, landed, send_sems, recv_sems, gather_send, gather_recv):
+def reduce_kernel(bits, local_ref, away_ref, out_ref, total, sent, landed, turned, crossed, arrived, send_sems, recv_sems, gather_send, gather_recv, cross_send, cross_recv):
     me = lax.axis_index("cell")
 
     def bit_of(b):
@@ -234,26 +234,26 @@
         pl.semaphore_signal(
             barrier, inc=1, device_id=partner(b), device_id_type=pl.DeviceIdType.MESH
         )
+    other = {"dir": 1 - lax.axis_index("dir")}
+    pl.semaphore_signal(barrier, inc=1, device_id=other, device_id_type=pl.DeviceIdType.MESH)
     orders = reduce_orders(bits)
     lengths = piece_rows(local_ref.shape[0], 16 * (1 << bits), len(orders))
     starts = [sum(lengths[:k]) for k in range(len(orders))]
     offsets = list(starts)
 
     def own(step, at):
-        if step == 0:
-            return local_ref[at, :] + came_ref[at, :].astype(jnp.float32)
-        return total[at, :]
+        return local_ref[at, :] if step == 0 else total[at, :]
 
     pieces = range(len(orders))
     running = {}
 
-    def copy_to(b, source, target, send_sem, recv_sem):
+    def copy_to(device, source, target, send_sem, recv_sem):
         copy = pltpu.make_async_remote_copy(
             src_ref=source,
             dst_ref=target,
             send_sem=send_sem,
             recv_sem=recv_sem,
-            device_id=partner(b),
+            device_id=device,
             device_id_type=pl.DeviceIdType.MESH,
         )
         copy.start()
@@ -266,15 +266,20 @@
             at = pl.ds(offsets[k], half)
             sent[at, :] = own(stage, pl.ds(away, half)).astype(jnp.bfloat16)
             if stage == 0 and k == 0:
-                pl.semaphore_wait(barrier, bits)
+                pl.semaphore_wait(barrier, bits + 1)
+            if stage == 0:
+                turned[at, :] = away_ref[pl.ds(away, half), :]
+                running[k, "turned"] = copy_to(
+                    partner(b), turned.at[at, :], crossed.at[at, :], cross_send.at[k, 0], cross_recv.at[k, 0]
+                )
             running[k, stage] = copy_to(
-                b, sent.at[at, :], landed.at[at, :], send_sems.at[k, stage], recv_sems.at[k, stage]
+                partner(b), sent.at[at, :], landed.at[at, :], send_sems.at[k, stage], recv_sems.at[k, stage]
             )
         else:
             step = 2 * bits - 1 - stage
             at = pl.ds(pl.multiple_of(starts[k], 16), lengths[k])
             running[k, stage] = copy_to(
-                orders[k][step], out_ref.at[at, :], out_ref.at[at, :],
+                partner(orders[k][step]), out_ref.at[at, :], out_ref.at[at, :],
                 gather_send.at[k, step], gather_recv.at[k, step],
             )
 
@@ -289,6 +294,15 @@
                 out_ref[pl.ds(keep, half), :] = summed.astype(jnp.bfloat16)
             else:
                 total[pl.ds(keep, half), :] = summed
+            if stage == 0:
+                running[k, "turned"].wait_recv()
+                rest = pl.ds(offsets[k] + half, half)
+                turned[rest, :] = (
+                    away_ref[pl.ds(keep, half), :].astype(jnp.float32) + crossed[at, :].astype(jnp.float32)
+                ).astype(jnp.bfloat16)
+                running[k, "across"] = copy_to(
+                    other, turned.at[rest, :], arrived.at[rest, :], cross_send.at[k, 1], cross_recv.at[k, 1]
+                )
             starts[k], lengths[k] = keep, half
             offsets[k] += half
         else:
@@ -296,9 +310,21 @@
             starts[k] = starts[k] - bit_of(orders[k][step]) * lengths[k]
             lengths[k] = 2 * lengths[k]
 
-    for stage in range(2 * bits + 1):
+    def absorb(k):
+        running[k, "across"].wait_recv()
+        held = pl.ds(pl.multiple_of(starts[k], 16), lengths[k])
+        came = arrived[pl.ds(offsets[k], lengths[k]), :]
+        total[held, :] = total[held, :] + came.astype(jnp.float32)
+
+    for k in pieces:
+        issue(k, 0)
+    for k in pieces:
+        finish(k, 0)
+    for stage in range(1, 2 * bits + 1):
         for k in pieces:
-            if stage > 0:
+            if stage == 1:
+                absorb(k)
+            else:
                 finish(k, stage - 1)
             if stage < 2 * bits:
                 issue(k, stage)
@@ -306,7 +332,7 @@
         copy.wait_send()
 
 
-def reduce_states(local, came, cells):
+def reduce_states(local, away, cells):
     bits = cells.bit_length() - 1
     rows, width = local.shape
     pieces = len(reduce_orders(bits))
@@ -317,14 +343,14 @@
         out_specs=pl.BlockSpec(memory_space=pltpu.VMEM),
         scratch_shapes=[
             pltpu.VMEM((rows, width), jnp.float32),
-            pltpu.VMEM((rows, width), jnp.bfloat16),
-            pltpu.VMEM((rows, width), jnp.bfloat16),
         ]
-        + [pltpu.SemaphoreType.DMA((pieces, bits))] * 4,
+        + [pltpu.VMEM((rows, width), jnp.bfloat16)] * 5
+        + [pltpu.SemaphoreType.DMA((pieces, bits))] * 4
+        + [pltpu.SemaphoreType.DMA((pieces, 2))] * 2,
         compiler_params=pltpu.CompilerParams(collective_id=0, has_side_effects=True),
         cost_estimate=pl.CostEstimate(flops=20_000_000_000, bytes_accessed=60_000_000, transcendentals=0),
         name="reduce_states",
-    )(local, came)
+    )(local, away)
 
 
 def radial_terms(own_positions, near_positions, near_features, filter_gains):
@@ -390,9 +416,10 @@
         ],
         axis=0,
     )
-    own_count = counts[cell_index]
+    cell_order = jnp.arange(cells, dtype=jnp.int32)
+    own_count = jnp.sum(jnp.where(cell_order == cell_index, counts, 0))
+    first_live = jnp.sum(jnp.where(cell_order < cell_index, counts, 0))
     count_ends = jnp.cumsum(counts)
-    first_live = (count_ends - counts)[cell_index]
     share_slots = capacity // dirs_count
     first_slot = (dir_index - first_live) % dirs_count
 
@@ -429,13 +456,9 @@
             padded_rows, dtype,
         )
 
-    came = jnp.zeros((padded_rows, width), jnp.bfloat16)
-    for hop in range(1, dirs_count):
-        away = states_of((dir_index + hop) % dirs_count, jnp.bfloat16)
-        arrived = lax.ppermute(away, "dir", [(i, (i + hop) % dirs_count) for i in range(dirs_count)])
-        came = arrived if hop == 1 else came + arrived
+    away_states = states_of((dir_index + 1) % dirs_count, jnp.bfloat16)
     local_states = states_of(dir_index, jnp.float32)
-    states = reduce_states(local_states, came, cells)
+    states = reduce_states(local_states, away_states, cells)
 
     slot_cap = max(1, 2 * balanced_blocks // cells)
     period = cells * slot_cap

time: 135 us -> 131 us (0.970)
  starting transfers between devices: 10.1 us -> 23.4 us
  local copies, waits for them, and re-layouts: 28.3 us -> 17.3 us
  matrix products: 11.5 us -> 6.94 us
  waiting for transfers between devices: 6.67 us -> 3.62 us
  Pallas kernels: 65.6 us -> 68 us
    pallas_call x1, Pallas kernels: 30.2 us -> 41.9 us  [reduce_states(): pl.pallas_call(functools.partial(reduce_kernel, bits), out_shape=jax.Shap...]
    all_to_all x1, starting transfers between devices: 3.58 us -> 14.6 us  [per_device(): lax.all_to_all(parcels, 'cell', split_axis=0, concat_axis=0, tiled=True)]
    pallas_call x2, Pallas kernels: 21.1 us -> 11.8 us  [kv_states(): pl.pallas_call(functools.partial(kv_kernel, chunk, share), out_shape=jax....]
    ppermute x2 -> x1, waiting for transfers between devices: 6.66 us -> 0.01 us  [per_device(): lax.ppermute(away, 'dir', [(i, (i + hop) % dirs_count) for i in range(dir...]
    dot_general x7 -> x3, matrix products: 7.88 us -> 3.34 us  [radial_terms(): jnp.einsum('gnkab,gnbf->gkaf', radial, near_features, preferred_element_t...]
    all_to_all x1, waiting for transfers between devices: 0.01 us -> 3.61 us  [per_device(): lax.all_to_all(parcels, 'cell', split_axis=0, concat_axis=0, tiled=True)]
    dynamic_update_slice x7 -> x3, local copies, waits for them, and re-layouts: 4.66 us -> 1.99 us  [block_advance(): return lax.dynamic_update_slice_in_dim(running, result, at, 0)]
    gather x7 -> x3, local copies, waits for them, and re-layouts: 4.18 us -> 1.79 us  [block_advance(): near_features = extended_features[picked]]
  transfers between devices with their start and end apart: 6 -> 5, of which waited for: 2 -> 1; matrix products, arithmetic and copies ran while one was open for 9% -> 8% of each run, Pallas kernels for 44% -> 47%
where the time goes in v5:
time: 131 us; the launch traced here: 130 us
  Pallas kernels  68 us (52%)
  starting transfers between devices  23.4 us (18%)
  local copies, waits for them, and re-layouts  17.3 us (13%)
  other arithmetic  9.3 us (7%)
  matrix products  6.94 us (5%)
  waiting for transfers between devices  3.62 us (3%)
  between operations  1.59 us (1%)
    pallas_call x1, Pallas kernels, reduce_states(): pl.pallas_call(functools.partial(reduce_kernel, bits), out_shape=jax.Shap...  41.9 us
    all_to_all x1, starting transfers between devices, per_device(): lax.all_to_all(parcels, 'cell', split_axis=0, concat_axis=0, tiled=True)  14.6 us
    pallas_call x2, Pallas kernels, query_mix(): pl.pallas_call(functools.partial(query_kernel, chunk, share), out_shape=j...  14.3 us
    pallas_call x2, Pallas kernels, kv_states(): pl.pallas_call(functools.partial(kv_kernel, chunk, share), out_shape=jax....  11.8 us
    ppermute x1, starting transfers between devices, per_device(): lax.ppermute(faces, 'cell', [((i + 1) % cells, i) for i in range(cells)])  5.53 us
    all_to_all x1, waiting for transfers between devices, per_device(): lax.all_to_all(parcels, 'cell', split_axis=0, concat_axis=0, tiled=True)  3.61 us
    dot_general x3, matrix products, radial_terms(): jnp.einsum('gnkab,gnbf->gkaf', radial, near_features, preferred_element_t...  3.34 us
  transfers between devices with their start and end apart: 5, of which 1 were waited for; matrix products, arithmetic and copies ran while one was open for 8% of the time, Pallas kernels for 47%

profile of v5, /device:TPU:0, one launch (start us, length us, event | category | flops | bytes accessed | tf_op | source)
XLA Modules:
  0.0 130.2 jit_solution(5418381298318806212)
XLA Ops:
  0.0 1.0 slice.24
  1.1 0.7 slice.25
  1.9 5.5 %collective-permute-start.1 = (bf16[4,144,128]{2,0,1:T(4,128)(2,1)S(1)}, bf16[4,144,128]{2,0,1:T(4,128)(2,1)S(1)}, u32[]{:S(2)}, u32[]{:S(2)}) collective-permute-start(bf16[4,144,128]{2,0,1:T(4,128)(2,1)S(1)} %fusion.20), channel_id=1, source_target_pairs={{2,0},{4,2},{6,4},{8,6},{10,8},{12,10},{14,12},{16,14},{18,16},{20... | collective-permute-start | bytes 442376 | tf_op jit(solution)/shard_map/ppermute | solution.py:404
  7.4 1.4 %fusion.32 = (s32[]{:T(128)}, s32[]{:T(128)}, s32[16]{0:T(128)S(1)}) fusion(s32[16]{0:T(128)} %param.14, s32[]{:T(128)S(6)} %axis_index.25), kind=kLoop, calls=%fused_computation.102 | loop fusion | flops 350 | bytes 140 | tf_op jit(solution)/shard_map/reduce_sum | solution.py:420
  9.4 0.7 copy.47
  10.6 0.8 copy.40
  11.4 0.8 constant_dynamic-slice_fusion.4
  12.2 1.3 fusion.37
  13.7 0.7 add_bitcast_fusion
  14.4 1.3 compare_and_fusion
  16.4 0.7 convert_element_type.79
  17.2 1.6 %copy.49 = bf16[128,384]{0,1:T(8,128)(2,1)} copy(bf16[128,384]{1,0:T(8,128)(2,1)} %weights_ref.3) | data formatting | bytes 196608 | tf_op args[6]
  20.0 1.1 broadcast_in_dim.27
  21.1 10.3 %while.10 = (s32[]{:T(128)}, f32[16,128,128]{2,1,0:T(8,128)}, s32[]{:T(128)}, f32[16,3,128]{2,1,0:T(4,128)S(1)}, s32[16,4]{1,0:T(8,128)S(1)}, /*index=5*/f32[40,...) while((s32[]{:T(128)}, f32[16,128,128]{2,1,0:T(8,128)}, ...), condition=%wide.region_5.6_spmd, body=%wide.region_2.0_spmd.sunk | while | flops 275219488 | bytes 3331535 | solution.py:384
  22.8 1.1 fusion.52
  26.2 1.1 fusion.52
  29.7 1.1 fusion.52
  30.8 0.7 constant_dynamic-update-slice_fusion.2
  31.5 1.6 %fusion.14 = bf16[16,128,128]{2,1,0:T(8,128)(2,1)S(1)} fusion(f32[16,128,128]{2,1,0:T(8,128)} %get-tuple-element.48, bf16[16,2,128,128]{3,2,1,0:T(8,128)(2,1)S(1)} %bitcast.74, s32[]{:T(128)S(6)} %select_n.199, bf16[128,128]{1,0:T(8,128)(2,1)S(1)} %copy-done), kind=kOutput, calls=%fused_computation.21 | convolution fusion | flops 69206016 | bytes 2129924 | tf_op jit(solution)/shard_map/dot_general | solution.py:440
  33.8 0.9 broadcast_select_fusion
  34.8 14.6 %all-to-all-start = ((bf16[16,144,128]{2,1,0:T(8,128)(2,1)}), bf16[16,144,128]{2,1,0:T(8,128)(2,1)S(1)}, u32[]{:S(2)}, u32[]{:S(2)}) async-start(bf16[16,144,128]{2,1,0:T(8,128)(2,1)} %broadcast_select_fusion), calls=%async_computation | async-start | bytes 1179648 | tf_op jit(solution)/shard_map/all_to_all | solution.py:480
  49.4 6.0 %kv_states.2.local_ref = f32[3328,128]{1,0:T(8,128)} custom-call(s32[1]{0:T(128)} %bitcast.25.live_ref, f32[32,128]{1,0:T(8,128)} %get-tuple-element.106.table_ref, f32[3,2048]{1,0:T(4,128)} %get-tuple-element.99.coords_ref, bf16[2048,128]{1,0:T(8,128)(2,1)} %bitcast.76, bf16[384,128]{1,0:T(8,128)(2,1)} %bitcast.82, bf16[128,384]{1,0:T(8,128)(2,1)} %weights_ref.3), custom_call_target="tpu_custom_call" | custom-call | flops 6710886400 | bytes 20000000 | tf_op jit(solution)/shard_map/kv_states/pallas_call | solution.py:170
  55.4 5.7 %kv_states.3.away_ref = bf16[3328,128]{1,0:T(8,128)(2,1)} custom-call(s32[1]{0:T(128)} %bitcast.25.live_ref, f32[32,128]{1,0:T(8,128)} %get-tuple-element.105.table_ref, f32[3,2048]{1,0:T(4,128)} %get-tuple-element.99.coords_ref, bf16[2048,128]{1,0:T(8,128)(2,1)} %bitcast.77, bf16[384,128]{1,0:T(8,128)(2,1)} %bitcast.83, bf16[128,384]{1,0:T(8,128)(2,1)} %weights_ref.3), custom_call_target="tpu_custom_call" | custom-call | flops 6710886400 | bytes 20000000 | tf_op jit(solution)/shard_map/kv_states/pallas_call | solution.py:170
  61.1 3.6 %all-to-all-done = bf16[16,144,128]{2,1,0:T(8,128)(2,1)S(1)} async-done(((bf16[16,144,128]{2,1,0:T(8,128)(2,1)}), bf16[16,144,128]{2,1,0:T(8,128)(2,1)S(1)}, u32[]{:S(2)}, u32[]{:S(2)}) %all-to-all-start) | async-done | bytes 589856 | tf_op jit(solution)/shard_map/all_to_all | solution.py:480
  65.3 1.6 %collective-permute-start.2 = (bf16[8,144,128]{2,1,0:T(8,128)(2,1)S(1)}, bf16[8,144,128]{2,1,0:T(8,128)(2,1)S(1)}, u32[]{:S(2)}, u32[]{:S(2)}) collective-permute-start(bf16[8,144,128]{2,1,0:T(8,128)(2,1)S(1)} %gather_fusion.3), channel_id=1, source_target_pairs={{0,1},{1,0},{2,3},{3,2},{4,5},{5,4},{6,7},{7,6},{8,9},{9,8},{10,11... | collective-permute-start | bytes 884744 | tf_op jit(solution)/shard_map/ppermute | solution.py:494
  66.9 41.9 %reduce_states.1.states_ref = bf16[3328,128]{1,0:T(8,128)(2,1)} custom-call(f32[3328,128]{1,0:T(8,128)} %kv_states.2.local_ref, bf16[3328,128]{1,0:T(8,128)(2,1)} %kv_states.3.away_ref), custom_call_target="tpu_custom_call" | custom-call | flops 20000000000 | bytes 60000000 | tf_op jit(solution)/shard_map/reduce_states/pallas_call | solution.py:339
  109.8 0.8 constant_dynamic-slice_fusion.1
  111.2 7.2 %query_mix.3 = f32[1024,128]{1,0:T(8,128)} custom-call(f32[32,128]{1,0:T(8,128)} %get-tuple-element.106.table_ref, f32[3,1024]{1,0:T(4,128)} %get-tuple-element.103.coords_ref, bf16[1024,128]{1,0:T(8,128)(2,1)} %bitcast.80, bf16[384,128]{1,0:T(8,128)(2,1)} %bitcast.84, bf16[3328,128]{1,0:T(8,128)(2,1)} %reduce_states.1.states_ref), custom_call_target="tpu_custom_call" | custom-call | flops 6710886400 | bytes 20000000 | tf_op jit(solution)/shard_map/query_mix/pallas_call | solution.py:192
  118.4 1.1 convert_element_type.88
  119.4 1.7 %collective-permute-start.3 = (bf16[1024,128]{1,0:T(8,128)(2,1)S(1)}, bf16[1024,128]{1,0:T(8,128)(2,1)S(1)}, u32[]{:S(2)}, u32[]{:S(2)}) collective-permute-start(bf16[1024,128]{1,0:T(8,128)(2,1)S(1)} %convert_element_type.88), channel_id=1, source_target_pairs={{0,1},{1,0},{2,3},{3,2},{4,5},{5,4},{6,7},{7,6},{8,9},{9,8},{10,11... | collective-permute-start | bytes 786440 | tf_op jit(solution)/shard_map/ppermute | solution.py:523
  121.1 7.2 %query_mix.2 = f32[1024,128]{1,0:T(8,128)} custom-call(f32[32,128]{1,0:T(8,128)} %get-tuple-element.106.table_ref, f32[3,1024]{1,0:T(4,128)} %get-tuple-element.104.coords_ref, bf16[1024,128]{1,0:T(8,128)(2,1)} %bitcast.79, bf16[384,128]{1,0:T(8,128)(2,1)} %bitcast.85, bf16[3328,128]{1,0:T(8,128)(2,1)} %reduce_states.1.states_ref), custom_call_target="tpu_custom_call" | custom-call | flops 6710886400 | bytes 20000000 | tf_op jit(solution)/shard_map/query_mix/pallas_call | solution.py:192
  128.3 2.0 %convolution_convert_fusion = bf16[1024,128]{1,0:T(8,128)(2,1)} fusion(bf16[128,128]{1,0:T(8,128)(2,1)S(1)} %copy-done.3, f32[1024,128]{1,0:T(8,128)} %query_mix.2, bf16[1024,128]{1,0:T(8,128)(2,1)S(1)} %collective-permute-done.3), kind=kOutput, calls=%fused_computation.22 | convolution fusion | flops 34209792 | bytes 1081344 | tf_op jit(solution)/shard_map/dot_general | solution.py:530
  (84 shorter events, 11.1 us)
Async XLA Ops:
  0.0 31.4 %copy-start = (bf16[128,128]{1,0:T(8,128)(2,1)S(1)}, bf16[128,128]{1,0:T(8,128)(2,1)}, u32[]{:S(2)}) copy-start(bf16[128,128]{1,0:T(8,128)(2,1)} %param.16) | copy-start | bytes 98308
  0.0 18.8 %copy-start.4 = (f32[2,32,128]{2,1,0:T(8,128)S(1)}, f32[2,32,128]{2,1,0:T(8,128)}, u32[]{:S(2)}) copy-start(f32[2,32,128]{2,1,0:T(8,128)} %constant.207.clone) | copy-start | bytes 98308
  0.0 19.8 %copy-start.1 = (bf16[32,128,128]{2,1,0:T(8,128)(2,1)S(1)}, bf16[32,128,128]{2,1,0:T(8,128)(2,1)}, u32[]{:S(2)}) copy-start(bf16[32,128,128]{2,1,0:T(8,128)(2,1)} %param.11) | copy-start | bytes 3145732
  1.9 17.6 %collective-permute-start.1 = (bf16[4,144,128]{2,0,1:T(4,128)(2,1)S(1)}, bf16[4,144,128]{2,0,1:T(4,128)(2,1)S(1)}, u32[]{:S(2)}, u32[]{:S(2)}) collective-permute-start(bf16[4,144,128]{2,0,1:T(4,128)(2,1)S(1)} %fusion.20), channel_id=1, source_target_pairs={{2,0},{4,2},{6,4},{8,6},{10,8},{12,10},{14,12},{16,14},{18,16},{20... | collective-permute-start | bytes 442376 | tf_op jit(solution)/shard_map/ppermute | solution.py:404
  7.4 12.1 %collective-permute-start = (bf16[4,144,128]{2,0,1:T(4,128)(2,1)S(1)}, bf16[4,144,128]{2,0,1:T(4,128)(2,1)S(1)}, u32[]{:S(2)}, u32[]{:S(2)}) collective-permute-start(bf16[4,144,128]{2,0,1:T(4,128)(2,1)S(1)} %fusion.20), channel_id=1, source_target_pairs={{0,2},{2,4},{4,6},{6,8},{8,10},{10,12},{12,14},{14,16},{16,18},{18... | collective-permute-start | bytes 442376 | tf_op jit(solution)/shard_map/ppermute | solution.py:403
  19.8 1.3 copy-start.5
  33.1 1.7 %copy-start.2 = (bf16[16,128,128]{2,1,0:T(8,128)(2,1)}, bf16[16,128,128]{2,1,0:T(8,128)(2,1)S(1)}, u32[]{:S(2)}) copy-start(bf16[16,128,128]{2,1,0:T(8,128)(2,1)S(1)} %fusion.14) | copy-start | bytes 1572868
  34.8 30.0 %all-to-all-start = ((bf16[16,144,128]{2,1,0:T(8,128)(2,1)}), bf16[16,144,128]{2,1,0:T(8,128)(2,1)S(1)}, u32[]{:S(2)}, u32[]{:S(2)}) async-start(bf16[16,144,128]{2,1,0:T(8,128)(2,1)} %broadcast_select_fusion), calls=%async_computation | async-start | bytes 1179648 | tf_op jit(solution)/shard_map/all_to_all | solution.py:480
  65.3 43.5 %collective-permute-start.2 = (bf16[8,144,128]{2,1,0:T(8,128)(2,1)S(1)}, bf16[8,144,128]{2,1,0:T(8,128)(2,1)S(1)}, u32[]{:S(2)}, u32[]{:S(2)}) collective-permute-start(bf16[8,144,128]{2,1,0:T(8,128)(2,1)S(1)} %gather_fusion.3), channel_id=1, source_target_pairs={{0,1},{1,0},{2,3},{3,2},{4,5},{5,4},{6,7},{7,6},{8,9},{9,8},{10,11... | collective-permute-start | bytes 884744 | tf_op jit(solution)/shard_map/ppermute | solution.py:494
  119.4 8.8 %collective-permute-start.3 = (bf16[1024,128]{1,0:T(8,128)(2,1)S(1)}, bf16[1024,128]{1,0:T(8,128)(2,1)S(1)}, u32[]{:S(2)}, u32[]{:S(2)}) collective-permute-start(bf16[1024,128]{1,0:T(8,128)(2,1)S(1)} %convert_element_type.88), channel_id=1, source_target_pairs={{0,1},{1,0},{2,3},{3,2},{4,5},{5,4},{6,7},{7,6},{8,9},{9,8},{10,11... | collective-permute-start | bytes 786440 | tf_op jit(solution)/shard_map/ppermute | solution.py:523
  121.1 7.2 %copy-start.3 = (bf16[128,128]{1,0:T(8,128)(2,1)S(1)}, bf16[128,128]{1,0:T(8,128)(2,1)}, u32[]{:S(2)}) copy-start(bf16[128,128]{1,0:T(8,128)(2,1)} %param.18) | copy-start | bytes 98308
